TPU v7x, 32 devices: a whole 2x2x4 slice. The times are simulated.
32 devices in a mesh: dp: 8 (over y, x, core), ctx: 4 (over z).
Axes of the slice: x: 2, y: 2, z: 4, core: 2. Of those that a mesh axis runs over, the one named last changes fastest.
Arguments:
- tokens: bfloat16 [2, 8, 1024, 1024], P(None, 'dp', 'ctx'), may hold values from -6 to 6
- segments: int32 [2, 8, 1024], P(None, 'dp', 'ctx'), may hold values from 0 to 18, as said below
- cotangent: bfloat16 [2, 8, 1024, 1024], P(None, 'dp', 'ctx'), may hold values from -6 to 6
- attn_gain: bfloat16 [1024], P(('dp', 'ctx')), may hold values from 0.5 to 1.5
- w_qkv: bfloat16 [1024, 3072], P(('dp', 'ctx')), may hold values from -0.1875 to 0.1875
- w_attn_out: bfloat16 [1024, 1024], P(('dp', 'ctx')), may hold values from -3 to 3
- mlp_gain: bfloat16 [1024], P(('dp', 'ctx')), may hold values from 0.5 to 1.5
- w_in: bfloat16 [1024, 5248], P(('dp', 'ctx')), may hold values from -0.1875 to 0.1875
- w_mlp_out: bfloat16 [1024, 2624], P(('dp', 'ctx')), may hold values from -0.25 to 0.25
Outputs:
- layer_out: bfloat16 [2, 8, 1024, 1024], P(None, 'dp', 'ctx')
- input_grad: bfloat16 [2, 8, 1024, 1024], P(None, 'dp', 'ctx')
- attn_gain_grad: float32 [1024], P(('dp', 'ctx'))
- qkv_grad: float32 [1024, 3072], P(('dp', 'ctx'))
- attn_out_grad: float32 [1024, 1024], P(('dp', 'ctx'))
- mlp_gain_grad: float32 [1024], P(('dp', 'ctx'))
- in_grad: float32 [1024, 5248], P(('dp', 'ctx'))
- mlp_out_grad: float32 [1024, 2624], P(('dp', 'ctx'))
Inputs may be any that keep to these rules, and one draw needn't show every extreme that they name: `segments`: in each sequence, ids 1, 2, 3 and so on number its documents in order, each of 60 to 800 tokens except the last, which may be cut shorter; a tail of segment 0 of at least one token ends every sequence.
All inputs are finite; a program needn't handle non-finite values.
Results may differ from a plain program's by a relative error of at most 0.017.
Values may be sent and summed in bfloat16 or wider, within the bound.
No kernel may reach another device: no remote copies, remote signals or barrier semaphores. Data moves between devices by JAX's collectives and lax.ppermute only.
A program may use at most 256 MiB of HBM per device.

v0:
```python
import math

import jax
import jax.numpy as jnp
from jax import lax
from jax.sharding import PartitionSpec as P

HEADS = 16
HEAD = 64


epsilon = 1e-05
rope_base = 160000.0


def layer_norm(values, gain_vec):
    centered = values - jnp.mean(values, axis=-1, keepdims=True)
    inv_scale = lax.rsqrt(jnp.mean(centered * centered, axis=-1, keepdims=True) + epsilon)
    normed = centered * inv_scale
    return (normed * gain_vec, normed, inv_scale)


def norm_back(incoming, gain_vec, normed, inv_scale):
    scaled = incoming * gain_vec
    gain_grad = jnp.sum(incoming * normed, axis=0)
    shifted = (
        scaled
        - jnp.mean(scaled, axis=-1, keepdims=True)
        - normed * jnp.mean(scaled * normed, axis=-1, keepdims=True)
    )
    return (inv_scale * shifted, gain_grad)


def rotary_tables(positions, head_width):
    half_width = head_width // 2
    exponent = jnp.arange(half_width, dtype=jnp.float32) * (2.0 / head_width)
    frequency = jnp.exp(-exponent * math.log(rope_base))
    angles = positions.astype(jnp.float32)[:, None] * frequency[None, :]
    angles = jnp.concatenate([angles, angles], axis=-1)
    return (jnp.cos(angles), jnp.sin(angles))


def rotate_heads(values, cosine_table, sine_table):
    half_width = values.shape[-1] // 2
    turned = jnp.concatenate([-values[..., half_width:], values[..., :half_width]], axis=-1)
    return values * cosine_table[:, None, :] + turned * sine_table[:, None, :]


def contract_rows(left_side, right_side):
    return lax.dot_general(
        left_side, right_side, (((0,), (0,)), ((), ())), preferred_element_type=jnp.float32
    )


def contract_cols(left_side, right_side):
    return lax.dot_general(
        left_side, right_side, (((1,), (1,)), ((), ())), preferred_element_type=jnp.float32
    )


def on_device(tokens, segments, cotangent, attn_gain, w_qkv, w_attn_out, mlp_gain, w_in, w_mlp_out):
    micro_count, seq_count, local_len, model_width = tokens.shape
    hidden_units = w_mlp_out.shape[1]
    head_count = HEADS
    head_width = HEAD
    score_scale = 1.0 / math.sqrt(head_width)
    row_count = seq_count * local_len
    shaped = (seq_count, local_len, head_count, head_width)
    ctx_count = lax.axis_size("ctx")
    dp_count = lax.axis_size("dp")
    row_part = model_width // (dp_count * ctx_count)
    group_rows = dp_count * row_part

    def spread(left_side):
        return left_side.reshape(row_count, dp_count, ctx_count, row_part)

    resident = (
        lax.all_gather(attn_gain, ("dp", "ctx"), axis=0, tiled=True),
        lax.all_gather(w_qkv, ("dp", "ctx"), axis=0, tiled=True),
        lax.all_gather(w_attn_out, ("dp", "ctx"), axis=0, tiled=True),
        lax.all_gather(mlp_gain, ("dp", "ctx"), axis=0, tiled=True),
        lax.all_gather(w_in, ("dp", "ctx"), axis=0, tiled=True),
        lax.all_gather(w_mlp_out, ("dp", "ctx"), axis=0, tiled=True),
    )
    positions = lax.axis_index("ctx") * local_len + jnp.arange(local_len, dtype=jnp.int32)
    cosine_table, sine_table = rotary_tables(positions, head_width)
    totals = (
        jnp.zeros((group_rows, 3 * model_width), jnp.float32),
        jnp.zeros((group_rows, model_width), jnp.float32),
        jnp.zeros((group_rows, 2 * hidden_units), jnp.float32),
        jnp.zeros((group_rows, hidden_units), jnp.float32),
    )
    gain_one_total = jnp.zeros((model_width,), jnp.float32)
    gain_two_total = jnp.zeros((model_width,), jnp.float32)
    outputs = []
    input_grads = []
    for micro_index in range(micro_count):
        hidden_in = tokens[micro_index].astype(jnp.float32).reshape(row_count, model_width)
        seg_ids = segments[micro_index]
        keep_rows = (seg_ids != 0).astype(jnp.float32).reshape(row_count, 1)
        gain_one = resident[0].astype(jnp.float32)
        gain_two = resident[3].astype(jnp.float32)
        scaled_one, normed_one, factor_one = layer_norm(hidden_in, gain_one)
        attn_in = scaled_one.astype(jnp.bfloat16)
        projected = jnp.dot(attn_in, resident[1], preferred_element_type=jnp.float32)
        queries = rotate_heads(
            projected[:, :model_width].reshape(shaped), cosine_table, sine_table
        ).astype(jnp.bfloat16)
        keys_local = rotate_heads(
            projected[:, model_width : 2 * model_width].reshape(shaped), cosine_table, sine_table
        ).astype(jnp.bfloat16)
        values_local = (
            projected[:, 2 * model_width :]
            .astype(jnp.bfloat16)
            .reshape(seq_count, local_len, model_width)
        )
        keys_all, values_all, seg_all = (
            lax.all_gather(
                keys_local.reshape(seq_count, local_len, model_width), "ctx", axis=1, tiled=True
            ),
            lax.all_gather(values_local, "ctx", axis=1, tiled=True),
            lax.all_gather(seg_ids.astype(jnp.bfloat16), "ctx", axis=1, tiled=True),
        )
        full_len = keys_all.shape[1]
        keys_heads = keys_all.reshape(seq_count, full_len, head_count, head_width)
        values_heads = values_all.reshape(seq_count, full_len, head_count, head_width)
        allowed = (
            seg_ids.astype(jnp.float32)[:, None, :, None]
            == seg_all.astype(jnp.float32)[:, None, None, :]
        )
        mask_bias = jnp.where(allowed, 0.0, -1e30).astype(jnp.float32)
        scores = (
            jnp.einsum("schd,slhd->shcl", queries, keys_heads, preferred_element_type=jnp.float32)
            * score_scale
            + mask_bias
        )
        row_top = jnp.max(scores, axis=-1, keepdims=True)
        exponents = jnp.exp(scores - row_top)
        row_total = jnp.sum(exponents, axis=-1, keepdims=True)
        log_total = row_top + jnp.log(row_total)
        weights_low = (exponents / row_total).astype(jnp.bfloat16)
        attended_full = jnp.einsum(
            "shcl,slhd->schd", weights_low, values_heads, preferred_element_type=jnp.float32
        )
        attended = attended_full.astype(jnp.bfloat16).reshape(row_count, model_width)
        attn_branch = jnp.dot(attended, resident[2], preferred_element_type=jnp.float32)
        middle = hidden_in + keep_rows * attn_branch
        scaled_two, normed_two, factor_two = layer_norm(middle, gain_two)
        mlp_in = scaled_two.astype(jnp.bfloat16)
        gate_up = jnp.dot(mlp_in, resident[4], preferred_element_type=jnp.float32)
        gate_part = gate_up[:, :hidden_units]
        up_part = gate_up[:, hidden_units:]
        normal_cdf = 0.5 * (1.0 + jax.scipy.special.erf(gate_part / math.sqrt(2.0)))
        activated = gate_part * normal_cdf
        mixed = (activated * up_part).astype(jnp.bfloat16)
        down_branch = contract_cols(mixed, resident[5])
        outputs.append(
            (middle + keep_rows * down_branch)
            .astype(jnp.bfloat16)
            .reshape(seq_count, local_len, model_width)
        )
        gain_one = resident[0].astype(jnp.float32)
        gain_two = resident[3].astype(jnp.float32)
        incoming = cotangent[micro_index].astype(jnp.float32).reshape(row_count, model_width)
        down_grad = (keep_rows * incoming).astype(jnp.bfloat16)
        mixed_grad = jnp.dot(down_grad, resident[5], preferred_element_type=jnp.float32)
        density = jnp.exp(-0.5 * gate_part * gate_part) / math.sqrt(2.0 * math.pi)
        gate_grad = mixed_grad * up_part * (normal_cdf + gate_part * density)
        up_grad = mixed_grad * activated
        gate_up_grad = jnp.concatenate([gate_grad, up_grad], axis=1).astype(jnp.bfloat16)
        mlp_in_grad = contract_cols(gate_up_grad, resident[4])
        middle_part, grad_gain_two = norm_back(mlp_in_grad, gain_two, normed_two, factor_two)
        middle_grad = incoming + middle_part
        attn_grad = (keep_rows * middle_grad).astype(jnp.bfloat16)
        attended_grad = contract_cols(attn_grad, resident[2]).astype(jnp.bfloat16).reshape(shaped)
        scores_again = (
            jnp.einsum("schd,slhd->shcl", queries, keys_heads, preferred_element_type=jnp.float32)
            * score_scale
            + mask_bias
        )
        probs_again = jnp.exp(scores_again - log_total)
        weights_again = probs_again.astype(jnp.bfloat16)
        prob_grad = jnp.einsum(
            "schd,slhd->shcl", attended_grad, values_heads, preferred_element_type=jnp.float32
        )
        row_inner = jnp.sum(probs_again * prob_grad, axis=-1, keepdims=True)
        score_grad = (probs_again * (prob_grad - row_inner)).astype(jnp.bfloat16)
        query_grad = (
            jnp.einsum(
                "shcl,slhd->schd", score_grad, keys_heads, preferred_element_type=jnp.float32
            )
            * score_scale
        )
        key_terms = (
            jnp.einsum("shcl,schd->slhd", score_grad, queries, preferred_element_type=jnp.float32)
            * score_scale
        )
        value_terms = jnp.einsum(
            "shcl,schd->slhd", weights_again, attended_grad, preferred_element_type=jnp.float32
        )
        key_grad, value_grad = (
            lax.psum_scatter(
                key_terms.reshape(seq_count, full_len, model_width).astype(jnp.bfloat16),
                "ctx",
                scatter_dimension=1,
                tiled=True,
            ).astype(jnp.float32),
            lax.psum_scatter(
                value_terms.reshape(seq_count, full_len, model_width).astype(jnp.bfloat16),
                "ctx",
                scatter_dimension=1,
                tiled=True,
            ).astype(jnp.float32),
        )
        query_low = query_grad.astype(jnp.bfloat16).astype(jnp.float32)
        key_low = key_grad.astype(jnp.bfloat16).astype(jnp.float32).reshape(shaped)
        value_low = value_grad.astype(jnp.bfloat16).reshape(row_count, model_width)
        query_raw = rotate_heads(query_low, cosine_table, -sine_table).reshape(
            row_count, model_width
        )
        key_raw = rotate_heads(key_low, cosine_table, -sine_table).reshape(row_count, model_width)
        projected_grad = jnp.concatenate(
            [query_raw.astype(jnp.bfloat16), key_raw.astype(jnp.bfloat16), value_low], axis=1
        )
        attn_in_grad = contract_cols(projected_grad, resident[1])
        input_part, grad_gain_one = norm_back(attn_in_grad, gain_one, normed_one, factor_one)
        input_grads.append(
            (middle_grad + input_part)
            .astype(jnp.bfloat16)
            .reshape(seq_count, local_len, model_width)
        )
        gain_one_total = gain_one_total + grad_gain_one
        gain_two_total = gain_two_total + grad_gain_two
        lefts = (
            lax.all_to_all(spread(attn_in), "ctx", split_axis=2, concat_axis=0, tiled=True),
            lax.all_to_all(spread(attended), "ctx", split_axis=2, concat_axis=0, tiled=True),
            lax.all_to_all(spread(mlp_in), "ctx", split_axis=2, concat_axis=0, tiled=True),
            lax.all_to_all(spread(down_grad), "ctx", split_axis=2, concat_axis=0, tiled=True),
        )
        rights = (
            lax.all_gather(projected_grad, "ctx", axis=0, tiled=True),
            lax.all_gather(attn_grad, "ctx", axis=0, tiled=True),
            lax.all_gather(gate_up_grad, "ctx", axis=0, tiled=True),
            lax.all_gather(mixed, "ctx", axis=0, tiled=True),
        )
        totals = tuple(
            (
                total + contract_rows(left.reshape(ctx_count * row_count, group_rows), right)
                for total, left, right in zip(totals, lefts, rights)
            )
        )
    summed = (
        lax.psum_scatter(totals[0], "dp", scatter_dimension=0, tiled=True),
        lax.psum_scatter(totals[1], "dp", scatter_dimension=0, tiled=True),
        lax.psum_scatter(totals[2], "dp", scatter_dimension=0, tiled=True),
        lax.psum_scatter(totals[3], "dp", scatter_dimension=0, tiled=True),
    )
    gains = (
        lax.psum_scatter(gain_one_total, ("dp", "ctx"), scatter_dimension=0, tiled=True),
        lax.psum_scatter(gain_two_total, ("dp", "ctx"), scatter_dimension=0, tiled=True),
    )
    layer_out = jnp.stack(outputs)
    input_grad = jnp.stack(input_grads)
    return (layer_out, input_grad, gains[0], summed[0], summed[1], gains[1], summed[2], summed[3])


def solution(mesh):
    return jax.shard_map(
        on_device,
        mesh=mesh,
        in_specs=(
            P(None, "dp", "ctx", None),
            P(None, "dp", "ctx"),
            P(None, "dp", "ctx", None),
            P(("dp", "ctx")),
            P(("dp", "ctx"), None),
            P(("dp", "ctx"), None),
            P(("dp", "ctx")),
            P(("dp", "ctx"), None),
            P(("dp", "ctx"), None),
        ),
        out_specs=(
            P(None, "dp", "ctx", None),
            P(None, "dp", "ctx", None),
            P(("dp", "ctx")),
            P(("dp", "ctx"), None),
            P(("dp", "ctx"), None),
            P(("dp", "ctx")),
            P(("dp", "ctx"), None),
            P(("dp", "ctx"), None),
        ),
        check_vma=False,
    )
```

profile of v0, /device:TPU:0, one launch (start us, length us, event | category | flops | bytes accessed | tf_op | source)
XLA Modules:
  0.0 1947.0 jit_solution(7054132023474240150)
XLA Ops:
  9.6 43.0 %all-reduce.5 = (bf16[1024]{0:T(1024)(128)(2,1)S(1)}, bf16[1024]{0:T(1024)(128)(2,1)S(1)}) all-reduce(bf16[1024]{0:T(1024)(128)(2,1)S(1)} %dynamic-update-slice, bf16[1024]{0:T(1024)(128)(2,1)S(1)} %dynamic-update-slice.1), channel_id=1, replica_groups=mesh['dp'=8,'ctx'=4] {'dp','ctx'}, use_global_device_ids=true, to_apply=%add | all-reduce | flops 2048 | bytes 8192
  162.5 34.3 %all-gather.51.cloned.1.call-done = bf16[1024,1024]{1,0:T(8,128)(2,1)} async-done(((bf16[256,1024]{1,0:T(8,128)(2,1)}), bf16[1024,1024]{1,0:T(8,128)(2,1)}) %all-gather.51.cloned.1.call-update) | async-done | bytes 2097168 | tf_op jit(solution)/shard_map/all_gather | solution.py:121
  200.8 42.2 %all-gather.47.cloned.1.call-done = bf16[1024,1024]{1,0:T(8,128)(2,1)} async-done(((bf16[256,1024]{1,0:T(8,128)(2,1)}), bf16[1024,1024]{1,0:T(8,128)(2,1)}) %all-gather.47.cloned.1.call-update) | async-done | bytes 2097168 | tf_op jit(solution)/shard_map/all_gather | solution.py:121
  246.9 42.1 %all-gather.53.cloned.1.call-done = bf16[1024,1024]{1,0:T(8,128)(2,1)} async-done(((bf16[256,1024]{1,0:T(8,128)(2,1)}), bf16[1024,1024]{1,0:T(8,128)(2,1)}) %all-gather.53.cloned.1.call-update) | async-done | bytes 2097168 | tf_op jit(solution)/shard_map/all_gather | solution.py:118
  309.1 38.0 %all-gather.25.cloned.1.call-done = bf16[1024,1024]{1,0:T(8,128)(2,1)} async-done(((bf16[32,1024]{1,0:T(8,128)(2,1)}), bf16[1024,1024]{1,0:T(8,128)(2,1)}) %all-gather.25.cloned.1.call-update) | async-done | bytes 2097168 | tf_op jit(solution)/shard_map/all_gather | solution.py:80
  366.8 69.8 %all-gather.27.cloned.1.call-done = bf16[1024,5248]{1,0:T(8,128)(2,1)} async-done(((bf16[32,5248]{1,0:T(8,128)(2,1)}), bf16[1024,5248]{1,0:T(8,128)(2,1)}) %all-gather.27.cloned.1.call-update) | async-done | bytes 10747920 | tf_op jit(solution)/shard_map/all_gather | solution.py:82
  445.8 58.3 %all-gather.29.cloned.1.call-done = bf16[1024,2624]{1,0:T(8,128)(2,1)} async-done(((bf16[32,2624]{1,0:T(8,128)(2,1)}), bf16[1024,2624]{1,0:T(8,128)(2,1)}) %all-gather.29.cloned.1.call-update) | async-done | bytes 5373968 | tf_op jit(solution)/shard_map/all_gather | solution.py:83
  670.0 41.7 %reduce-scatter.11.cloned.1.call-done = bf16[1,256,1024]{1,2,0:T(8,128)(2,1)} async-done(((bf16[1,1024,1024]{1,2,0:T(8,128)(2,1)}), bf16[1,256,1024]{1,2,0:T(8,128)(2,1)}) %reduce-scatter.11.cloned.1.call-update) | async-done | bytes 524304 | tf_op jit(solution)/shard_map/reduce_scatter | solution.py:208
  714.0 43.1 %reduce-scatter.15.cloned.1.call-done = bf16[1,256,1024]{1,2,0:T(8,128)(2,1)} async-done(((bf16[1,1024,1024]{1,2,0:T(8,128)(2,1)}), bf16[1,256,1024]{1,2,0:T(8,128)(2,1)}) %reduce-scatter.15.cloned.1.call-update) | async-done | bytes 524304 | tf_op jit(solution)/shard_map/reduce_scatter | solution.py:208
  766.1 27.9 %all-to-all-done.2 = bf16[256,8,4,32]{0,3,1,2:T(8,128)(2,1)S(1)} async-done(((bf16[256,8,4,32]{0,3,1,2:T(8,128)(2,1)}), bf16[256,8,4,32]{0,3,1,2:T(8,128)(2,1)S(1)}, u32[]{:S(2)}, u32[]{:S(2)}) %all-to-all-start.2) | async-done | bytes 524320 | tf_op jit(solution)/shard_map/all_to_all | solution.py:236
  854.0 30.9 %all-gather.37.cloned.1.call-done = bf16[1024,1024]{1,0:T(8,128)(2,1)} async-done(((bf16[256,1024]{1,0:T(8,128)(2,1)}), bf16[1024,1024]{1,0:T(8,128)(2,1)}) %all-gather.37.cloned.1.call-update) | async-done | bytes 2097168 | tf_op jit(solution)/shard_map/all_gather | solution.py:242
  890.4 97.1 %all-gather.43.cloned.1.call-done = bf16[1024,2624]{1,0:T(8,128)(2,1)} async-done(((bf16[256,2624]{1,0:T(8,128)(2,1)}), bf16[1024,2624]{1,0:T(8,128)(2,1)}) %all-gather.43.cloned.1.call-update) | async-done | bytes 5373968 | tf_op jit(solution)/shard_map/all_gather | solution.py:244
  993.2 96.5 %all-gather.45.cloned.1.call-done = bf16[1024,2624]{1,0:T(8,128)(2,1)} async-done(((bf16[256,2624]{1,0:T(8,128)(2,1)}), bf16[1024,2624]{1,0:T(8,128)(2,1)}) %all-gather.45.cloned.1.call-update) | async-done | bytes 5373968 | tf_op jit(solution)/shard_map/all_gather | solution.py:244
  1105.1 31.6 %all-to-all-done.1 = bf16[256,8,4,32]{0,3,1,2:T(8,128)(2,1)S(1)} async-done(((bf16[256,8,4,32]{0,3,1,2:T(8,128)(2,1)}), bf16[256,8,4,32]{0,3,1,2:T(8,128)(2,1)S(1)}, u32[]{:S(2)}, u32[]{:S(2)}) %all-to-all-start.1) | async-done | bytes 524320 | tf_op jit(solution)/shard_map/all_to_all | solution.py:235
  1140.7 37.5 %all-to-all-done = bf16[256,8,4,32]{0,3,1,2:T(8,128)(2,1)S(1)} async-done(((bf16[256,8,4,32]{0,3,1,2:T(8,128)(2,1)}), bf16[256,8,4,32]{0,3,1,2:T(8,128)(2,1)S(1)}, u32[]{:S(2)}, u32[]{:S(2)}) %all-to-all-start) | async-done | bytes 524320 | tf_op jit(solution)/shard_map/all_to_all | solution.py:235
  1178.7 48.6 %all-gather.31.cloned.1.call-done = bf16[1024,3072]{0,1:T(8,128)(2,1)} async-done(((bf16[256,3072]{0,1:T(8,128)(2,1)}), bf16[1024,3072]{0,1:T(8,128)(2,1)}) %all-gather.31.cloned.1.call-update) | async-done | bytes 6291472 | tf_op jit(solution)/shard_map/all_gather | solution.py:241
  1233.7 110.2 %all-gather.33.cloned.1.call-done = bf16[1024,3072]{0,1:T(8,128)(2,1)} async-done(((bf16[256,3072]{0,1:T(8,128)(2,1)}), bf16[1024,3072]{0,1:T(8,128)(2,1)}) %all-gather.33.cloned.1.call-update) | async-done | bytes 6291472 | tf_op jit(solution)/shard_map/all_gather | solution.py:241
  1357.8 31.8 %all-to-all-done.4 = bf16[256,8,4,32]{0,3,1,2:T(8,128)(2,1)S(1)} async-done(((bf16[256,8,4,32]{0,3,1,2:T(8,128)(2,1)}), bf16[256,8,4,32]{0,3,1,2:T(8,128)(2,1)S(1)}, u32[]{:S(2)}, u32[]{:S(2)}) %all-to-all-start.4) | async-done | bytes 524320 | tf_op jit(solution)/shard_map/all_to_all | solution.py:237
  1393.8 33.2 %all-to-all-done.5 = bf16[256,8,4,32]{0,3,1,2:T(8,128)(2,1)S(1)} async-done(((bf16[256,8,4,32]{0,3,1,2:T(8,128)(2,1)}), bf16[256,8,4,32]{0,3,1,2:T(8,128)(2,1)S(1)}, u32[]{:S(2)}, u32[]{:S(2)}) %all-to-all-start.5) | async-done | bytes 524320 | tf_op jit(solution)/shard_map/all_to_all | solution.py:237
  1427.5 126.7 %all-gather.39.cloned.1.call-done = bf16[1024,5248]{1,0:T(8,128)(2,1)} async-done(((bf16[256,5248]{1,0:T(8,128)(2,1)}), bf16[1024,5248]{1,0:T(8,128)(2,1)}) %all-gather.39.cloned.1.call-update) | async-done | bytes 10747920 | tf_op jit(solution)/shard_map/all_gather | solution.py:243
  1563.0 179.0 %all-gather.41.cloned.1.call-done = bf16[1024,5248]{1,0:T(8,128)(2,1)} async-done(((bf16[256,5248]{1,0:T(8,128)(2,1)}), bf16[1024,5248]{1,0:T(8,128)(2,1)}) %all-gather.41.cloned.1.call-update) | async-done | bytes 10747920 | tf_op jit(solution)/shard_map/all_gather | solution.py:243
  1768.9 38.5 %all-reduce.4 = (f32[1024]{0:T(1024)S(1)}, f32[1024]{0:T(1024)S(1)}) all-reduce(f32[1024]{0:T(1024)S(1)} %add.236, f32[1024]{0:T(1024)S(1)} %add.239), channel_id=12, replica_groups=mesh['dp'=8,'ctx'=4] {'dp','ctx'}, use_global_device_ids=true, to_apply=%region_28.29.clone | all-reduce | flops 2048 | bytes 16384
  1828.3 50.6 %reduce-scatter.17.cloned.1.call-done = f32[32,3072]{1,0:T(8,128)} async-done(((f32[256,3072]{1,0:T(8,128)}), f32[32,3072]{1,0:T(8,128)}) %reduce-scatter.17.cloned.1.call-update) | async-done | bytes 393232 | tf_op jit(solution)/shard_map/reduce_scatter | solution.py:253
  1878.9 61.1 %reduce-scatter.21.cloned.1.call-done = f32[32,5248]{1,0:T(8,128)} async-done(((f32[256,5248]{1,0:T(8,128)}), f32[32,5248]{1,0:T(8,128)}) %reduce-scatter.21.cloned.1.call-update) | async-done | bytes 671760 | tf_op jit(solution)/shard_map/reduce_scatter | solution.py:255
  (422 shorter events, 517.2 us)
Async XLA Ops:
  7.2 76.2 %all-gather.23.cloned.1.call-start = ((), (), s32[]{:S(2)}) async-start(), calls=%async_computation.16 | async-start | bytes 6488064 | tf_op jit(solution)/shard_map/all_gather | solution.py:79
  7.9 142.1 %all-gather.49.cloned.1.call-start = ((), (), s32[]{:S(2)}) async-start(), calls=%async_computation.37 | async-start | bytes 2621440 | tf_op jit(solution)/shard_map/all_gather | solution.py:118
  105.3 91.5 %all-gather.51.cloned.1.call-start = ((), (), s32[]{:S(2)}) async-start(), calls=%async_computation.38 | async-start | bytes 2621440 | tf_op jit(solution)/shard_map/all_gather | solution.py:121
  107.5 135.5 %all-gather.47.cloned.1.call-start = ((), (), s32[]{:S(2)}) async-start(), calls=%async_computation.36 | async-start | bytes 2621440 | tf_op jit(solution)/shard_map/all_gather | solution.py:121
  109.7 179.4 %all-gather.53.cloned.1.call-start = ((), (), s32[]{:S(2)}) async-start(), calls=%async_computation.39 | async-start | bytes 2621440 | tf_op jit(solution)/shard_map/all_gather | solution.py:118
  110.3 236.8 %all-gather.25.cloned.1.call-start = ((), (), s32[]{:S(2)}) async-start(), calls=%async_computation.17 | async-start | bytes 2162688 | tf_op jit(solution)/shard_map/all_gather | solution.py:80
  110.9 325.7 %all-gather.27.cloned.1.call-start = ((), (), s32[]{:S(2)}) async-start(), calls=%async_computation.18 | async-start | bytes 11083776 | tf_op jit(solution)/shard_map/all_gather | solution.py:82
  111.6 392.5 %all-gather.29.cloned.1.call-start = ((), (), s32[]{:S(2)}) async-start(), calls=%async_computation.19 | async-start | bytes 5677056 | tf_op jit(solution)/shard_map/all_gather | solution.py:83
  112.3 536.4 %reduce-scatter.13.cloned.1.call-start = ((), (), s32[]{:S(2)}) async-start(), calls=%async_computation.22 | async-start | bytes 2621440 | tf_op jit(solution)/shard_map/reduce_scatter | solution.py:202
  577.9 88.3 %reduce-scatter.9.cloned.1.call-start = ((), (), s32[]{:S(2)}) async-start(), calls=%async_computation.20 | async-start | bytes 2621440 | tf_op jit(solution)/shard_map/reduce_scatter | solution.py:202
  612.2 99.4 %reduce-scatter.11.cloned.1.call-start = ((), (), s32[]{:S(2)}) async-start(), calls=%async_computation.21 | async-start | bytes 2621440 | tf_op jit(solution)/shard_map/reduce_scatter | solution.py:208
  621.7 135.5 %reduce-scatter.15.cloned.1.call-start = ((), (), s32[]{:S(2)}) async-start(), calls=%async_computation.23 | async-start | bytes 2621440 | tf_op jit(solution)/shard_map/reduce_scatter | solution.py:208
  630.8 201.0 %all-gather.35.cloned.1.call-start = ((), (), s32[]{:S(2)}) async-start(), calls=%async_computation.27 | async-start | bytes 2621440 | tf_op jit(solution)/shard_map/all_gather | solution.py:242
  631.5 253.4 %all-gather.37.cloned.1.call-start = ((), (), s32[]{:S(2)}) async-start(), calls=%async_computation.28 | async-start | bytes 2621440 | tf_op jit(solution)/shard_map/all_gather | solution.py:242
  632.1 355.4 %all-gather.43.cloned.1.call-start = ((), (), s32[]{:S(2)}) async-start(), calls=%async_computation.33 | async-start | bytes 6881280 | tf_op jit(solution)/shard_map/all_gather | solution.py:244
  632.7 457.0 %all-gather.45.cloned.1.call-start = ((), (), s32[]{:S(2)}) async-start(), calls=%async_computation.34 | async-start | bytes 6881280 | tf_op jit(solution)/shard_map/all_gather | solution.py:244
  633.3 594.1 %all-gather.31.cloned.1.call-start = ((), (), s32[]{:S(2)}) async-start(), calls=%async_computation.24 | async-start | bytes 7864320 | tf_op jit(solution)/shard_map/all_gather | solution.py:241
  714.0 629.9 %all-gather.33.cloned.1.call-start = ((), (), s32[]{:S(2)}) async-start(), calls=%async_computation.25 | async-start | bytes 7864320 | tf_op jit(solution)/shard_map/all_gather | solution.py:241
  759.5 794.7 %all-gather.39.cloned.1.call-start = ((), (), s32[]{:S(2)}) async-start(), calls=%async_computation.30 | async-start | bytes 13434880 | tf_op jit(solution)/shard_map/all_gather | solution.py:243
  760.3 981.7 %all-gather.41.cloned.1.call-start = ((), (), s32[]{:S(2)}) async-start(), calls=%async_computation.31 | async-start | bytes 13434880 | tf_op jit(solution)/shard_map/all_gather | solution.py:243
  854.0 958.0 %reduce-scatter.19.cloned.1.call-start = ((), (), s32[]{:S(2)}) async-start(), calls=%async_computation.29 | async-start | bytes 1179648 | tf_op jit(solution)/shard_map/reduce_scatter | solution.py:254
  888.3 940.0 %reduce-scatter.23.cloned.1.call-start = ((), (), s32[]{:S(2)}) async-start(), calls=%async_computation.35 | async-start | bytes 3096576 | tf_op jit(solution)/shard_map/reduce_scatter | solution.py:256
  1140.1 738.8 %reduce-scatter.17.cloned.1.call-start = ((), (), s32[]{:S(2)}) async-start(), calls=%async_computation.26 | async-start | bytes 3538944 | tf_op jit(solution)/shard_map/reduce_scatter | solution.py:253
  1393.1 546.9 %reduce-scatter.21.cloned.1.call-start = ((), (), s32[]{:S(2)}) async-start(), calls=%async_computation.32 | async-start | bytes 6045696 | tf_op jit(solution)/shard_map/reduce_scatter | solution.py:255
  (100 other events, 1824.7 us)
Sparse Core Ops, SparseCore 0:
  10.9 72.4 all-gather.22
  105.4 44.5 all-gather.48
  152.2 44.6 all-gather.50
  198.3 44.6 all-gather.46
  244.4 44.6 all-gather.52
  291.9 55.1 all-gather.24
  349.9 86.5 all-gather.26
  439.4 64.6 all-gather.28
  578.0 42.8 reduce-scatter.12
  623.1 42.9 reduce-scatter.8
  668.5 43.1 reduce-scatter.10
  713.9 43.1 reduce-scatter.14
  758.7 66.4 all-gather.34
  826.6 58.2 all-gather.36
  886.3 101.0 all-gather.42
  988.9 100.7 all-gather.44
  1091.1 136.2 all-gather.30
  1228.8 115.0 all-gather.32
  1345.4 208.7 all-gather.38
  1555.6 186.3 all-gather.40
  1745.8 34.2 reduce-scatter.18
  1784.0 44.2 reduce-scatter.22
  1832.6 46.2 reduce-scatter.16
  1882.8 57.1 reduce-scatter.20
where the time goes:
time: 1960 us; the launch traced here: 1950 us
  waiting for transfers between devices  1440 us (73%)
  matrix products  215 us (11%)
  blocking collectives  99.1 us (5%)
  local copies, waits for them, and re-layouts  74.2 us (4%)
  other arithmetic  64.9 us (3%)
  starting transfers between devices  32.5 us (2%)
    all_gather x2, waiting for transfers between devices, on_device(): lax.all_gather(gate_up_grad, 'ctx', axis=0, tiled=True)  306 us
    all_gather x2, waiting for transfers between devices, on_device(): lax.all_gather(mixed, 'ctx', axis=0, tiled=True)  194 us
    all_gather x2, waiting for transfers between devices, on_device(): lax.all_gather(projected_grad, 'ctx', axis=0, tiled=True)  159 us
    reduce_scatter x2, waiting for transfers between devices, on_device(): lax.psum_scatter(value_terms.reshape(seq_count, full_len, model_width).as...  84.8 us
    unnamed x2, blocking collectives  81.6 us
    all_gather x2, waiting for transfers between devices, on_device(): lax.all_gather(values_local, 'ctx', axis=1, tiled=True)  76.5 us
    all_gather x1, waiting for transfers between devices, on_device(): lax.all_gather(w_in, ('dp', 'ctx'), axis=0, tiled=True)  69.8 us
    all_to_all x2, waiting for transfers between devices, on_device(): lax.all_to_all(spread(attn_in), 'ctx', split_axis=2, concat_axis=0, tiled...  69.1 us
  transfers between devices with their start and end apart: 32, of which 28 were waited for; matrix products, arithmetic and copies ran while one was open for 13% of the time, Pallas kernels for 0%

commit v1 on v0

v1 whole, which is shorter than its diff:
```python
import functools
import math

import jax
import jax.numpy as jnp
from jax import lax
from jax.experimental import pallas as pl
from jax.experimental.pallas import tpu as pltpu
from jax.sharding import PartitionSpec as P

HEADS = 16
HEAD = 64
LANE = 128

epsilon = 1e-05
rope_base = 160000.0
NEG = -1e30
LOG2E = math.log2(math.e)

F32 = jnp.float32
BF16 = jnp.bfloat16
ANY = pl.BlockSpec(memory_space=pl.ANY)
SMEM = pl.BlockSpec(memory_space=pltpu.SMEM)


def params(*, mib=56):
    return pltpu.CompilerParams(vmem_limit_bytes=mib << 20)


def sds(shape, dtype):
    return jax.ShapeDtypeStruct(shape, dtype)


def nt(a, b):
    return lax.dot_general(a, b, (((1,), (1,)), ((), ())), preferred_element_type=F32)


def nn(a, b):
    return lax.dot_general(a, b, (((1,), (0,)), ((), ())), preferred_element_type=F32)


def lanes(perm, m):
    return pl.ds(pl.multiple_of(perm[m] * LANE, LANE), LANE)


def weight_copies(pieces, col, count, dst, dst_col, sems):
    out = []
    for m, piece in enumerate(pieces):
        rows = piece.shape[0]
        out.append(
            pltpu.make_async_copy(
                piece.at[:, col : col + count],
                dst.at[m * rows : (m + 1) * rows, dst_col : dst_col + count],
                sems.at[m],
            )
        )
    return out


def start(copies):
    for c in copies:
        c.start()


def wait(copies):
    for c in copies:
        c.wait()


def norm_rows(v):
    centered = v - jnp.mean(v, axis=-1, keepdims=True)
    inv = lax.rsqrt(jnp.mean(centered * centered, axis=-1, keepdims=True) + epsilon)
    return centered * inv, inv


def turn(u, cos, sin):
    first = lax.broadcasted_iota(jnp.int32, (1, LANE), 1) % HEAD < HEAD // 2
    out = []
    for h in range(u.shape[1] // LANE):
        b = u[:, h * LANE : (h + 1) * LANE]
        t = jnp.where(first, pltpu.roll(b, LANE - HEAD // 2, 1), pltpu.roll(b, HEAD // 2, 1))
        out.append(b * cos + t * sin)
    return jnp.concatenate(out, axis=1)


def qkv_body(n0, n1, perm, x_ref, cos_ref, sin_ref, *rest):
    p0, p1 = rest[:n0], rest[n0 : n0 + n1]
    a_ref, q_ref, kv_ref, gains_ref, w, g, ap, sems = rest[n0 + n1 :]
    j = pl.program_id(0)
    chunk = q_ref.shape[1]
    steps = w.shape[1] // chunk
    half = steps // 2

    def copies(s):
        if s < half:
            return weight_copies(p0, s * chunk, chunk, w, s * chunk, sems.at[s])
        return weight_copies(p1, (s - half) * chunk, chunk, w, s * chunk, sems.at[s])

    gain_copies = weight_copies(p0, half * chunk, LANE, g, 0, sems.at[steps])

    @pl.when(j == 0)
    def _():
        start(gain_copies)
        for s in range(steps):
            start(copies(s))
        wait(gain_copies)
        blocks = a_ref.shape[1] // LANE
        for m in range(blocks):
            t = g[m * LANE : (m + 1) * LANE, :].astype(F32).T
            gains_ref[:, lanes(perm, m)] = t[0:8, :]

        def rows(i, carry):
            r = pl.ds(pl.multiple_of(i * LANE, LANE), LANE)
            normed, _ = norm_rows(x_ref[r, :].astype(F32))
            a_ref[r, :] = (normed * gains_ref[0:1, :]).astype(BF16)
            return carry

        lax.fori_loop(0, a_ref.shape[0] // LANE, rows, 0)
        for m in range(blocks):
            ap[:, m * LANE : (m + 1) * LANE] = a_ref[:, lanes(perm, m)]

    for s in range(steps):

        @pl.when(j == s)
        def _(s=s):
            wait(copies(s))

    u = nn(ap[...], w[:, pl.ds(pl.multiple_of(j * chunk, chunk), chunk)])
    third = steps // 3

    @pl.when(j < third)
    def _():
        q_ref[...] = turn(u, cos_ref[...], sin_ref[...]).astype(BF16)

    @pl.when((j >= third) & (j < 2 * third))
    def _():
        kv_ref[...] = turn(u, cos_ref[...], sin_ref[...]).astype(BF16)

    @pl.when(j >= 2 * third)
    def _():
        kv_ref[...] = u.astype(BF16)


def qkv_call(perm, x, cos, sin, p0, p1):
    rows, width = x.shape
    chunk = 512
    steps = 3 * width // chunk
    third = steps // 3
    full = lambda j: (0, 0)
    return pl.pallas_call(
        functools.partial(qkv_body, len(p0), len(p1)),
        grid=(steps,),
        out_shape=(
            sds((rows, width), BF16),
            sds((rows, width), BF16),
            sds((rows, 2 * width), BF16),
            sds((8, width), F32),
        ),
        in_specs=[
            SMEM,
            pl.BlockSpec((rows, width), full),
            pl.BlockSpec((rows, LANE), full),
            pl.BlockSpec((rows, LANE), full),
        ]
        + [ANY] * (len(p0) + len(p1)),
        out_specs=(
            pl.BlockSpec((rows, width), full),
            pl.BlockSpec((rows, chunk), lambda j: (0, jnp.minimum(j, third - 1))),
            pl.BlockSpec((rows, chunk), lambda j: (0, jnp.maximum(j - third, 0))),
            pl.BlockSpec((8, width), full),
        ),
        scratch_shapes=[
            pltpu.VMEM((width, 3 * width), BF16),
            pltpu.VMEM((width, LANE), BF16),
            pltpu.VMEM((rows, width), BF16),
            pltpu.SemaphoreType.DMA((steps + 1, len(p0))),
        ],
        compiler_params=params(),
        cost_estimate=pl.CostEstimate(
            flops=6 * rows * width * width, transcendentals=0, bytes_accessed=6 * width * width + 10 * rows * width
        ),
        name="qkv",
    )(perm, x, cos, sin, *p0, *p1)


def attend_body(segk_ref, segq_ref, q_ref, k0_ref, k1_ref, v0_ref, v1_ref, o_ref, lse_ref, bias, vt):
    j = pl.program_id(0)
    rows = q_ref.shape[0]
    tile = 256

    @pl.when(j == 0)
    def _():
        bias[...] = jnp.where(segk_ref[...] == segq_ref[...], 0.0, NEG)

    for i in range(rows // LANE):
        r = slice(i * LANE, (i + 1) * LANE)
        vt[:, r] = v0_ref[r, :].astype(F32).T.astype(BF16)
        vt[:, rows + i * LANE : rows + (i + 1) * LANE] = v1_ref[r, :].astype(F32).T.astype(BF16)
    head_of = lax.broadcasted_iota(jnp.int32, (1, LANE), 1) // HEAD
    scale = LOG2E / math.sqrt(HEAD)
    for t in range(rows // tile):
        cols = slice(t * tile, (t + 1) * tile)
        q = q_ref[cols, :]
        parts = []
        for h in range(LANE // HEAD):
            qm = jnp.where(head_of == h, q, jnp.zeros_like(q))
            s = jnp.concatenate([nt(k0_ref[...], qm), nt(k1_ref[...], qm)], axis=0) * scale + bias[:, cols]
            top = jnp.max(s, axis=0, keepdims=True)
            e = jnp.exp2(s - top)
            total = jnp.sum(e, axis=0, keepdims=True)
            p = (e * (1.0 / total)).astype(BF16)
            ot = nn(vt[...], p)
            parts.append(ot[h * HEAD : (h + 1) * HEAD, :])
            lse_ref[0, h : h + 1, cols] = top + jnp.log2(total)
        o_ref[cols, :] = jnp.concatenate(parts, axis=0).T.astype(BF16)


def attend_call(segk, segq, q, kv0, kv1):
    rows, width = q.shape
    pairs = width // LANE
    full = lambda j: (0, 0)
    at = lambda j: (0, j)
    vat = lambda j: (0, pairs + j)
    block = (rows, LANE)
    return pl.pallas_call(
        attend_body,
        grid=(pairs,),
        out_shape=(sds((rows, width), BF16), sds((pairs, 8, rows), F32)),
        in_specs=[
            pl.BlockSpec((2 * rows, 1), full),
            pl.BlockSpec((1, rows), full),
            pl.BlockSpec(block, at),
            pl.BlockSpec(block, at),
            pl.BlockSpec(block, at),
            pl.BlockSpec(block, vat),
            pl.BlockSpec(block, vat),
        ],
        out_specs=(pl.BlockSpec(block, at), pl.BlockSpec((1, 8, rows), lambda j: (j, 0, 0))),
        scratch_shapes=[pltpu.VMEM((2 * rows, rows), F32), pltpu.VMEM((LANE, 2 * rows), BF16)],
        compiler_params=params(),
        cost_estimate=pl.CostEstimate(
            flops=16 * rows * rows * width, transcendentals=2 * rows * rows * HEADS, bytes_accessed=12 * rows * width
        ),
        name="attend",
    )(segk, segq, q, kv0, kv1, kv0, kv1)


def middle_body(n, perm, gains_ref, x_ref, keep_ref, o_ref, *rest):
    pieces = rest[:n]
    h1_ref, b_ref, w, op, sems = rest[n:]
    copies = weight_copies(pieces, 0, w.shape[1], w, 0, sems)

    @pl.when(pl.program_id(0) == 0)
    def _():
        start(copies)

    for m in range(op.shape[1] // LANE):
        op[:, m * LANE : (m + 1) * LANE] = o_ref[:, lanes(perm, m)]

    @pl.when(pl.program_id(0) == 0)
    def _():
        wait(copies)

    h1 = x_ref[...].astype(F32) + keep_ref[...] * nn(op[...], w[...])
    h1_ref[...] = h1
    normed, _ = norm_rows(h1)
    b_ref[...] = (normed * gains_ref[1:2, :]).astype(BF16)


def middle_call(perm, gains, x, keep, o, pieces):
    rows, width = x.shape
    tile = 128
    full = lambda i: (0, 0)
    row = lambda i: (i, 0)
    return pl.pallas_call(
        functools.partial(middle_body, len(pieces)),
        grid=(rows // tile,),
        out_shape=(sds((rows, width), F32), sds((rows, width), BF16)),
        in_specs=[
            SMEM,
            pl.BlockSpec((8, width), full),
            pl.BlockSpec((tile, width), row),
            pl.BlockSpec((tile, 1), row),
            pl.BlockSpec((tile, width), row),
        ]
        + [ANY] * len(pieces),
        out_specs=(pl.BlockSpec((tile, width), row), pl.BlockSpec((tile, width), row)),
        scratch_shapes=[
            pltpu.VMEM((width, width), BF16),
            pltpu.VMEM((tile, width), BF16),
            pltpu.SemaphoreType.DMA((len(pieces),)),
        ],
        compiler_params=params(),
        cost_estimate=pl.CostEstimate(
            flops=2 * rows * width * width, transcendentals=0, bytes_accessed=2 * width * width + 10 * rows * width
        ),
        name="middle",
    )(perm, gains, x, keep, o, *pieces)


def gate_body(n, perm, b_ref, *rest):
    pg, pu = rest[:n], rest[n : 2 * n]
    m_ref, f1_ref, f2_ref, wg, wu, bp, sems = rest[2 * n :]
    j = pl.program_id(0)
    chunk = m_ref.shape[1]
    steps = wg.shape[1] // chunk

    def copies(s):
        return weight_copies(pg, s * chunk, chunk, wg, s * chunk, sems.at[s, 0]) + weight_copies(
            pu, s * chunk, chunk, wu, s * chunk, sems.at[s, 1]
        )

    @pl.when(j == 0)
    def _():
        for s in range(steps):
            start(copies(s))
        for m in range(bp.shape[1] // LANE):
            bp[:, m * LANE : (m + 1) * LANE] = b_ref[:, lanes(perm, m)]

    for s in range(steps):

        @pl.when(j == s)
        def _(s=s):
            wait(copies(s))

    cols = pl.ds(pl.multiple_of(j * chunk, LANE), chunk)
    rows = bp.shape[0]
    tile = 128

    def step(i, carry):
        r = pl.ds(pl.multiple_of(i * tile, tile), tile)
        gate = nn(bp[r, :], wg[:, cols])
        up = nn(bp[r, :], wu[:, cols])
        cdf = 0.5 * (1.0 + lax.erf(gate * (1.0 / math.sqrt(2.0))))
        density = jnp.exp(-0.5 * gate * gate) * (1.0 / math.sqrt(2.0 * math.pi))
        act = gate * cdf
        m_ref[r, :] = (act * up).astype(BF16)
        f1_ref[r, :] = (up * (cdf + gate * density)).astype(f1_ref.dtype)
        f2_ref[r, :] = act.astype(f2_ref.dtype)
        return carry

    lax.fori_loop(0, rows // tile, step, 0)


def gate_call(perm, b, pg, pu, hidden):
    rows, width = b.shape
    chunk = hidden // 3
    full = lambda j: (0, 0)
    at = lambda j: (0, j)
    return pl.pallas_call(
        functools.partial(gate_body, len(pg)),
        grid=(hidden // chunk,),
        out_shape=(sds((rows, hidden), BF16), sds((rows, hidden), BF16), sds((rows, hidden), BF16)),
        in_specs=[SMEM, pl.BlockSpec((rows, width), full)] + [ANY] * (2 * len(pg)),
        out_specs=(pl.BlockSpec((rows, chunk), at),) * 3,
        scratch_shapes=[
            pltpu.VMEM((width, hidden), BF16),
            pltpu.VMEM((width, hidden), BF16),
            pltpu.VMEM((rows, width), BF16),
            pltpu.SemaphoreType.DMA((hidden // chunk, 2, len(pg))),
        ],
        compiler_params=params(),
        cost_estimate=pl.CostEstimate(
            flops=4 * rows * width * hidden,
            transcendentals=2 * rows * hidden,
            bytes_accessed=4 * width * hidden + 6 * rows * hidden,
        ),
        name="gate",
    )(perm, b, *pg, *pu)


def dgate_body(n, perm, cot_ref, keep_ref, f1_ref, f2_ref, *rest):
    pd = rest[:n]
    dg_ref, du_ref, wd, ep, sems = rest[n:]
    j = pl.program_id(0)
    chunk = dg_ref.shape[1]
    steps = wd.shape[1] // chunk

    def copies(s):
        return weight_copies(pd, s * chunk, chunk, wd, s * chunk, sems.at[s])

    @pl.when(j == 0)
    def _():
        for s in range(steps):
            start(copies(s))
        for m in range(ep.shape[1] // LANE):
            ep[:, m * LANE : (m + 1) * LANE] = (keep_ref[...] * cot_ref[:, lanes(perm, m)].astype(F32)).astype(BF16)

    for s in range(steps):

        @pl.when(j == s)
        def _(s=s):
            wait(copies(s))

    cols = pl.ds(pl.multiple_of(j * chunk, LANE), chunk)
    rows = ep.shape[0]
    tile = 256

    def step(i, carry):
        r = pl.ds(pl.multiple_of(i * tile, tile), tile)
        dm = nn(ep[r, :], wd[:, cols])
        dg_ref[r, :] = (dm * f1_ref[r, :].astype(F32)).astype(BF16)
        du_ref[r, :] = (dm * f2_ref[r, :].astype(F32)).astype(BF16)
        return carry

    lax.fori_loop(0, rows // tile, step, 0)


def dgate_call(perm, cot, keep, f1, f2, pd):
    rows, width = cot.shape
    hidden = f1.shape[1]
    chunk = hidden // 3
    full = lambda j: (0, 0)
    at = lambda j: (0, j)
    return pl.pallas_call(
        functools.partial(dgate_body, len(pd)),
        grid=(hidden // chunk,),
        out_shape=(sds((rows, hidden), BF16), sds((rows, hidden), BF16)),
        in_specs=[
            SMEM,
            pl.BlockSpec((rows, width), full),
            pl.BlockSpec((rows, 1), full),
            pl.BlockSpec((rows, chunk), at),
            pl.BlockSpec((rows, chunk), at),
        ]
        + [ANY] * len(pd),
        out_specs=(pl.BlockSpec((rows, chunk), at),) * 2,
        scratch_shapes=[
            pltpu.VMEM((width, hidden), BF16),
            pltpu.VMEM((rows, width), BF16),
            pltpu.SemaphoreType.DMA((hidden // chunk, len(pd))),
        ],
        compiler_params=params(),
        cost_estimate=pl.CostEstimate(
            flops=2 * rows * width * hidden, transcendentals=0, bytes_accessed=2 * width * hidden + 8 * rows * hidden
        ),
        name="dgate",
    )(perm, cot, keep, f1, f2, *pd)


def down_body(n, perm, h1_ref, keep_ref, m_ref, *rest):
    pd = rest[:n]
    out_ref, wd, acc, sems = rest[n:]
    j = pl.program_id(0)
    chunk = m_ref.shape[1]
    steps = wd.shape[1] // chunk

    def copies(s):
        return weight_copies(pd, s * chunk, chunk, wd, s * chunk, sems.at[s])

    @pl.when(j == 0)
    def _():
        for s in range(steps):
            start(copies(s))
        acc[...] = jnp.zeros_like(acc)

    for s in range(steps):

        @pl.when(j == s)
        def _(s=s):
            wait(copies(s))

    cols = pl.ds(pl.multiple_of(j * chunk, LANE), chunk)
    acc[...] += nt(m_ref[...], wd[:, cols])

    @pl.when(j == steps - 1)
    def _():
        for m in range(acc.shape[1] // LANE):
            at = lanes(perm, m)
            out_ref[:, at] = (h1_ref[:, at] + keep_ref[...] * acc[:, m * LANE : (m + 1) * LANE]).astype(BF16)


def down_call(perm, h1, keep, mixed, pd):
    rows, width = h1.shape
    hidden = mixed.shape[1]
    chunk = hidden // 3
    full = lambda j: (0, 0)
    at = lambda j: (0, j)
    return pl.pallas_call(
        functools.partial(down_body, len(pd)),
        grid=(hidden // chunk,),
        out_shape=sds((rows, width), BF16),
        in_specs=[
            SMEM,
            pl.BlockSpec((rows, width), full),
            pl.BlockSpec((rows, 1), full),
            pl.BlockSpec((rows, chunk), at),
        ]
        + [ANY] * len(pd),
        out_specs=pl.BlockSpec((rows, width), full),
        scratch_shapes=[
            pltpu.VMEM((width, hidden), BF16),
            pltpu.VMEM((rows, width), F32),
            pltpu.SemaphoreType.DMA((hidden // chunk, len(pd))),
        ],
        compiler_params=params(),
        cost_estimate=pl.CostEstimate(
            flops=2 * rows * width * hidden, transcendentals=0, bytes_accessed=2 * width * hidden + 2 * rows * hidden
        ),
        name="down",
    )(perm, h1, keep, mixed, *pd)


def norm_back(e, gain, normed, inv):
    scaled = e * gain
    return inv * (
        scaled
        - jnp.mean(scaled, axis=-1, keepdims=True)
        - normed * jnp.mean(scaled * normed, axis=-1, keepdims=True)
    )


def dmiddle_body(n, perm, gains_ref, cot_ref, keep_ref, h1_ref, dg_ref, du_ref, *rest):
    pg, pu, po = rest[:n], rest[n : 2 * n], rest[2 * n : 3 * n]
    dh1_ref, e_ref, do_ref, gg_ref, wg, wu, wo, acc, db, sems, osems = rest[3 * n :]
    j = pl.program_id(0)
    chunk = dg_ref.shape[1]
    steps = wg.shape[1] // chunk

    def copies(s):
        return weight_copies(pg, s * chunk, chunk, wg, s * chunk, sems.at[s, 0]) + weight_copies(
            pu, s * chunk, chunk, wu, s * chunk, sems.at[s, 1]
        )

    out_copies = weight_copies(po, 0, wo.shape[1], wo, 0, osems)

    @pl.when(j == 0)
    def _():
        for s in range(steps):
            start(copies(s))
        start(out_copies)
        acc[...] = jnp.zeros_like(acc)

    for s in range(steps):

        @pl.when(j == s)
        def _(s=s):
            wait(copies(s))

    cols = pl.ds(pl.multiple_of(j * chunk, LANE), chunk)
    acc[...] += nt(dg_ref[...], wg[:, cols]) + nt(du_ref[...], wu[:, cols])

    @pl.when(j == steps - 1)
    def _():
        blocks = acc.shape[1] // LANE
        for m in range(blocks):
            db[:, lanes(perm, m)] = acc[:, m * LANE : (m + 1) * LANE]
        wait(out_copies)
        gg_ref[...] = jnp.zeros_like(gg_ref)
        tile = 128

        def step(i, carry):
            r = pl.ds(pl.multiple_of(i * tile, tile), tile)
            normed, inv = norm_rows(h1_ref[r, :])
            e = db[r, :]
            gg_ref[...] += jnp.sum(e * normed, axis=0, keepdims=True)
            dh1 = cot_ref[r, :].astype(F32) + norm_back(e, gains_ref[1:2, :], normed, inv)
            dh1_ref[r, :] = dh1
            ea = (keep_ref[r, :] * dh1).astype(BF16)
            e_ref[r, :] = ea
            d = nt(ea, wo[...])
            for m in range(blocks):
                do_ref[r, lanes(perm, m)] = d[:, m * LANE : (m + 1) * LANE].astype(BF16)
            return carry

        lax.fori_loop(0, acc.shape[0] // tile, step, 0)


def dmiddle_call(perm, gains, cot, keep, h1, dg, du, pg, pu, po):
    rows, width = h1.shape
    hidden = dg.shape[1]
    chunk = hidden // 3
    full = lambda j: (0, 0)
    at = lambda j: (0, j)
    whole = pl.BlockSpec((rows, width), full)
    return pl.pallas_call(
        functools.partial(dmiddle_body, len(pg)),
        grid=(hidden // chunk,),
        out_shape=(
            sds((rows, width), F32),
            sds((rows, width), BF16),
            sds((rows, width), BF16),
            sds((1, width), F32),
        ),
        in_specs=[
            SMEM,
            pl.BlockSpec((8, width), full),
            whole,
            pl.BlockSpec((rows, 1), full),
            whole,
            pl.BlockSpec((rows, chunk), at),
            pl.BlockSpec((rows, chunk), at),
        ]
        + [ANY] * (3 * len(pg)),
        out_specs=(whole, whole, whole, pl.BlockSpec((1, width), full)),
        scratch_shapes=[
            pltpu.VMEM((width, hidden), BF16),
            pltpu.VMEM((width, hidden), BF16),
            pltpu.VMEM((width, width), BF16),
            pltpu.VMEM((rows, width), F32),
            pltpu.VMEM((rows, width), F32),
            pltpu.SemaphoreType.DMA((hidden // chunk, 2, len(pg))),
            pltpu.SemaphoreType.DMA((len(po),)),
        ],
        compiler_params=params(),
        cost_estimate=pl.CostEstimate(
            flops=4 * rows * width * hidden + 2 * rows * width * width,
            transcendentals=0,
            bytes_accessed=4 * width * hidden + 4 * rows * hidden + 16 * rows * width,
        ),
        name="dmiddle",
    )(perm, gains, cot, keep, h1, dg, du, *pg, *pu, *po)


def dattend_body(
    segk_ref, segq_ref, q_ref, k0_ref, k1_ref, v0_ref, v1_ref, do_ref, lse_ref,
    dq_ref, dk0_ref, dv0_ref, dk1_ref, dv1_ref, bias, kt, dk, dv,
):
    j = pl.program_id(0)
    rows = q_ref.shape[0]
    tile = 256

    @pl.when(j == 0)
    def _():
        bias[...] = jnp.where(segk_ref[...] == segq_ref[...], 0.0, NEG)

    for i in range(rows // LANE):
        r = slice(i * LANE, (i + 1) * LANE)
        kt[:, r] = k0_ref[r, :].astype(F32).T.astype(BF16)
        kt[:, rows + i * LANE : rows + (i + 1) * LANE] = k1_ref[r, :].astype(F32).T.astype(BF16)
    head_of = lax.broadcasted_iota(jnp.int32, (1, LANE), 1) // HEAD
    scale = LOG2E / math.sqrt(HEAD)
    back = 1.0 / math.sqrt(HEAD)
    for t in range(rows // tile):
        cols = slice(t * tile, (t + 1) * tile)
        q = q_ref[cols, :]
        do = do_ref[cols, :]
        parts = []
        for h in range(LANE // HEAD):
            qm = jnp.where(head_of == h, q, jnp.zeros_like(q))
            dom = jnp.where(head_of == h, do, jnp.zeros_like(do))
            s = jnp.concatenate([nt(k0_ref[...], qm), nt(k1_ref[...], qm)], axis=0) * scale + bias[:, cols]
            p = jnp.exp2(s - lse_ref[0, h : h + 1, cols])
            dp = jnp.concatenate([nt(v0_ref[...], dom), nt(v1_ref[...], dom)], axis=0)
            inner = jnp.sum(p * dp, axis=0, keepdims=True)
            ds = (p * (dp - inner)).astype(BF16)
            dv_new = nn(p.astype(BF16), dom)
            dk_new = nn(ds, qm)
            if t == 0 and h == 0:
                dv[...] = dv_new
                dk[...] = dk_new
            else:
                dv[...] += dv_new
                dk[...] += dk_new
            parts.append(nn(kt[...], ds)[h * HEAD : (h + 1) * HEAD, :])
        dq_ref[cols, :] = (jnp.concatenate(parts, axis=0).T * back).astype(BF16)
    dk0_ref[...] = dk[:rows, :]
    dv0_ref[...] = dv[:rows, :]
    dk1_ref[...] = dk[rows:, :].astype(BF16)
    dv1_ref[...] = dv[rows:, :].astype(BF16)


def dattend_call(segk, segq, q, kv0, kv1, do, lse):
    rows, width = q.shape
    pairs = width // LANE
    full = lambda j: (0, 0)
    at = lambda j: (0, j)
    vat = lambda j: (0, pairs + j)
    block = (rows, LANE)
    return pl.pallas_call(
        dattend_body,
        grid=(pairs,),
        out_shape=(
            sds((rows, width), BF16),
            sds((rows, width), F32),
            sds((rows, width), F32),
            sds((rows, width), BF16),
            sds((rows, width), BF16),
        ),
        in_specs=[
            pl.BlockSpec((2 * rows, 1), full),
            pl.BlockSpec((1, rows), full),
            pl.BlockSpec(block, at),
            pl.BlockSpec(block, at),
            pl.BlockSpec(block, at),
            pl.BlockSpec(block, vat),
            pl.BlockSpec(block, vat),
            pl.BlockSpec(block, at),
            pl.BlockSpec((1, 8, rows), lambda j: (j, 0, 0)),
        ],
        out_specs=(pl.BlockSpec(block, at),) * 5,
        scratch_shapes=[
            pltpu.VMEM((2 * rows, rows), F32),
            pltpu.VMEM((LANE, 2 * rows), BF16),
            pltpu.VMEM((2 * rows, LANE), F32),
            pltpu.VMEM((2 * rows, LANE), F32),
        ],
        compiler_params=params(),
        cost_estimate=pl.CostEstimate(
            flops=40 * rows * rows * width, transcendentals=2 * rows * rows * HEADS, bytes_accessed=24 * rows * width
        ),
        name="dattend",
    )(segk, segq, q, kv0, kv1, kv0, kv1, do, lse)


def dqkv_body(cos_ref, sin_ref, dq_ref, dk0_ref, dv0_ref, dk1_ref, dv1_ref, out_ref):
    width = dq_ref.shape[1]
    cos = cos_ref[...]
    sin = -sin_ref[...]
    out_ref[:, :width] = turn(dq_ref[...].astype(F32), cos, sin).astype(BF16)
    key = ((dk0_ref[...] + dk1_ref[...].astype(F32)) * (1.0 / math.sqrt(HEAD))).astype(BF16)
    out_ref[:, width : 2 * width] = turn(key.astype(F32), cos, sin).astype(BF16)
    out_ref[:, 2 * width :] = (dv0_ref[...] + dv1_ref[...].astype(F32)).astype(BF16)


def dqkv_call(cos, sin, dq, dk0, dv0, dk1, dv1):
    rows, width = dq.shape
    tile = 64
    row = lambda i: (i, 0)
    block = pl.BlockSpec((tile, width), row)
    return pl.pallas_call(
        dqkv_body,
        grid=(rows // tile,),
        out_shape=sds((rows, 3 * width), BF16),
        in_specs=[pl.BlockSpec((tile, LANE), row)] * 2 + [block] * 5,
        out_specs=pl.BlockSpec((tile, 3 * width), row),
        compiler_params=params(),
        cost_estimate=pl.CostEstimate(flops=20 * rows * width, transcendentals=0, bytes_accessed=20 * rows * width),
        name="dqkv",
    )(cos, sin, dq, dk0, dv0, dk1, dv1)


def dinput_body(n0, n1, perm, gains_ref, x_ref, dh1_ref, d_ref, *rest):
    p0, p1 = rest[:n0], rest[n0 : n0 + n1]
    out_ref, gg_ref, w, acc, da, sems = rest[n0 + n1 :]
    j = pl.program_id(0)
    chunk = d_ref.shape[1]
    steps = w.shape[1] // chunk
    half = steps // 2

    def copies(s):
        if s < half:
            return weight_copies(p0, s * chunk, chunk, w, s * chunk, sems.at[s])
        return weight_copies(p1, (s - half) * chunk, chunk, w, s * chunk, sems.at[s])

    @pl.when(j == 0)
    def _():
        for s in range(steps):
            start(copies(s))
        acc[...] = jnp.zeros_like(acc)

    for s in range(steps):

        @pl.when(j == s)
        def _(s=s):
            wait(copies(s))

    acc[...] += nt(d_ref[...], w[:, pl.ds(pl.multiple_of(j * chunk, chunk), chunk)])

    @pl.when(j == steps - 1)
    def _():
        for m in range(acc.shape[1] // LANE):
            da[:, lanes(perm, m)] = acc[:, m * LANE : (m + 1) * LANE]
        gg_ref[...] = jnp.zeros_like(gg_ref)
        tile = 64

        def step(i, carry):
            r = pl.ds(pl.multiple_of(i * tile, tile), tile)
            normed, inv = norm_rows(x_ref[r, :].astype(F32))
            e = da[r, :]
            gg_ref[...] += jnp.sum(e * normed, axis=0, keepdims=True)
            out_ref[r, :] = (dh1_ref[r, :] + norm_back(e, gains_ref[0:1, :], normed, inv)).astype(BF16)
            return carry

        lax.fori_loop(0, acc.shape[0] // tile, step, 0)


def dinput_call(perm, gains, x, dh1, d, p0, p1):
    rows, width = x.shape
    chunk = 512
    steps = 3 * width // chunk
    full = lambda j: (0, 0)
    whole = pl.BlockSpec((rows, width), full)
    return pl.pallas_call(
        functools.partial(dinput_body, len(p0), len(p1)),
        grid=(steps,),
        out_shape=(sds((rows, width), BF16), sds((1, width), F32)),
        in_specs=[SMEM, pl.BlockSpec((8, width), full), whole, whole, pl.BlockSpec((rows, chunk), lambda j: (0, j))]
        + [ANY] * (len(p0) + len(p1)),
        out_specs=(whole, pl.BlockSpec((1, width), full)),
        scratch_shapes=[
            pltpu.VMEM((width, 3 * width), BF16),
            pltpu.VMEM((rows, width), F32),
            pltpu.VMEM((rows, width), F32),
            pltpu.SemaphoreType.DMA((steps, len(p0))),
        ],
        compiler_params=params(),
        cost_estimate=pl.CostEstimate(
            flops=6 * rows * width * width, transcendentals=0, bytes_accessed=6 * width * width + 14 * rows * width
        ),
        name="dinput",
    )(perm, gains, x, dh1, d, *p0, *p1)


def grad_body(first, keeps, masked, form, perm, left_ref, keep_ref, right_ref, *rest):
    left_t = rest[-1]
    outs = rest[1:-1] if form in "xy" else rest[:-1]

    @pl.when(pl.program_id(0) == 0)
    def _():
        for i in range(keeps):
            block = left_ref[:, lanes(perm, first + i)].astype(F32)
            if masked:
                block = block * keep_ref[...]
            left_t[i * LANE : (i + 1) * LANE, :] = block.T.astype(BF16)

    g = nn(left_t[...], right_ref[...])
    if form in "xy":
        g = g + rest[0][...].astype(F32)
        q = [g[i * LANE : (i + 1) * LANE, :].astype(BF16) for i in range(4)]
        order = (1, 3, 0, 2) if form == "x" else (2, 3, 0, 1)
        outs[0][:LANE, :] = q[order[0]]
        outs[0][LANE:, :] = q[order[1]]
        outs[1][:LANE, :] = q[order[2]]
        outs[1][LANE:, :] = q[order[3]]
    else:
        outs[0][...] = g.astype(outs[0].dtype)


def grad_call(perm, left, keep, right, col, count, chunk, first, blocks, form, recv=None, masked=False):
    rows = left.shape[0]
    full = lambda j: (0, 0)
    at = lambda j: (0, j)
    base = col // chunk
    height = blocks * LANE
    specs = [
        SMEM,
        pl.BlockSpec(left.shape, full),
        pl.BlockSpec((rows, 1), full),
        pl.BlockSpec((rows, chunk), lambda j: (0, base + j)),
    ]
    args = [perm, left, keep, right]
    if form in "xy":
        specs.append(pl.BlockSpec((height, chunk), at))
        args.append(recv)
        out_shape = (sds((height // 2, count), BF16),) * 2
        out_specs = (pl.BlockSpec((height // 2, chunk), at),) * 2
    else:
        out_shape = sds((height, count), BF16 if form == "c" else F32)
        out_specs = pl.BlockSpec((height, chunk), at)
    return pl.pallas_call(
        functools.partial(grad_body, first, blocks, masked, form),
        grid=(count // chunk,),
        out_shape=out_shape,
        in_specs=specs,
        out_specs=out_specs,
        scratch_shapes=[pltpu.VMEM((height, rows), BF16)],
        compiler_params=params(),
        cost_estimate=pl.CostEstimate(
            flops=2 * rows * height * count, transcendentals=0, bytes_accessed=2 * rows * (1024 + count) + 4 * height * count
        ),
        name="grad_" + form,
    )(*args)


def rotary_tables(positions):
    half = HEAD // 2
    exponent = jnp.arange(half, dtype=F32) * (2.0 / HEAD)
    frequency = jnp.exp(-exponent * math.log(rope_base))
    angles = positions.astype(F32)[:, None] * frequency[None, :]
    cos, sin = jnp.cos(angles), jnp.sin(angles)
    return jnp.concatenate([cos, cos, cos, cos], axis=-1), jnp.concatenate([-sin, sin, -sin, sin], axis=-1)


def on_device(tokens, segments, cotangent, attn_gain, w_qkv, w_attn_out, mlp_gain, w_in, w_mlp_out):
    micro_count, seq_count, local_len, width = tokens.shape
    hidden = w_mlp_out.shape[1]
    padded = -(-hidden // (3 * LANE)) * (3 * LANE)
    dp_count = lax.axis_size("dp")
    ctx_count = lax.axis_size("ctx")
    part = width // (dp_count * ctx_count)
    blocks = width // LANE
    half_len = local_len // 2
    rows = ctx_count * half_len
    assert seq_count == 1 and ctx_count == 2 * micro_count and dp_count % 2 == 0
    fast = dp_count == 8 and ctx_count * part == LANE
    dp = lax.axis_index("dp")
    low = dp % 2

    def swap(v, bit):
        return lax.ppermute(v, "dp", [(i, i ^ bit) for i in range(dp_count)])

    def across(v):
        return lax.all_to_all(v, "ctx", split_axis=0, concat_axis=0, tiled=True)

    def pick(zero, one):
        return jnp.where(low == 0, zero, one)

    def to_chip(v):
        halves = v.reshape(micro_count, 2, half_len, width)
        mine = pick(halves[:, 0], halves[:, 1])
        other = swap(pick(halves[:, 1], halves[:, 0]), 1)
        both = jnp.stack([pick(mine, other), pick(other, mine)], axis=1)
        return across(both.reshape(ctx_count, half_len, width)).reshape(rows, width)

    def from_chip(v):
        got = across(v.reshape(ctx_count, half_len, width)).reshape(micro_count, 2, half_len, width)
        mine = pick(got[:, 0], got[:, 1])
        other = swap(pick(got[:, 1], got[:, 0]), 1)
        both = jnp.stack([pick(mine, other), pick(other, mine)], axis=1)
        return both.reshape(micro_count, 1, local_len, width)

    def gather(shard, first):
        if not fast:
            return [lax.all_gather(shard, ("dp", "ctx"), axis=0, tiled=True)]
        count = shard.shape[1]
        own = across(jnp.broadcast_to(shard[None], (ctx_count, part, count))).reshape(ctx_count * part, count)
        rx, ry = swap(own, 2), swap(own, 4)
        rxy = swap(rx, 4) if first == "x" else swap(ry, 2)
        near = [own, rx, ry, rxy]
        return near + [swap(v, 1) for v in near]

    seg = segments.reshape(micro_count, local_len)
    seg_other = swap(seg, 1)
    seg_all = across(jnp.stack([pick(seg, seg_other), pick(seg_other, seg)], axis=1).reshape(ctx_count, local_len))
    seg_halves = seg_all.reshape(ctx_count, 2, half_len)
    seg_mine = pick(seg_halves[:, 0], seg_halves[:, 1]).reshape(rows)
    seg_theirs = pick(seg_halves[:, 1], seg_halves[:, 0]).reshape(rows)
    segq = seg_mine.reshape(1, rows)
    segk = jnp.concatenate([seg_mine, seg_theirs]).reshape(2 * rows, 1)
    keep = (seg_mine != 0).astype(F32).reshape(rows, 1)

    step = jnp.arange(rows, dtype=jnp.int32)
    positions = step // half_len * local_len + low * half_len + step % half_len
    cos, sin = rotary_tables(positions)

    index = jnp.arange(blocks, dtype=jnp.int32)
    if fast:
        turned = (index // 4) + 4 * (index // 2 % 2) + 2 * (index % 2)
        perm = jnp.bitwise_xor(turned, dp.astype(jnp.int32))
    else:
        perm = index

    third = 3 * width // 2
    gain_cols = jnp.concatenate(
        [attn_gain[:, None], mlp_gain[:, None], jnp.zeros((part, LANE - 2), BF16)], axis=1
    )
    shards = (
        jnp.concatenate([w_qkv[:, :third], gain_cols], axis=1),
        w_qkv[:, third:],
        w_attn_out,
        jnp.pad(w_in[:, :hidden], ((0, 0), (0, padded - hidden))),
        jnp.pad(w_in[:, hidden:], ((0, 0), (0, padded - hidden))),
        jnp.pad(w_mlp_out, ((0, 0), (0, padded - hidden))),
    )
    forms = ("x", "y", "x", "y", "x", "y")
    qkv0 = gather(shards[0], forms[0])
    qkv1 = gather(shards[1], forms[1])
    x = to_chip(tokens)
    wout = gather(shards[2], forms[2])
    wgate = gather(shards[3], forms[3])
    wup = gather(shards[4], forms[4])
    wdown = gather(shards[5], forms[5])
    cot = to_chip(cotangent)

    def reduce(left, right, col, count, chunk, form, masked=False):
        call = functools.partial(grad_call, perm, left, keep, right, col, count, chunk, masked=masked)
        if not fast:
            return lax.psum_scatter(call(0, blocks, "f"), ("dp", "ctx"), scatter_dimension=0, tiled=True)
        recv = swap(call(4, 4, "c"), 1)
        send, kept = call(0, 4, form, recv=recv)
        one, two = (2, 4) if form == "x" else (4, 2)
        got = swap(send, one)
        half = send.shape[0] // 2
        send2 = (kept[half:].astype(F32) + got[half:].astype(F32)).astype(BF16)
        kept2 = kept[:half].astype(F32) + got[:half].astype(F32)
        total = (kept2 + swap(send2, two).astype(F32)).astype(BF16)
        return jnp.sum(across(total.reshape(ctx_count, part, count)).astype(F32), axis=0)

    attn_in, q, kv, gains = qkv_call(perm, x, cos, sin, qkv0, qkv1)
    kv_other = swap(kv, 1)
    attended, lse = attend_call(segk, segq, q, kv, kv_other)
    h1, mlp_in = middle_call(perm, gains, x, keep, attended, wout)
    mixed, f1, f2 = gate_call(perm, mlp_in, wgate, wup, padded)
    third_hidden = padded // 3
    down_grad = reduce(cot, mixed, 0, padded, third_hidden, forms[5], masked=True)
    dgate, dup = dgate_call(perm, cot, keep, f1, f2, wdown)
    gate_grad = reduce(mlp_in, dgate, 0, padded, third_hidden, forms[3])
    up_grad = reduce(mlp_in, dup, 0, padded, third_hidden, forms[4])
    dh1, e_attn, d_o, gain_two = dmiddle_call(perm, gains, cot, keep, h1, dgate, dup, wgate, wup, wout)
    out_grad = reduce(attended, e_attn, 0, width, 512, forms[2])
    layer_out = from_chip(down_call(perm, h1, keep, mixed, wdown))
    dq, dk0, dv0, dk1, dv1 = dattend_call(segk, segq, q, kv, kv_other, d_o, lse)
    d_qkv = dqkv_call(cos, sin, dq, dk0, dv0, swap(dk1, 1), swap(dv1, 1))
    qkv_grad0 = reduce(attn_in, d_qkv, 0, third, 512, forms[0])
    qkv_grad1 = reduce(attn_in, d_qkv, third, third, 512, forms[1])
    input_rows, gain_one = dinput_call(perm, gains, x, dh1, d_qkv, qkv0, qkv1)
    input_grad = from_chip(input_rows)

    gain_rows = jnp.concatenate([gain_one, gain_two], axis=0)
    if fast:
        for bit in (1, 2, 4):
            gain_rows = gain_rows + swap(gain_rows, bit)
        mine = lax.dynamic_slice(gain_rows, (0, dp * LANE), (2, LANE))
        mine = jnp.transpose(mine.reshape(2, ctx_count, part), (1, 0, 2))
        gain_grads = jnp.sum(across(mine), axis=0)
    else:
        gain_grads = lax.psum_scatter(gain_rows, ("dp", "ctx"), scatter_dimension=1, tiled=True)
    return (
        layer_out,
        input_grad,
        gain_grads[0],
        jnp.concatenate([qkv_grad0, qkv_grad1], axis=1),
        out_grad,
        gain_grads[1],
        jnp.concatenate([gate_grad[:, :hidden], up_grad[:, :hidden]], axis=1),
        down_grad[:, :hidden],
    )


def solution(mesh):
    return jax.shard_map(
        on_device,
        mesh=mesh,
        in_specs=(
            P(None, "dp", "ctx", None),
            P(None, "dp", "ctx"),
            P(None, "dp", "ctx", None),
            P(("dp", "ctx")),
            P(("dp", "ctx"), None),
            P(("dp", "ctx"), None),
            P(("dp", "ctx")),
            P(("dp", "ctx"), None),
            P(("dp", "ctx"), None),
        ),
        out_specs=(
            P(None, "dp", "ctx", None),
            P(None, "dp", "ctx", None),
            P(("dp", "ctx")),
            P(("dp", "ctx"), None),
            P(("dp", "ctx"), None),
            P(("dp", "ctx")),
            P(("dp", "ctx"), None),
            P(("dp", "ctx"), None),
        ),
        check_vma=False,
    )
```

time: 1960 us -> 658 us (0.34)
  waiting for transfers between devices: 1440 us -> 251 us
  Pallas kernels: 0 us -> 219 us
  matrix products: 215 us -> 0 us
  blocking collectives: 99.1 us -> 10.2 us
  starting transfers between devices: 32.5 us -> 113 us
  local copies, waits for them, and re-layouts: 74.2 us -> 18.8 us
  other arithmetic: 64.9 us -> 33.9 us
    all_gather x16 -> x0, waiting for transfers between devices: 1010 us -> none  [the longest x2 306 us: on_device(): lax.all_gather(gate_up_grad, 'ctx', axis=0, tiled=True)]
    reduce_scatter x8 -> x0, waiting for transfers between devices: 227 us -> none  [the longest x2 84.8 us: on_device(): lax.psum_scatter(value_terms.reshape(seq_count, full_len, model_width).as...]
    pallas_call x0 -> x22, Pallas kernels: none -> 219 us  [the longest x12 63.8 us: grad_call(): pl.pallas_call(functools.partial(grad_body, first, blocks, masked, form),...]
    dot_general x36 -> x0, matrix products: 215 us -> none  [the longest x8 50 us: contract_rows(): lax.dot_general(left_side, right_side, (((0,), (0,)), ((), ())), preferre...]
    ppermute x0 -> x71, waiting for transfers between devices: none -> 138 us  [swap(): return lax.ppermute(v, 'dp', [(i, i ^ bit) for i in range(dp_count)])]
    all_to_all x8 -> x17, waiting for transfers between devices: 196 us -> 113 us  [across(): return lax.all_to_all(v, 'ctx', split_axis=0, concat_axis=0, tiled=True)]
    unnamed x2 -> x0, blocking collectives: 81.6 us -> none
    ppermute x0 -> x71, starting transfers between devices: none -> 41.3 us  [swap(): return lax.ppermute(v, 'dp', [(i, i ^ bit) for i in range(dp_count)])]
  transfers between devices with their start and end apart: 32 -> 88, of which waited for: 28 -> 30; matrix products, arithmetic and copies ran while one was open for 13% -> 6% of each run, Pallas kernels for 0% -> 24%
where the time goes in v1:
time: 658 us; the launch traced here: 648 us
  waiting for transfers between devices  251 us (38%)
  Pallas kernels  219 us (33%)
  starting transfers between devices  113 us (17%)
  other arithmetic  33.9 us (5%)
  local copies, waits for them, and re-layouts  18.8 us (3%)
  blocking collectives  10.2 us (2%)
    ppermute x71, waiting for transfers between devices, swap(): return lax.ppermute(v, 'dp', [(i, i ^ bit) for i in range(dp_count)])  138 us
    all_to_all x17, waiting for transfers between devices, across(): return lax.all_to_all(v, 'ctx', split_axis=0, concat_axis=0, tiled=True)  113 us
    all_to_all x17, starting transfers between devices, across(): return lax.all_to_all(v, 'ctx', split_axis=0, concat_axis=0, tiled=True)  71.6 us
    pallas_call x12, Pallas kernels, grad_call(): pl.pallas_call(functools.partial(grad_body, first, blocks, masked, form),...  63.8 us
    ppermute x71, starting transfers between devices, swap(): return lax.ppermute(v, 'dp', [(i, i ^ bit) for i in range(dp_count)])  41.3 us
    pallas_call x1, Pallas kernels, dattend_call(): pl.pallas_call(dattend_body, grid=(pairs,), out_shape=(sds((rows, width),...  33.9 us
    pallas_call x1, Pallas kernels, attend_call(): pl.pallas_call(attend_body, grid=(pairs,), out_shape=(sds((rows, width),...  25.9 us
    pallas_call x1, Pallas kernels, dmiddle_call(): pl.pallas_call(functools.partial(dmiddle_body, len(pg)), grid=(hidden //...  19.5 us
  transfers between devices with their start and end apart: 88, of which 30 were waited for; matrix products, arithmetic and copies ran while one was open for 6% of the time, Pallas kernels for 24%

profile of v1, /device:TPU:0, one launch (start us, length us, event | category | flops | bytes accessed | tf_op | source)
XLA Modules:
  0.0 647.6 jit_solution(6858915567800281097)
XLA Ops:
  9.5 8.0 %all-to-all-done.4 = bf16[4,32,1024]{2,1,0:T(8,128)(2,1)S(1)} async-done(((bf16[4,32,1024]{2,1,0:T(8,128)(2,1)}), bf16[4,32,1024]{2,1,0:T(8,128)(2,1)S(1)}, u32[]{:S(2)}, u32[]{:S(2)}) %all-to-all-start.4) | async-done | bytes 262176 | tf_op jit(solution)/shard_map/all_to_all | solution.py:894
  22.0 10.0 %all-to-all-done.2 = bf16[4,32,1536]{2,1,0:T(8,128)(2,1)S(1)} async-done(((bf16[4,32,1536]{2,1,0:T(8,128)(2,1)}), bf16[4,32,1536]{2,1,0:T(8,128)(2,1)S(1)}, u32[]{:S(2)}, u32[]{:S(2)}) %all-to-all-start.2) | async-done | bytes 393248 | tf_op jit(solution)/shard_map/all_to_all | solution.py:894
  36.4 10.5 %all-to-all-done.1 = bf16[4,32,1664]{2,1,0:T(8,128)(2,1)S(1)} async-done(((bf16[4,32,1664]{2,1,0:T(8,128)(2,1)}), bf16[4,32,1664]{2,1,0:T(8,128)(2,1)S(1)}, u32[]{:S(2)}, u32[]{:S(2)}) %all-to-all-start.1) | async-done | bytes 426016 | tf_op jit(solution)/shard_map/all_to_all | solution.py:894
  52.0 15.4 %all-to-all-done.5 = bf16[4,32,2688]{2,1,0:T(8,128)(2,1)} async-done(((bf16[4,32,2688]{2,1,0:T(8,128)(2,1)}), bf16[4,32,2688]{2,1,0:T(8,128)(2,1)}, u32[]{:S(2)}, u32[]{:S(2)}) %all-to-all-start.5) | async-done | bytes 688160 | tf_op jit(solution)/shard_map/all_to_all | solution.py:894
  75.1 12.7 %all-to-all-done.7 = bf16[4,32,2688]{2,1,0:T(8,128)(2,1)S(1)} async-done(((bf16[4,32,2688]{2,1,0:T(8,128)(2,1)}), bf16[4,32,2688]{2,1,0:T(8,128)(2,1)S(1)}, u32[]{:S(2)}, u32[]{:S(2)}) %all-to-all-start.7) | async-done | bytes 688160 | tf_op jit(solution)/shard_map/all_to_all | solution.py:894
  148.1 13.2 %qkv.1 = (bf16[512,1024]{1,0:T(8,128)(2,1)}, bf16[512,1024]{1,0:T(8,128)(2,1)}, bf16[512,2048]{1,0:T(8,128)(2,1)}, f32[8,1024]{1,0:T(8,128)}) custom-call(s32[8]{0:T(128)} %fusion.22.perm, bf16[512,1024]{1,0:T(8,128)(2,1)} %bitcast.192, f32[512,128]{1,0:T(8,128)} %get-tuple-element.99.cos_ref, f32[512,128]{1,0:T(8,128)} %get-tuple-element.100.sin_ref, ...), custom_call_target="tpu_custom_call" | custom-call | flops 3221225472 | bytes 11534336 | tf_op jit(solution)/shard_map/qkv/pallas_call | solution.py:150
  162.6 11.6 %collective-permute-done.25.rest_2_ = bf16[128,2688]{1,0:T(8,128)(2,1)} collective-permute-done((bf16[128,2688]{1,0:T(8,128)(2,1)}, bf16[128,2688]{1,0:T(8,128)(2,1)}, u32[]{:S(2)}, u32[]{:S(2)}) %collective-permute-start.25) | collective-permute-done | bytes 688160 | tf_op jit(solution)/shard_map/ppermute | solution.py:891
  176.3 12.1 %collective-permute-done.32.rest_10_ = bf16[128,2688]{1,0:T(8,128)(2,1)} collective-permute-done((bf16[128,2688]{1,0:T(8,128)(2,1)}, bf16[128,2688]{1,0:T(8,128)(2,1)}, u32[]{:S(2)}, u32[]{:S(2)}) %collective-permute-start.32) | collective-permute-done | bytes 688160 | tf_op jit(solution)/shard_map/ppermute | solution.py:891
  192.9 14.6 %collective-permute-done.40.rest_3_ = bf16[128,2688]{1,0:T(8,128)(2,1)S(1)} collective-permute-done((bf16[128,2688]{1,0:T(8,128)(2,1)S(1)}, bf16[128,2688]{1,0:T(8,128)(2,1)S(1)}, u32[]{:S(2)}, u32[]{:S(2)}) %collective-permute-start.40) | collective-permute-done | bytes 688160 | tf_op jit(solution)/shard_map/ppermute | solution.py:891
  208.2 10.2 %all_to_all.95 = s32[4,1,256]{2,1,0:T(1,128)S(1)} all-to-all(s32[4,1,256]{2,1,0:T(1,128)S(1)} %all_to_all.76), channel_id=1, replica_groups=mesh['dp'=8,'ctx'=4] {'ctx'}, dimensions={0} | all-to-all | bytes 8192 | tf_op jit(solution)/shard_map/all_to_all | solution.py:894
  230.5 25.9 %attend.1 = (bf16[512,1024]{1,0:T(8,128)(2,1)}, f32[8,8,512]{2,1,0:T(8,128)}) custom-call(s32[1024,1]{1,0:T(8,128)} %copy.144.segk_ref, s32[1,512]{1,0:T(1,128)} %bitcast.236, bf16[512,1024]{1,0:T(8,128)(2,1)} %get-tuple-element.45.q_ref, bf16[512,2048]{1,0:T(8,128)(2,1)} %get-tuple-element.46.k0_ref.v0_ref, ...), custom_call_target="tpu_custom_call" | custom-call | flops 4294967296 | bytes 6291456 | tf_op jit(solution)/shard_map/attend/pallas_call | solution.py:225
  263.3 15.0 %gate.1 = (bf16[512,2688]{1,0:T(8,128)(2,1)}, bf16[512,2688]{1,0:T(8,128)(2,1)}, bf16[512,2688]{1,0:T(8,128)(2,1)}) custom-call(s32[8]{0:T(128)} %fusion.22.perm, bf16[512,1024]{1,0:T(8,128)(2,1)} %get-tuple-element.49.b_ref.left_ref, bf16[128,2688]{1,0:T(8,128)(2,1)} %bitcast.20.rest_0_, bf16[128,2688]{1,0:T(8,128)(2,1)} %collective-permute-done.24.rest_1_, ...), custom_call_target="tpu_custom_call" | custom-call | flops 5637144576 | bytes 19267584 | tf_op jit(solution)/shard_map/gate/pallas_call | solution.py:350
  279.4 10.5 %dgate.1 = (bf16[512,2688]{1,0:T(8,128)(2,1)}, bf16[512,2688]{1,0:T(8,128)(2,1)}) custom-call(s32[8]{0:T(128)} %fusion.22.perm, bf16[512,1024]{1,0:T(8,128)(2,1)} %bitcast.188, f32[512,1]{1,0:T(8,128)} %copy.145.keep_ref, bf16[512,2688]{1,0:T(8,128)(2,1)} %get-tuple-element.51.f1_ref, bf16[512,2688]{1,0:T(8,128)(2,1)} %get-tuple-element.52.f2_ref, ...), custom_call_target="tpu_custom_call" | custom-call | flops 2818572288 | bytes 16515072 | tf_op jit(solution)/shard_map/dgate/pallas_call | solution.py:415
  289.9 19.5 %dmiddle.1 = (f32[512,1024]{1,0:T(8,128)}, bf16[512,1024]{1,0:T(8,128)(2,1)}, bf16[512,1024]{1,0:T(8,128)(2,1)}, f32[1,1024]{1,0:T(1,128)}) custom-call(s32[8]{0:T(128)} %fusion.22.perm, f32[8,1024]{1,0:T(8,128)} %get-tuple-element.44.gains_ref, bf16[512,1024]{1,0:T(8,128)(2,1)} %bitcast.189, f32[512,1]{1,0:T(8,128)} %copy.145.keep_ref, ...), custom_call_target="tpu_custom_call" | custom-call | flops 6710886400 | bytes 24903680 | tf_op jit(solution)/shard_map/dmiddle/pallas_call | solution.py:576
  309.4 33.9 %dattend.1 = (bf16[512,1024]{1,0:T(8,128)(2,1)}, f32[512,1024]{1,0:T(8,128)}, f32[512,1024]{1,0:T(8,128)}, bf16[512,1024]{1,0:T(8,128)(2,1)}, bf16[512,1024]{1,0:T(8,128)(2,1)}) custom-call(s32[1024,1]{1,0:T(8,128)} %copy.144.segk_ref, s32[1,512]{1,0:T(1,128)} %bitcast.237, bf16[512,1024]{1,0:T(8,128)(2,1)} %get-tuple-element.45.q_ref, ...), custom_call_target="tpu_custom_call" | custom-call | flops 10737418240 | bytes 12582912 | tf_op jit(solution)/shard_map/dattend/pallas_call | solution.py:670
  343.8 9.2 %down.1 = bf16[512,1024]{1,0:T(8,128)(2,1)} custom-call(s32[8]{0:T(128)} %fusion.22.perm, f32[512,1024]{1,0:T(8,128)} %get-tuple-element.48.h1_ref, f32[512,1]{1,0:T(8,128)} %copy.145.keep_ref, bf16[512,2688]{1,0:T(8,128)(2,1)} %get-tuple-element.50.m_ref.right_ref, bf16[128,2688]{1,0:T(8,128)(2,1)} %bitcast.203, ...), custom_call_target="tpu_custom_call" | custom-call | flops 2818572288 | bytes 8257536 | tf_op jit(solution)/shard_map/down/pallas_call | solution.py:479
  368.5 7.8 %dqkv.1.d_ref.right_ref = bf16[512,3072]{1,0:T(8,128)(2,1)} custom-call(f32[512,128]{1,0:T(8,128)} %get-tuple-element.99.cos_ref, f32[512,128]{1,0:T(8,128)} %get-tuple-element.100.sin_ref, bf16[512,1024]{1,0:T(8,128)(2,1)} %get-tuple-element.58.dq_ref, f32[512,1024]{1,0:T(8,128)} %get-tuple-element.59.dk0_ref, f32[512,1024]{1,0:T(8,128)} %get-tuple-element.60.dv0_ref, ...), custom_call_target="tpu_custom_call" | custom-call | flops 10485760 | bytes 10485760 | tf_op jit(solution)/shard_map/dqkv/pallas_call | solution.py:721
  376.3 13.4 %dinput.1 = (bf16[512,1024]{1,0:T(8,128)(2,1)}, f32[1,1024]{1,0:T(1,128)}) custom-call(s32[8]{0:T(128)} %fusion.22.perm, f32[8,1024]{1,0:T(8,128)} %get-tuple-element.44.gains_ref, bf16[512,1024]{1,0:T(8,128)(2,1)} %bitcast.194, f32[512,1024]{1,0:T(8,128)} %get-tuple-element.55.dh1_ref, bf16[512,3072]{1,0:T(8,128)(2,1)} %dqkv.1.d_ref.right_ref, ...), custom_call_target="tpu_custom_call" | custom-call | flops 3221225472 | bytes 13631488 | tf_op jit(solution)/shard_map/dinput/pallas_call | solution.py:784
  442.4 8.1 %all-to-all-done.10 = bf16[4,128,1024]{2,1,0:T(8,128)(2,1)S(1)} async-done(((bf16[4,128,1024]{2,1,0:T(8,128)(2,1)}), bf16[4,128,1024]{2,1,0:T(8,128)(2,1)S(1)}, u32[]{:S(2)}, u32[]{:S(2)}) %all-to-all-start.10) | async-done | bytes 1048608 | tf_op jit(solution)/shard_map/all_to_all | solution.py:894
  469.2 6.9 %grad_y.5 = (bf16[256,2688]{1,0:T(8,128)(2,1)}, bf16[256,2688]{1,0:T(8,128)(2,1)}) custom-call(s32[8]{0:T(128)} %fusion.22.perm, bf16[512,1024]{1,0:T(8,128)(2,1)} %bitcast.191, f32[512,1]{1,0:T(8,128)} %copy.145.keep_ref, bf16[512,2688]{1,0:T(8,128)(2,1)} %get-tuple-element.50.m_ref.right_ref, bf16[512,2688]{1,0:T(8,128)(2,1)} %collective-permute-done.68.rest_0_), custom_call_target="tpu_custom_call" | custom-call | flops 1409286144 | bytes 9306112 | tf_op jit(solution)/shard_map/grad_y/pallas_call | solution.py:851
  497.2 57.4 %collective-permute-done.55 = bf16[128,1536]{1,0:T(8,128)(2,1)S(1)} collective-permute-done((bf16[128,1536]{1,0:T(8,128)(2,1)S(1)}, bf16[128,1536]{1,0:T(8,128)(2,1)S(1)}, u32[]{:S(2)}, u32[]{:S(2)}) %collective-permute-start.55) | collective-permute-done | bytes 393248 | tf_op jit(solution)/shard_map/ppermute | solution.py:891
  594.3 10.6 %all-to-all-done.16 = bf16[4,32,2688]{2,1,0:T(8,128)(2,1)S(1)} async-done(((bf16[4,32,2688]{2,1,0:T(8,128)(2,1)}), bf16[4,32,2688]{2,1,0:T(8,128)(2,1)S(1)}, u32[]{:S(2)}, u32[]{:S(2)}) %all-to-all-start.16) | async-done | bytes 688160 | tf_op jit(solution)/shard_map/all_to_all | solution.py:894
  612.5 12.8 %all-to-all-done.15 = bf16[4,32,2688]{2,1,0:T(8,128)(2,1)S(1)} async-done(((bf16[4,32,2688]{2,1,0:T(8,128)(2,1)}), bf16[4,32,2688]{2,1,0:T(8,128)(2,1)S(1)}, u32[]{:S(2)}, u32[]{:S(2)}) %all-to-all-start.15) | async-done | bytes 688160 | tf_op jit(solution)/shard_map/all_to_all | solution.py:894
  630.8 15.5 %all-to-all-done.17 = bf16[4,32,2688]{2,1,0:T(8,128)(2,1)S(1)} async-done(((bf16[4,32,2688]{2,1,0:T(8,128)(2,1)}), bf16[4,32,2688]{2,1,0:T(8,128)(2,1)S(1)}, u32[]{:S(2)}, u32[]{:S(2)}) %all-to-all-start.17) | async-done | bytes 688160 | tf_op jit(solution)/shard_map/all_to_all | solution.py:894
  (343 shorter events, 280.8 us)
Async XLA Ops:
  87.8 46.2 %all-to-all-start = ((bf16[4,128,1024]{2,1,0:T(8,128)(2,1)}), bf16[4,128,1024]{2,1,0:T(8,128)(2,1)S(1)}, u32[]{:S(2)}, u32[]{:S(2)}) async-start(bf16[4,128,1024]{2,1,0:T(8,128)(2,1)} %bitcast.209), calls=%async_computation | async-start | bytes 2097152 | tf_op jit(solution)/shard_map/all_to_all | solution.py:894
  143.3 31.0 %collective-permute-start.25 = (bf16[128,2688]{1,0:T(8,128)(2,1)}, bf16[128,2688]{1,0:T(8,128)(2,1)}, u32[]{:S(2)}, u32[]{:S(2)}) collective-permute-start(bf16[128,2688]{1,0:T(8,128)(2,1)} %bitcast.20.rest_0_), channel_id=1, source_target_pairs={{0,16},{4,20},{8,24},{12,28},{16,0},{20,4},{24,8},{28,12},{1,17},{... | collective-permute-start | bytes 2064392 | tf_op jit(solution)/shard_map/ppermute | solution.py:891
  161.3 69.1 %collective-permute-start.16 = (bf16[512,2048]{1,0:T(8,128)(2,1)}, bf16[512,2048]{1,0:T(8,128)(2,1)}, u32[]{:S(2)}, u32[]{:S(2)}) collective-permute-start(bf16[512,2048]{1,0:T(8,128)(2,1)} %get-tuple-element.46.k0_ref.v0_ref), channel_id=1, source_target_pairs={{0,4},{4,0},{8,12},{12,8},{16,20},{20,16},{24,28},{28,24},{1,5},{5... | collective-permute-start | bytes 6291464 | tf_op jit(solution)/shard_map/ppermute | solution.py:891
  175.7 31.8 %collective-permute-start.40 = (bf16[128,2688]{1,0:T(8,128)(2,1)S(1)}, bf16[128,2688]{1,0:T(8,128)(2,1)S(1)}, u32[]{:S(2)}, u32[]{:S(2)}) collective-permute-start(bf16[128,2688]{1,0:T(8,128)(2,1)S(1)} %collective-permute-done.39.rest_2_), channel_id=1, source_target_pairs={{0,8},{4,12},{8,0},{12,4},{16,24},{20,28},{24,16},{28,20},{1,9},{5... | collective-permute-start | bytes 2064392 | tf_op jit(solution)/shard_map/ppermute | solution.py:891
  176.3 43.3 %collective-permute-start.29 = (bf16[128,2688]{1,0:T(8,128)(2,1)}, bf16[128,2688]{1,0:T(8,128)(2,1)}, u32[]{:S(2)}, u32[]{:S(2)}) collective-permute-start(bf16[128,2688]{1,0:T(8,128)(2,1)} %collective-permute-done.25.rest_2_), channel_id=1, source_target_pairs={{0,4},{4,0},{8,12},{12,8},{16,20},{20,16},{24,28},{28,24},{1,5},{5... | collective-permute-start | bytes 2064392 | tf_op jit(solution)/shard_map/ppermute | solution.py:891
  188.3 31.9 %collective-permute-start.26 = (bf16[128,2688]{1,0:T(8,128)(2,1)}, bf16[128,2688]{1,0:T(8,128)(2,1)}, u32[]{:S(2)}, u32[]{:S(2)}) collective-permute-start(bf16[128,2688]{1,0:T(8,128)(2,1)} %collective-permute-done.25.rest_2_), channel_id=1, source_target_pairs={{0,8},{4,12},{8,0},{12,4},{16,24},{20,28},{24,16},{28,20},{1,9},{5... | collective-permute-start | bytes 2064392 | tf_op jit(solution)/shard_map/ppermute | solution.py:891
  221.9 56.5 %all-to-all-start.9 = ((bf16[4,128,1024]{2,1,0:T(8,128)(2,1)}), bf16[4,128,1024]{2,1,0:T(8,128)(2,1)S(1)}, u32[]{:S(2)}, u32[]{:S(2)}) async-start(bf16[4,128,1024]{2,1,0:T(8,128)(2,1)} %bitcast.35), calls=%async_computation.9 | async-start | bytes 2097152 | tf_op jit(solution)/shard_map/all_to_all | solution.py:894
  227.4 35.9 %collective-permute-start.37 = (bf16[128,2688]{1,0:T(8,128)(2,1)}, bf16[128,2688]{1,0:T(8,128)(2,1)}, u32[]{:S(2)}, u32[]{:S(2)}) collective-permute-start(bf16[128,2688]{1,0:T(8,128)(2,1)} %collective-permute-done.33.rest_11_), channel_id=1, source_target_pairs={{0,4},{4,0},{8,12},{12,8},{16,20},{20,16},{24,28},{28,24},{1,5},{5... | collective-permute-start | bytes 2064392 | tf_op jit(solution)/shard_map/ppermute | solution.py:891
  229.4 48.9 %collective-permute-start.41 = (bf16[128,2688]{1,0:T(8,128)(2,1)S(1)}, bf16[128,2688]{1,0:T(8,128)(2,1)}, u32[]{:S(2)}, u32[]{:S(2)}) collective-permute-start(bf16[128,2688]{1,0:T(8,128)(2,1)S(1)} %bitcast.201), channel_id=1, source_target_pairs={{0,4},{4,0},{8,12},{12,8},{16,20},{20,16},{24,28},{28,24},{1,5},{5... | collective-permute-start | bytes 2064392 | tf_op jit(solution)/shard_map/ppermute | solution.py:891
  229.9 48.5 %collective-permute-start.43 = (bf16[128,2688]{1,0:T(8,128)(2,1)S(1)}, bf16[128,2688]{1,0:T(8,128)(2,1)}, u32[]{:S(2)}, u32[]{:S(2)}) collective-permute-start(bf16[128,2688]{1,0:T(8,128)(2,1)S(1)} %collective-permute-done.39.rest_2_), channel_id=1, source_target_pairs={{0,4},{4,0},{8,12},{12,8},{16,20},{20,16},{24,28},{28,24},{1,5},{5... | collective-permute-start | bytes 2064392 | tf_op jit(solution)/shard_map/ppermute | solution.py:891
  230.0 48.4 %collective-permute-start.42 = (bf16[128,2688]{1,0:T(8,128)(2,1)}, bf16[128,2688]{1,0:T(8,128)(2,1)}, u32[]{:S(2)}, u32[]{:S(2)}) collective-permute-start(bf16[128,2688]{1,0:T(8,128)(2,1)} %collective-permute-done.38.rest_1_), channel_id=1, source_target_pairs={{0,4},{4,0},{8,12},{12,8},{16,20},{20,16},{24,28},{28,24},{1,5},{5... | collective-permute-start | bytes 2064392 | tf_op jit(solution)/shard_map/ppermute | solution.py:891
  230.4 48.0 %collective-permute-start.44 = (bf16[128,2688]{1,0:T(8,128)(2,1)S(1)}, bf16[128,2688]{1,0:T(8,128)(2,1)}, u32[]{:S(2)}, u32[]{:S(2)}) collective-permute-start(bf16[128,2688]{1,0:T(8,128)(2,1)S(1)} %collective-permute-done.40.rest_3_), channel_id=1, source_target_pairs={{0,4},{4,0},{8,12},{12,8},{16,20},{20,16},{24,28},{28,24},{1,5},{5... | collective-permute-start | bytes 2064392 | tf_op jit(solution)/shard_map/ppermute | solution.py:891
  353.1 58.4 %all-to-all-start.8 = ((bf16[4,128,1024]{2,1,0:T(8,128)(2,1)}), bf16[4,128,1024]{2,1,0:T(8,128)(2,1)S(1)}, u32[]{:S(2)}, u32[]{:S(2)}) async-start(bf16[4,128,1024]{2,1,0:T(8,128)(2,1)} %bitcast.208), calls=%async_computation.8 | async-start | bytes 2097152 | tf_op jit(solution)/shard_map/all_to_all | solution.py:894
  361.7 37.0 %collective-permute-start.59 = (bf16[512,1024]{1,0:T(8,128)(2,1)}, bf16[512,1024]{1,0:T(8,128)(2,1)S(1)}, u32[]{:S(2)}, u32[]{:S(2)}) collective-permute-start(bf16[512,1024]{1,0:T(8,128)(2,1)} %grad_c.8), channel_id=1, source_target_pairs={{0,4},{4,0},{8,12},{12,8},{16,20},{20,16},{24,28},{28,24},{1,5},{5... | collective-permute-start | bytes 3145736 | tf_op jit(solution)/shard_map/ppermute | solution.py:891
  397.0 70.8 %collective-permute-start.68 = (bf16[512,2688]{1,0:T(8,128)(2,1)}, bf16[512,2688]{1,0:T(8,128)(2,1)}, u32[]{:S(2)}, u32[]{:S(2)}) collective-permute-start(bf16[512,2688]{1,0:T(8,128)(2,1)} %grad_c.11), channel_id=1, source_target_pairs={{0,4},{4,0},{8,12},{12,8},{16,20},{20,16},{24,28},{28,24},{1,5},{5... | collective-permute-start | bytes 8257544 | tf_op jit(solution)/shard_map/ppermute | solution.py:891
  410.3 65.9 %collective-permute-start.65 = (bf16[512,2688]{1,0:T(8,128)(2,1)}, bf16[512,2688]{1,0:T(8,128)(2,1)}, u32[]{:S(2)}, u32[]{:S(2)}) collective-permute-start(bf16[512,2688]{1,0:T(8,128)(2,1)} %grad_c.10), channel_id=1, source_target_pairs={{0,4},{4,0},{8,12},{12,8},{16,20},{20,16},{24,28},{28,24},{1,5},{5... | collective-permute-start | bytes 8257544 | tf_op jit(solution)/shard_map/ppermute | solution.py:891
  410.3 73.2 %collective-permute-start.62 = (bf16[512,2688]{1,0:T(8,128)(2,1)}, bf16[512,2688]{1,0:T(8,128)(2,1)}, u32[]{:S(2)}, u32[]{:S(2)}) collective-permute-start(bf16[512,2688]{1,0:T(8,128)(2,1)} %grad_c.9), channel_id=1, source_target_pairs={{0,4},{4,0},{8,12},{12,8},{16,20},{20,16},{24,28},{28,24},{1,5},{5... | collective-permute-start | bytes 8257544 | tf_op jit(solution)/shard_map/ppermute | solution.py:891
  455.1 36.3 %collective-permute-start.49 = (bf16[2,128,1024]{2,1,0:T(8,128)(2,1)S(1)}, bf16[2,128,1024]{2,1,0:T(8,128)(2,1)S(1)}, u32[]{:S(2)}, u32[]{:S(2)}) collective-permute-start(bf16[2,128,1024]{2,1,0:T(8,128)(2,1)S(1)} %select_bitcast_fusion), channel_id=1, source_target_pairs={{0,4},{4,0},{8,12},{12,8},{16,20},{20,16},{24,28},{28,24},{1,5},{5... | collective-permute-start | bytes 1572872 | tf_op jit(solution)/shard_map/ppermute | solution.py:891
  460.2 34.6 %collective-permute-start.54 = (bf16[256,1536]{1,0:T(8,128)(2,1)}, bf16[256,1536]{1,0:T(8,128)(2,1)S(1)}, u32[]{:S(2)}, u32[]{:S(2)}) collective-permute-start(bf16[256,1536]{1,0:T(8,128)(2,1)} %get-tuple-element.68), channel_id=1, source_target_pairs={{0,8},{4,12},{8,0},{12,4},{16,24},{20,28},{24,16},{28,20},{1,9},{5... | collective-permute-start | bytes 2359304 | tf_op jit(solution)/shard_map/ppermute | solution.py:891
  476.2 112.7 %collective-permute-start.69 = (bf16[256,2688]{1,0:T(8,128)(2,1)}, bf16[256,2688]{1,0:T(8,128)(2,1)}, u32[]{:S(2)}, u32[]{:S(2)}) collective-permute-start(bf16[256,2688]{1,0:T(8,128)(2,1)} %get-tuple-element.79), channel_id=1, source_target_pairs={{0,16},{4,20},{8,24},{12,28},{16,0},{20,4},{24,8},{28,12},{1,17},{... | collective-permute-start | bytes 4128776 | tf_op jit(solution)/shard_map/ppermute | solution.py:891
  483.5 79.2 %collective-permute-start.66 = (bf16[256,2688]{1,0:T(8,128)(2,1)}, bf16[256,2688]{1,0:T(8,128)(2,1)}, u32[]{:S(2)}, u32[]{:S(2)}) collective-permute-start(bf16[256,2688]{1,0:T(8,128)(2,1)} %get-tuple-element.77), channel_id=1, source_target_pairs={{0,8},{4,12},{8,0},{12,4},{16,24},{20,28},{24,16},{28,20},{1,9},{5... | collective-permute-start | bytes 4128776 | tf_op jit(solution)/shard_map/ppermute | solution.py:891
  492.3 74.0 %collective-permute-start.63 = (bf16[256,2688]{1,0:T(8,128)(2,1)}, bf16[256,2688]{1,0:T(8,128)(2,1)}, u32[]{:S(2)}, u32[]{:S(2)}) collective-permute-start(bf16[256,2688]{1,0:T(8,128)(2,1)} %get-tuple-element.75), channel_id=1, source_target_pairs={{0,16},{4,20},{8,24},{12,28},{16,0},{20,4},{24,8},{28,12},{1,17},{... | collective-permute-start | bytes 4128776 | tf_op jit(solution)/shard_map/ppermute | solution.py:891
  494.9 59.7 %collective-permute-start.55 = (bf16[128,1536]{1,0:T(8,128)(2,1)S(1)}, bf16[128,1536]{1,0:T(8,128)(2,1)S(1)}, u32[]{:S(2)}, u32[]{:S(2)}) collective-permute-start(bf16[128,1536]{1,0:T(8,128)(2,1)S(1)} %add_convert_fusion.9), channel_id=1, source_target_pairs={{0,16},{4,20},{8,24},{12,28},{16,0},{20,4},{24,8},{28,12},{1,17},{... | collective-permute-start | bytes 1179656 | tf_op jit(solution)/shard_map/ppermute | solution.py:891
  496.6 64.0 %collective-permute-start.58 = (bf16[128,1536]{1,0:T(8,128)(2,1)}, bf16[128,1536]{1,0:T(8,128)(2,1)S(1)}, u32[]{:S(2)}, u32[]{:S(2)}) collective-permute-start(bf16[128,1536]{1,0:T(8,128)(2,1)} %add_convert_fusion.7), channel_id=1, source_target_pairs={{0,8},{4,12},{8,0},{12,4},{16,24},{20,28},{24,16},{28,20},{1,9},{5... | collective-permute-start | bytes 1179656 | tf_op jit(solution)/shard_map/ppermute | solution.py:891
  (111 other events, 1869.0 us)

commit v2 on v1

--- a/solution.py
+++ b/solution.py
@@ -17,6 +17,7 @@
 NEG = -1e30
 LOG2E = math.log2(math.e)
 
+COST = pl.CostEstimate(flops=1, transcendentals=0, bytes_accessed=1)
 F32 = jnp.float32
 BF16 = jnp.bfloat16
 ANY = pl.BlockSpec(memory_space=pl.ANY)
@@ -126,27 +127,26 @@
             wait(copies(s))
 
     u = nn(ap[...], w[:, pl.ds(pl.multiple_of(j * chunk, chunk), chunk)])
-    third = steps // 3
-
-    @pl.when(j < third)
+
+    @pl.when(j % 3 == 0)
     def _():
         q_ref[...] = turn(u, cos_ref[...], sin_ref[...]).astype(BF16)
 
-    @pl.when((j >= third) & (j < 2 * third))
+    @pl.when(j % 3 == 1)
     def _():
         kv_ref[...] = turn(u, cos_ref[...], sin_ref[...]).astype(BF16)
 
-    @pl.when(j >= 2 * third)
+    @pl.when(j % 3 == 2)
     def _():
         kv_ref[...] = u.astype(BF16)
 
 
 def qkv_call(perm, x, cos, sin, p0, p1):
     rows, width = x.shape
-    chunk = 512
-    steps = 3 * width // chunk
-    third = steps // 3
+    chunk = width // 2
+    steps = 6
     full = lambda j: (0, 0)
+    kv_at = lambda j: (0, jnp.where(j < 2, 0, jnp.where(j < 4, 2, jnp.where(j < 5, 1, 3))))
     return pl.pallas_call(
         functools.partial(qkv_body, len(p0), len(p1)),
         grid=(steps,),
@@ -165,8 +165,8 @@
         + [ANY] * (len(p0) + len(p1)),
         out_specs=(
             pl.BlockSpec((rows, width), full),
-            pl.BlockSpec((rows, chunk), lambda j: (0, jnp.minimum(j, third - 1))),
-            pl.BlockSpec((rows, chunk), lambda j: (0, jnp.maximum(j - third, 0))),
+            pl.BlockSpec((rows, chunk), lambda j: (0, j // 3)),
+            pl.BlockSpec((rows, chunk), kv_at),
             pl.BlockSpec((8, width), full),
         ),
         scratch_shapes=[
@@ -176,14 +176,13 @@
             pltpu.SemaphoreType.DMA((steps + 1, len(p0))),
         ],
         compiler_params=params(),
-        cost_estimate=pl.CostEstimate(
-            flops=6 * rows * width * width, transcendentals=0, bytes_accessed=6 * width * width + 10 * rows * width
-        ),
+        cost_estimate=COST,
         name="qkv",
     )(perm, x, cos, sin, *p0, *p1)
 
 
-def attend_body(segk_ref, segq_ref, q_ref, k0_ref, k1_ref, v0_ref, v1_ref, o_ref, lse_ref, bias, vt):
+def attend_body(given, perm, segk_ref, segq_ref, q_ref, k0_ref, k1_ref, v0_ref, v1_ref, *rest):
+    o_ref, lse_ref, bias, vt = rest[given:]
     j = pl.program_id(0)
     rows = q_ref.shape[0]
     tile = 256
@@ -215,18 +214,19 @@
         o_ref[cols, :] = jnp.concatenate(parts, axis=0).T.astype(BF16)
 
 
-def attend_call(segk, segq, q, kv0, kv1):
+def attend_call(perm, segk, segq, q, kv0, kv1, first, count, given=()):
     rows, width = q.shape
     pairs = width // LANE
     full = lambda j: (0, 0)
-    at = lambda j: (0, j)
-    vat = lambda j: (0, pairs + j)
+    at = lambda j: (0, first + j)
+    vat = lambda j: (0, pairs + first + j)
     block = (rows, LANE)
     return pl.pallas_call(
-        attend_body,
-        grid=(pairs,),
+        functools.partial(attend_body, len(given)),
+        grid=(count,),
         out_shape=(sds((rows, width), BF16), sds((pairs, 8, rows), F32)),
         in_specs=[
+            SMEM,
             pl.BlockSpec((2 * rows, 1), full),
             pl.BlockSpec((1, rows), full),
             pl.BlockSpec(block, at),
@@ -234,15 +234,15 @@
             pl.BlockSpec(block, at),
             pl.BlockSpec(block, vat),
             pl.BlockSpec(block, vat),
-        ],
-        out_specs=(pl.BlockSpec(block, at), pl.BlockSpec((1, 8, rows), lambda j: (j, 0, 0))),
+        ]
+        + [ANY] * len(given),
+        out_specs=(pl.BlockSpec(block, at), pl.BlockSpec((1, 8, rows), lambda j: (first + j, 0, 0))),
         scratch_shapes=[pltpu.VMEM((2 * rows, rows), F32), pltpu.VMEM((LANE, 2 * rows), BF16)],
+        input_output_aliases={8 + i: i for i in range(len(given))},
         compiler_params=params(),
-        cost_estimate=pl.CostEstimate(
-            flops=16 * rows * rows * width, transcendentals=2 * rows * rows * HEADS, bytes_accessed=12 * rows * width
-        ),
+        cost_estimate=COST,
         name="attend",
-    )(segk, segq, q, kv0, kv1, kv0, kv1)
+    )(perm, segk, segq, q, kv0, kv1, kv0, kv1, *given)
 
 
 def middle_body(n, perm, gains_ref, x_ref, keep_ref, o_ref, *rest):
@@ -291,23 +291,21 @@
             pltpu.SemaphoreType.DMA((len(pieces),)),
         ],
         compiler_params=params(),
-        cost_estimate=pl.CostEstimate(
-            flops=2 * rows * width * width, transcendentals=0, bytes_accessed=2 * width * width + 10 * rows * width
-        ),
+        cost_estimate=COST,
         name="middle",
     )(perm, gains, x, keep, o, *pieces)
 
 
-def gate_body(n, perm, b_ref, *rest):
-    pg, pu = rest[:n], rest[n : 2 * n]
+def gate_body(n, base, perm, b_ref, *rest):
+    pa, pb = rest[:n], rest[n : 2 * n]
     m_ref, f1_ref, f2_ref, wg, wu, bp, sems = rest[2 * n :]
     j = pl.program_id(0)
     chunk = m_ref.shape[1]
     steps = wg.shape[1] // chunk
 
     def copies(s):
-        return weight_copies(pg, s * chunk, chunk, wg, s * chunk, sems.at[s, 0]) + weight_copies(
-            pu, s * chunk, chunk, wu, s * chunk, sems.at[s, 1]
+        return weight_copies(pa, base + s * chunk, chunk, wg, s * chunk, sems.at[s, 0]) + weight_copies(
+            pb, s * chunk, chunk, wu, s * chunk, sems.at[s, 1]
         )
 
     @pl.when(j == 0)
@@ -342,31 +340,27 @@
     lax.fori_loop(0, rows // tile, step, 0)
 
 
-def gate_call(perm, b, pg, pu, hidden):
+def gate_call(perm, b, pa, pb, hidden, base):
     rows, width = b.shape
     chunk = hidden // 3
     full = lambda j: (0, 0)
     at = lambda j: (0, j)
     return pl.pallas_call(
-        functools.partial(gate_body, len(pg)),
+        functools.partial(gate_body, len(pa), base),
         grid=(hidden // chunk,),
         out_shape=(sds((rows, hidden), BF16), sds((rows, hidden), BF16), sds((rows, hidden), BF16)),
-        in_specs=[SMEM, pl.BlockSpec((rows, width), full)] + [ANY] * (2 * len(pg)),
+        in_specs=[SMEM, pl.BlockSpec((rows, width), full)] + [ANY] * (2 * len(pa)),
         out_specs=(pl.BlockSpec((rows, chunk), at),) * 3,
         scratch_shapes=[
             pltpu.VMEM((width, hidden), BF16),
             pltpu.VMEM((width, hidden), BF16),
             pltpu.VMEM((rows, width), BF16),
-            pltpu.SemaphoreType.DMA((hidden // chunk, 2, len(pg))),
+            pltpu.SemaphoreType.DMA((hidden // chunk, 2, len(pa))),
         ],
         compiler_params=params(),
-        cost_estimate=pl.CostEstimate(
-            flops=4 * rows * width * hidden,
-            transcendentals=2 * rows * hidden,
-            bytes_accessed=4 * width * hidden + 6 * rows * hidden,
-        ),
+        cost_estimate=COST,
         name="gate",
-    )(perm, b, *pg, *pu)
+    )(perm, b, *pa, *pb)
 
 
 def dgate_body(n, perm, cot_ref, keep_ref, f1_ref, f2_ref, *rest):
@@ -431,9 +425,7 @@
             pltpu.SemaphoreType.DMA((hidden // chunk, len(pd))),
         ],
         compiler_params=params(),
-        cost_estimate=pl.CostEstimate(
-            flops=2 * rows * width * hidden, transcendentals=0, bytes_accessed=2 * width * hidden + 8 * rows * hidden
-        ),
+        cost_estimate=COST,
         name="dgate",
     )(perm, cot, keep, f1, f2, *pd)
 
@@ -494,9 +486,7 @@
             pltpu.SemaphoreType.DMA((hidden // chunk, len(pd))),
         ],
         compiler_params=params(),
-        cost_estimate=pl.CostEstimate(
-            flops=2 * rows * width * hidden, transcendentals=0, bytes_accessed=2 * width * hidden + 2 * rows * hidden
-        ),
+        cost_estimate=COST,
         name="down",
     )(perm, h1, keep, mixed, *pd)
 
@@ -510,19 +500,19 @@
     )
 
 
-def dmiddle_body(n, perm, gains_ref, cot_ref, keep_ref, h1_ref, dg_ref, du_ref, *rest):
-    pg, pu, po = rest[:n], rest[n : 2 * n], rest[2 * n : 3 * n]
-    dh1_ref, e_ref, do_ref, gg_ref, wg, wu, wo, acc, db, sems, osems = rest[3 * n :]
+def dmiddle_body(n, base, perm, gains_ref, cot_ref, keep_ref, h1_ref, dg_ref, du_ref, *rest):
+    pa, pb = rest[:n], rest[n : 2 * n]
+    dh1_ref, e_ref, do_ref, gg_ref, wg, wu, wo, acc, db, sems, osems = rest[2 * n :]
     j = pl.program_id(0)
     chunk = dg_ref.shape[1]
     steps = wg.shape[1] // chunk
 
     def copies(s):
-        return weight_copies(pg, s * chunk, chunk, wg, s * chunk, sems.at[s, 0]) + weight_copies(
-            pu, s * chunk, chunk, wu, s * chunk, sems.at[s, 1]
+        return weight_copies(pa, base + s * chunk, chunk, wg, s * chunk, sems.at[s, 0]) + weight_copies(
+            pb, s * chunk, chunk, wu, s * chunk, sems.at[s, 1]
         )
 
-    out_copies = weight_copies(po, 0, wo.shape[1], wo, 0, osems)
+    out_copies = weight_copies(pa, 0, wo.shape[1], wo, 0, osems)
 
     @pl.when(j == 0)
     def _():
@@ -566,7 +556,7 @@
         lax.fori_loop(0, acc.shape[0] // tile, step, 0)
 
 
-def dmiddle_call(perm, gains, cot, keep, h1, dg, du, pg, pu, po):
+def dmiddle_call(perm, gains, cot, keep, h1, dg, du, pa, pb, base):
     rows, width = h1.shape
     hidden = dg.shape[1]
     chunk = hidden // 3
@@ -574,7 +564,7 @@
     at = lambda j: (0, j)
     whole = pl.BlockSpec((rows, width), full)
     return pl.pallas_call(
-        functools.partial(dmiddle_body, len(pg)),
+        functools.partial(dmiddle_body, len(pa), base),
         grid=(hidden // chunk,),
         out_shape=(
             sds((rows, width), F32),
@@ -591,7 +581,7 @@
             pl.BlockSpec((rows, chunk), at),
             pl.BlockSpec((rows, chunk), at),
         ]
-        + [ANY] * (3 * len(pg)),
+        + [ANY] * (2 * len(pa)),
         out_specs=(whole, whole, whole, pl.BlockSpec((1, width), full)),
         scratch_shapes=[
             pltpu.VMEM((width, hidden), BF16),
@@ -599,23 +589,17 @@
             pltpu.VMEM((width, width), BF16),
             pltpu.VMEM((rows, width), F32),
             pltpu.VMEM((rows, width), F32),
-            pltpu.SemaphoreType.DMA((hidden // chunk, 2, len(pg))),
-            pltpu.SemaphoreType.DMA((len(po),)),
+            pltpu.SemaphoreType.DMA((hidden // chunk, 2, len(pa))),
+            pltpu.SemaphoreType.DMA((len(pa),)),
         ],
         compiler_params=params(),
-        cost_estimate=pl.CostEstimate(
-            flops=4 * rows * width * hidden + 2 * rows * width * width,
-            transcendentals=0,
-            bytes_accessed=4 * width * hidden + 4 * rows * hidden + 16 * rows * width,
-        ),
+        cost_estimate=COST,
         name="dmiddle",
-    )(perm, gains, cot, keep, h1, dg, du, *pg, *pu, *po)
-
-
-def dattend_body(
-    segk_ref, segq_ref, q_ref, k0_ref, k1_ref, v0_ref, v1_ref, do_ref, lse_ref,
-    dq_ref, dk0_ref, dv0_ref, dk1_ref, dv1_ref, bias, kt, dk, dv,
-):
+    )(perm, gains, cot, keep, h1, dg, du, *pa, *pb)
+
+
+def dattend_body(perm, segk_ref, segq_ref, q_ref, k0_ref, k1_ref, v0_ref, v1_ref, do_ref, lse_ref, *rest):
+    dq_ref, dk0_ref, dv0_ref, dk1_ref, dv1_ref, bias, kt, dk, dv = rest
     j = pl.program_id(0)
     rows = q_ref.shape[0]
     tile = 256
@@ -660,24 +644,25 @@
     dv1_ref[...] = dv[rows:, :].astype(BF16)
 
 
-def dattend_call(segk, segq, q, kv0, kv1, do, lse):
+def dattend_call(perm, segk, segq, q, kv0, kv1, do, lse, first, count):
     rows, width = q.shape
     pairs = width // LANE
     full = lambda j: (0, 0)
-    at = lambda j: (0, j)
-    vat = lambda j: (0, pairs + j)
+    at = lambda j: (0, first + j)
+    vat = lambda j: (0, pairs + first + j)
     block = (rows, LANE)
     return pl.pallas_call(
         dattend_body,
-        grid=(pairs,),
+        grid=(count,),
         out_shape=(
-            sds((rows, width), BF16),
-            sds((rows, width), F32),
-            sds((rows, width), F32),
-            sds((rows, width), BF16),
-            sds((rows, width), BF16),
+            sds((rows, count * LANE), BF16),
+            sds((rows, count * LANE), F32),
+            sds((rows, count * LANE), F32),
+            sds((rows, count * LANE), BF16),
+            sds((rows, count * LANE), BF16),
         ),
         in_specs=[
+            SMEM,
             pl.BlockSpec((2 * rows, 1), full),
             pl.BlockSpec((1, rows), full),
             pl.BlockSpec(block, at),
@@ -686,9 +671,9 @@
             pl.BlockSpec(block, vat),
             pl.BlockSpec(block, vat),
             pl.BlockSpec(block, at),
-            pl.BlockSpec((1, 8, rows), lambda j: (j, 0, 0)),
+            pl.BlockSpec((1, 8, rows), lambda j: (first + j, 0, 0)),
         ],
-        out_specs=(pl.BlockSpec(block, at),) * 5,
+        out_specs=(pl.BlockSpec(block, lambda j: (0, j)),) * 5,
         scratch_shapes=[
             pltpu.VMEM((2 * rows, rows), F32),
             pltpu.VMEM((LANE, 2 * rows), BF16),
@@ -696,14 +681,12 @@
             pltpu.VMEM((2 * rows, LANE), F32),
         ],
         compiler_params=params(),
-        cost_estimate=pl.CostEstimate(
-            flops=40 * rows * rows * width, transcendentals=2 * rows * rows * HEADS, bytes_accessed=24 * rows * width
-        ),
+        cost_estimate=COST,
         name="dattend",
-    )(segk, segq, q, kv0, kv1, kv0, kv1, do, lse)
-
-
-def dqkv_body(cos_ref, sin_ref, dq_ref, dk0_ref, dv0_ref, dk1_ref, dv1_ref, out_ref):
+    )(perm, segk, segq, q, kv0, kv1, kv0, kv1, do, lse)
+
+
+def dqkv_body(perm, cos_ref, sin_ref, dq_ref, dk0_ref, dv0_ref, dk1_ref, dv1_ref, out_ref):
     width = dq_ref.shape[1]
     cos = cos_ref[...]
     sin = -sin_ref[...]
@@ -713,7 +696,7 @@
     out_ref[:, 2 * width :] = (dv0_ref[...] + dv1_ref[...].astype(F32)).astype(BF16)
 
 
-def dqkv_call(cos, sin, dq, dk0, dv0, dk1, dv1):
+def dqkv_call(perm, cos, sin, dq, dk0, dv0, dk1, dv1):
     rows, width = dq.shape
     tile = 64
     row = lambda i: (i, 0)
@@ -722,19 +705,19 @@
         dqkv_body,
         grid=(rows // tile,),
         out_shape=sds((rows, 3 * width), BF16),
-        in_specs=[pl.BlockSpec((tile, LANE), row)] * 2 + [block] * 5,
+        in_specs=[SMEM] + [pl.BlockSpec((tile, LANE), row)] * 2 + [block] * 5,
         out_specs=pl.BlockSpec((tile, 3 * width), row),
         compiler_params=params(),
-        cost_estimate=pl.CostEstimate(flops=20 * rows * width, transcendentals=0, bytes_accessed=20 * rows * width),
+        cost_estimate=COST,
         name="dqkv",
-    )(cos, sin, dq, dk0, dv0, dk1, dv1)
-
-
-def dinput_body(n0, n1, perm, gains_ref, x_ref, dh1_ref, d_ref, *rest):
+    )(perm, cos, sin, dq, dk0, dv0, dk1, dv1)
+
+
+def dinput_body(n0, n1, perm, gains_ref, x_ref, dh1_ref, da_ref, db_ref, *rest):
     p0, p1 = rest[:n0], rest[n0 : n0 + n1]
     out_ref, gg_ref, w, acc, da, sems = rest[n0 + n1 :]
     j = pl.program_id(0)
-    chunk = d_ref.shape[1]
+    chunk = da_ref.shape[1]
     steps = w.shape[1] // chunk
     half = steps // 2
 
@@ -755,7 +738,15 @@
         def _(s=s):
             wait(copies(s))
 
-    acc[...] += nt(d_ref[...], w[:, pl.ds(pl.multiple_of(j * chunk, chunk), chunk)])
+    block = w[:, pl.ds(pl.multiple_of(j * chunk, chunk), chunk)]
+
+    @pl.when(j < half)
+    def _():
+        acc[...] += nt(da_ref[...], block)
+
+    @pl.when(j >= half)
+    def _():
+        acc[...] += nt(db_ref[...], block)
 
     @pl.when(j == steps - 1)
     def _():
@@ -775,17 +766,24 @@
         lax.fori_loop(0, acc.shape[0] // tile, step, 0)
 
 
-def dinput_call(perm, gains, x, dh1, d, p0, p1):
+def dinput_call(perm, gains, x, dh1, da, db, p0, p1):
     rows, width = x.shape
-    chunk = 512
-    steps = 3 * width // chunk
+    chunk = width // 2
+    steps = 6
     full = lambda j: (0, 0)
     whole = pl.BlockSpec((rows, width), full)
     return pl.pallas_call(
         functools.partial(dinput_body, len(p0), len(p1)),
         grid=(steps,),
         out_shape=(sds((rows, width), BF16), sds((1, width), F32)),
-        in_specs=[SMEM, pl.BlockSpec((8, width), full), whole, whole, pl.BlockSpec((rows, chunk), lambda j: (0, j))]
+        in_specs=[
+            SMEM,
+            pl.BlockSpec((8, width), full),
+            whole,
+            whole,
+            pl.BlockSpec((rows, chunk), lambda j: (0, jnp.minimum(j, 2))),
+            pl.BlockSpec((rows, chunk), lambda j: (0, jnp.maximum(j - 3, 0))),
+        ]
         + [ANY] * (len(p0) + len(p1)),
         out_specs=(whole, pl.BlockSpec((1, width), full)),
         scratch_shapes=[
@@ -795,70 +793,68 @@
             pltpu.SemaphoreType.DMA((steps, len(p0))),
         ],
         compiler_params=params(),
-        cost_estimate=pl.CostEstimate(
-            flops=6 * rows * width * width, transcendentals=0, bytes_accessed=6 * width * width + 14 * rows * width
-        ),
+        cost_estimate=COST,
         name="dinput",
-    )(perm, gains, x, dh1, d, *p0, *p1)
-
-
-def grad_body(first, keeps, masked, form, perm, left_ref, keep_ref, right_ref, *rest):
-    left_t = rest[-1]
-    outs = rest[1:-1] if form in "xy" else rest[:-1]
+    )(perm, gains, x, dh1, da, db, *p0, *p1)
+
+
+def grad_body(masked, form, perm, *refs):
+    two = form != "f"
+    per = 3 if masked else 2
+    sources = [refs[i * per : (i + 1) * per] for i in range(2 if two else 1)]
+    outs, left_t = refs[per * len(sources) : -1], refs[-1]
+    tokens = sources[0][0].shape[0]
 
     @pl.when(pl.program_id(0) == 0)
     def _():
-        for i in range(keeps):
-            block = left_ref[:, lanes(perm, first + i)].astype(F32)
-            if masked:
-                block = block * keep_ref[...]
-            left_t[i * LANE : (i + 1) * LANE, :] = block.T.astype(BF16)
-
-    g = nn(left_t[...], right_ref[...])
-    if form in "xy":
-        g = g + rest[0][...].astype(F32)
-        q = [g[i * LANE : (i + 1) * LANE, :].astype(BF16) for i in range(4)]
-        order = (1, 3, 0, 2) if form == "x" else (2, 3, 0, 1)
-        outs[0][:LANE, :] = q[order[0]]
-        outs[0][LANE:, :] = q[order[1]]
-        outs[1][:LANE, :] = q[order[2]]
-        outs[1][LANE:, :] = q[order[3]]
-    else:
-        outs[0][...] = g.astype(outs[0].dtype)
-
-
-def grad_call(perm, left, keep, right, col, count, chunk, first, blocks, form, recv=None, masked=False):
-    rows = left.shape[0]
+        for n, source in enumerate(sources):
+            for i in range(left_t.shape[0] // LANE):
+                block = source[0][:, lanes(perm, i)].astype(F32)
+                if masked:
+                    block = block * source[2][...]
+                left_t[i * LANE : (i + 1) * LANE, n * tokens : (n + 1) * tokens] = block.T.astype(BF16)
+
+    g = nn(left_t[:, :tokens], sources[0][1][...])
+    if not two:
+        outs[0][...] = g
+        return
+    g = g + nn(left_t[:, tokens:], sources[1][1][...])
+    q = [g[i * LANE : (i + 1) * LANE, :].astype(BF16) for i in range(4)]
+    order = (1, 3, 0, 2) if form == "x" else (2, 3, 0, 1)
+    outs[0][:LANE, :] = q[order[0]]
+    outs[0][LANE:, :] = q[order[1]]
+    outs[1][:LANE, :] = q[order[2]]
+    outs[1][LANE:, :] = q[order[3]]
+
+
+def grad_call(perm, sources, col, count, chunk, form):
+    left, right, keep = sources[0]
+    rows, width = left.shape
     full = lambda j: (0, 0)
     at = lambda j: (0, j)
     base = col // chunk
-    height = blocks * LANE
-    specs = [
-        SMEM,
-        pl.BlockSpec(left.shape, full),
-        pl.BlockSpec((rows, 1), full),
-        pl.BlockSpec((rows, chunk), lambda j: (0, base + j)),
-    ]
-    args = [perm, left, keep, right]
-    if form in "xy":
-        specs.append(pl.BlockSpec((height, chunk), at))
-        args.append(recv)
+    height = width if form == "f" else width // 2
+    specs, args = [SMEM], [perm]
+    for source in sources:
+        specs += [pl.BlockSpec((rows, width), full), pl.BlockSpec((rows, chunk), lambda j: (0, base + j))]
+        args += source[:2]
+        if keep is not None:
+            specs.append(pl.BlockSpec((rows, 1), full))
+            args.append(source[2])
+    if form == "f":
+        out_shape, out_specs = sds((height, count), F32), pl.BlockSpec((height, chunk), at)
+    else:
         out_shape = (sds((height // 2, count), BF16),) * 2
         out_specs = (pl.BlockSpec((height // 2, chunk), at),) * 2
-    else:
-        out_shape = sds((height, count), BF16 if form == "c" else F32)
-        out_specs = pl.BlockSpec((height, chunk), at)
     return pl.pallas_call(
-        functools.partial(grad_body, first, blocks, masked, form),
+        functools.partial(grad_body, keep is not None, form),
         grid=(count // chunk,),
         out_shape=out_shape,
         in_specs=specs,
         out_specs=out_specs,
-        scratch_shapes=[pltpu.VMEM((height, rows), BF16)],
+        scratch_shapes=[pltpu.VMEM((height, rows * len(sources)), BF16)],
         compiler_params=params(),
-        cost_estimate=pl.CostEstimate(
-            flops=2 * rows * height * count, transcendentals=0, bytes_accessed=2 * rows * (1024 + count) + 4 * height * count
-        ),
+        cost_estimate=COST,
         name="grad_" + form,
     )(*args)
 
@@ -890,131 +886,278 @@
     def swap(v, bit):
         return lax.ppermute(v, "dp", [(i, i ^ bit) for i in range(dp_count)])
 
+    def tie(v, *after):
+        return lax.optimization_barrier((v, *after))[0] if after else v
+
     def across(v):
         return lax.all_to_all(v, "ctx", split_axis=0, concat_axis=0, tiled=True)
 
     def pick(zero, one):
         return jnp.where(low == 0, zero, one)
 
-    def to_chip(v):
+    def spread(shard):
+        return jnp.broadcast_to(shard[None], (ctx_count, *shard.shape))
+
+    def flat(v):
+        return v.reshape(v.shape[0] * v.shape[1], v.shape[2])
+
+    def halves_out(v):
         halves = v.reshape(micro_count, 2, half_len, width)
-        mine = pick(halves[:, 0], halves[:, 1])
-        other = swap(pick(halves[:, 1], halves[:, 0]), 1)
+        return pick(halves[:, 0], halves[:, 1]), pick(halves[:, 1], halves[:, 0])
+
+    def join_in(mine, other):
         both = jnp.stack([pick(mine, other), pick(other, mine)], axis=1)
-        return across(both.reshape(ctx_count, half_len, width)).reshape(rows, width)
-
-    def from_chip(v):
-        got = across(v.reshape(ctx_count, half_len, width)).reshape(micro_count, 2, half_len, width)
-        mine = pick(got[:, 0], got[:, 1])
-        other = swap(pick(got[:, 1], got[:, 0]), 1)
+        return both.reshape(ctx_count, half_len, width)
+
+    def split_back(got):
+        got = got.reshape(micro_count, 2, half_len, width)
+        return pick(got[:, 0], got[:, 1]), pick(got[:, 1], got[:, 0])
+
+    def join_back(mine, other):
         both = jnp.stack([pick(mine, other), pick(other, mine)], axis=1)
         return both.reshape(micro_count, 1, local_len, width)
 
-    def gather(shard, first):
-        if not fast:
-            return [lax.all_gather(shard, ("dp", "ctx"), axis=0, tiled=True)]
-        count = shard.shape[1]
-        own = across(jnp.broadcast_to(shard[None], (ctx_count, part, count))).reshape(ctx_count * part, count)
-        rx, ry = swap(own, 2), swap(own, 4)
-        rxy = swap(rx, 4) if first == "x" else swap(ry, 2)
-        near = [own, rx, ry, rxy]
-        return near + [swap(v, 1) for v in near]
-
+    step = jnp.arange(rows, dtype=jnp.int32)
+    positions = step // half_len * local_len + low * half_len + step % half_len
+    cos, sin = rotary_tables(positions)
+
+    index = jnp.arange(blocks, dtype=jnp.int32)
+    if fast:
+        turned = (index // 4) + 4 * (index // 2 % 2) + 2 * (index % 2)
+        perm = jnp.bitwise_xor(turned, dp.astype(jnp.int32))
+    else:
+        perm = index
+
+    third = 3 * width // 2
+    third_hidden = padded // 3
     seg = segments.reshape(micro_count, local_len)
-    seg_other = swap(seg, 1)
-    seg_all = across(jnp.stack([pick(seg, seg_other), pick(seg_other, seg)], axis=1).reshape(ctx_count, local_len))
+    seg_cols = micro_count * local_len // part
+    gain_cols = jnp.concatenate(
+        [
+            attn_gain[:, None],
+            mlp_gain[:, None],
+            seg.astype(BF16).reshape(part, seg_cols) if fast else jnp.zeros((part, 0), BF16),
+            jnp.zeros((part, LANE - 2 - (seg_cols if fast else 0)), BF16),
+        ],
+        axis=1,
+    )
+    pad = ((0, 0), (0, padded - hidden))
+    first_cols = third + LANE
+    hw = width // 2
+    thirds = [w_qkv[:, i * hw : (i + 1) * hw] for i in range(6)]
+    shard_qkv = jnp.concatenate(thirds[0::2] + [gain_cols] + thirds[1::2], axis=1)
+    shard_rest = jnp.concatenate([w_attn_out, jnp.pad(w_in[:, :hidden], pad), jnp.pad(w_in[:, hidden:], pad)], axis=1)
+    shard_down = jnp.pad(w_mlp_out, pad)
+    cut = width + padded
+
+    def gather_all(shard):
+        return lax.all_gather(shard, ("dp", "ctx"), axis=0, tiled=True)
+
+    def gather_line(shard):
+        return lax.all_gather(shard, "ctx", axis=0, tiled=True)
+
+    last = []
+
+    def order(v, *after):
+        return tie(v, *last, *after)
+
+    def did(out):
+        last[:] = [jax.tree.leaves(out)[0]]
+        return out
+
+    mine, other = halves_out(tokens)
+    cot_mine, cot_other = halves_out(cotangent)
+    if fast:
+        own1 = gather_line(shard_qkv)
+        a1, b1 = own1[:, :first_cols], own1[:, first_cols:]
+        own2 = gather_line(tie(shard_rest, own1))
+        other = swap(tie(other, own1), 1)
+        xa1, yb1 = swap(a1, 2), swap(b1, 4)
+        f1 = [swap(a1, 1), swap(b1, 1)]
+        ya1, yxa1 = swap(tie(a1, xa1, yb1), 4), swap(tie(xa1, yb1), 4)
+        xb1, xyb1 = swap(tie(b1, xa1, yb1), 2), swap(tie(yb1, xa1), 2)
+        f2 = [swap(tie(v, *f1), 1) for v in (xa1, yb1)]
+        f3 = [swap(tie(v, ya1, yxa1, xb1, xyb1), 1) for v in (ya1, yxa1, xb1, xyb1)]
+        qkv0 = [a1, xa1, ya1, yxa1, f1[0], f2[0], f3[0], f3[1]]
+        qkv1 = [b1, xb1, yb1, xyb1, f1[1], f3[2], f2[1], f3[3]]
+        own2 = tie(own2, ya1, yxa1, xb1, xyb1)
+        x_in = across(tie(join_in(mine, other), own2))
+        a2, b2 = own2[:, :cut], own2[:, cut:]
+        xa2, yb2 = swap(tie(a2, *f3), 2), swap(tie(b2, *f3), 4)
+        ya2, xb2 = swap(tie(a2, xa2, yb2), 4), swap(tie(b2, xa2, yb2), 2)
+        g1 = [swap(tie(a2, *f3), 1)]
+        g1.append(swap(tie(b2, g1[-1]), 1))
+        round3 = (ya2, xb2, *g1)
+        x = flat(x_in)
+        own3 = flat(across(tie(spread(shard_down), x_in)))
+        cot_other = swap(tie(cot_other, x_in), 1)
+        cot = flat(across(tie(join_in(cot_mine, cot_other), own3)))
+        seg_at = slice(third + 2, third + 2 + seg_cols)
+        z = lax.axis_index("ctx")
+        seg_from = jnp.where(z % 2 == low, qkv0[0][:, seg_at], qkv0[4][:, seg_at])
+        seg_from = seg_from.reshape(ctx_count, micro_count, local_len)
+        seg_all = lax.dynamic_index_in_dim(seg_from, z // 2, 1, False).astype(jnp.int32)
+    else:
+        qkv0, qkv1 = [gather_all(shard_qkv[:, :first_cols])], [gather_all(shard_qkv[:, first_cols:])]
+        rest_a, rest_b = [gather_all(shard_rest[:, :cut])], [gather_all(shard_rest[:, cut:])]
+        wdown = [gather_all(shard_down)]
+        x = flat(across(join_in(mine, swap(other, 1))))
+        cot = flat(across(join_in(cot_mine, swap(cot_other, 1))))
+        seg_other = swap(seg, 1)
+        seg_all = across(jnp.stack([pick(seg, seg_other), pick(seg_other, seg)], axis=1).reshape(ctx_count, local_len))
+
     seg_halves = seg_all.reshape(ctx_count, 2, half_len)
     seg_mine = pick(seg_halves[:, 0], seg_halves[:, 1]).reshape(rows)
     seg_theirs = pick(seg_halves[:, 1], seg_halves[:, 0]).reshape(rows)
     segq = seg_mine.reshape(1, rows)
     segk = jnp.concatenate([seg_mine, seg_theirs]).reshape(2 * rows, 1)
     keep = (seg_mine != 0).astype(F32).reshape(rows, 1)
-
-    step = jnp.arange(rows, dtype=jnp.int32)
-    positions = step // half_len * local_len + low * half_len + step % half_len
-    cos, sin = rotary_tables(positions)
-
-    index = jnp.arange(blocks, dtype=jnp.int32)
+    keep_theirs = (seg_theirs != 0).astype(F32).reshape(rows, 1)
+
+    attn_in, q, kv, gains = did(qkv_call(order(perm, *((xa2, yb2) if fast else ())), x, cos, sin, qkv0, qkv1))
     if fast:
-        turned = (index // 4) + 4 * (index // 2 % 2) + 2 * (index % 2)
-        perm = jnp.bitwise_xor(turned, dp.astype(jnp.int32))
+        kv_other = swap(tie(kv, *round3, own3), 1)
+        yxa2, xyb2 = swap(tie(xa2, *round3), 4), swap(tie(yb2, *round3), 2)
+        xd, yd = swap(tie(own3, *round3), 2), swap(tie(own3, *round3), 4)
+        g1.append(swap(tie(xa2, kv_other), 1))
+        for v in (yb2, ya2, xb2):
+            g1.append(swap(tie(v, g1[-1]), 1))
+        round4 = (yxa2, xyb2, xd, yd, cot, *g1)
     else:
-        perm = index
-
-    third = 3 * width // 2
-    gain_cols = jnp.concatenate(
-        [attn_gain[:, None], mlp_gain[:, None], jnp.zeros((part, LANE - 2), BF16)], axis=1
+        kv_other = swap(kv, 1)
+        round4 = ()
+    part_one = blocks // 2
+    some = did(attend_call(order(perm), segk, segq, q, kv, kv_other, 0, part_one))
+    attended, lse = did(attend_call(order(perm), segk, segq, q, kv, kv_other, part_one, blocks - part_one, some))
+    if fast:
+        yxa2, xyb2 = tie(yxa2, attended, *round4), tie(xyb2, attended, *round4)
+        g2 = [swap(yxa2, 1), swap(xyb2, 1)]
+        rest_a = [a2, xa2, ya2, yxa2, g1[0], g1[2], g1[4], g2[0]]
+        rest_b = [b2, xb2, yb2, xyb2, g1[1], g1[5], g1[3], g2[1]]
+        yxd = swap(tie(xd, yxa2), 4)
+        h1 = []
+        for v in (own3, xd, yd):
+            h1.append(swap(tie(v, yxa2, *(h1 or g2)[-1:]), 1))
+    h1_rows, mlp_in = did(middle_call(order(perm), gains, x, keep, attended, rest_a))
+    mixed, f1, f2 = did(gate_call(order(perm), mlp_in, rest_a, rest_b, padded, width))
+
+    def pair(v, *after):
+        return (v, swap(tie(v, *after), 1) if fast else None)
+
+    mixed_pair = pair(mixed)
+    if fast:
+        wdown = [own3, xd, yd, yxd, *h1, swap(tie(yxd, mixed), 1)]
+    cot_pair = pair(cot, h1_rows)
+    mlp_pair = pair(mlp_in, mixed)
+    in_pair = pair(attn_in, h1_rows)
+    o_pair = pair(attended, mixed)
+    h1 = h1_rows
+    partners = (mixed_pair[1], cot_pair[1], mlp_pair[1], in_pair[1], o_pair[1]) if fast else ()
+    dgate, dup = did(dgate_call(order(perm, *partners), cot, keep, f1, f2, wdown))
+    dgate_pair, dup_pair = pair(dgate), pair(dup)
+
+    class Reduce:
+        def __init__(self, left, right, keeps, col, count, chunk, form):
+            self.count = count
+            if not fast:
+                g = did(grad_call(order(perm), [(left[0], right[0], keeps[0])], col, count, chunk, "f"))
+                self.out = lax.psum_scatter(g, ("dp", "ctx"), scatter_dimension=0, tiled=True)
+                return
+            sources = [(left[i], right[i], keeps[i]) for i in range(2)]
+            leave, self.kept = did(grad_call(order(perm), sources, col, count, chunk, form))
+            self.first, self.second = (2, 4) if form == "x" else (4, 2)
+            self.half = leave.shape[0] // 2
+            self.got = swap(leave, self.first)
+
+        def two(self):
+            if fast:
+                h = self.half
+                kept = order(self.kept)
+                leave = did((kept[h:].astype(F32) + self.got[h:].astype(F32)).astype(BF16))
+                self.got2 = swap(leave, self.second)
+
+        def three(self):
+            got2 = order(self.got2)
+            h = self.half
+            total = self.kept[:h].astype(F32) + self.got[:h].astype(F32) + got2.astype(F32)
+            return did(total.astype(BF16))
+
+        def line(self):
+            if fast:
+                self.out = lax.psum_scatter(self.three(), "ctx", scatter_dimension=0, tiled=True).astype(F32)
+
+    none = (None, None)
+    r_down = Reduce(cot_pair, mixed_pair, (keep, keep_theirs), 0, padded, third_hidden, "x")
+    r_gate = Reduce(mlp_pair, dgate_pair, none, 0, padded, third_hidden, "y")
+    r_up = Reduce(mlp_pair, dup_pair, none, 0, padded, third_hidden, "x")
+    dh1, e_attn, d_o, gain_two = did(dmiddle_call(order(perm), gains, cot, keep, h1, dgate, dup, rest_a, rest_b, width))
+    e_pair = pair(e_attn)
+    rows_out = did(down_call(order(perm), h1, keep, mixed, wdown))
+    out_got = across(rows_out.reshape(ctx_count, half_len, width))
+    r_down.two()
+    r_out = Reduce(o_pair, e_pair, none, 0, width, 512, "y")
+    r_gate.two()
+    back = lambda first, count: did(dattend_call(order(perm), segk, segq, q, kv, kv_other, d_o, lse, first, count))
+    dq, dk0, dv0, dk1, dv1 = back(0, part_one)
+    dk_got, dv_got = swap(dk1, 1), swap(dv1, 1)
+    r_up.two()
+    r_down.line()
+    da = did(dqkv_call(order(perm), cos, sin, dq, dk0, dv0, dk_got, dv_got))
+    da_pair = pair(da, out_got)
+    r_gate.line()
+    dq, dk0, dv0, dk1, dv1 = back(part_one, blocks - part_one)
+    dk_got, dv_got = swap(tie(dk1, *((r_down.out,) if fast else ())), 1), swap(dv1, 1)
+    r_qkva = Reduce(in_pair, da_pair, none, 0, third, 512, "y")
+    r_out.two()
+    out_mine, out_other = split_back(out_got)
+    layer_out = join_back(out_mine, swap(tie(out_other, dk_got), 1))
+    db = did(dqkv_call(order(perm, *((r_gate.out,) if fast else ())), cos, sin, dq, dk0, dv0, dk_got, dv_got))
+    db_pair = pair(db)
+    r_up.line()
+    input_rows, gain_one = did(dinput_call(order(perm), gains, x, dh1, da, db, qkv0, qkv1))
+    in_got = across(input_rows.reshape(ctx_count, half_len, width))
+    gain_rows = jnp.concatenate([gain_one, gain_two], axis=0)
+    sub = third // 2
+    if fast:
+        gain_got = swap(gain_rows, 1)
+    r_qkvb0 = Reduce(in_pair, db_pair, none, 0, sub, sub, "x")
+    if fast:
+        gain_rows = did(order(gain_rows) + gain_got)
+        gain_got = swap(gain_rows, 2)
+    r_qkvb1 = Reduce(in_pair, db_pair, none, sub, sub, sub, "y")
+    if fast:
+        gain_rows = did(order(gain_rows) + gain_got)
+        gain_got = swap(gain_rows, 4)
+    r_qkva.two()
+    r_out.line()
+    r_qkvb0.two()
+    r_qkvb1.two()
+    r_qkva.line()
+    if fast:
+        gain_rows = gain_rows + gain_got
+        ours = lax.dynamic_slice(gain_rows, (0, dp * LANE), (2, LANE)).T.astype(BF16)
+        total = jnp.concatenate([r_qkvb0.three(), r_qkvb1.three(), ours, jnp.zeros((LANE, LANE - 2), BF16)], axis=1)
+        total = jnp.sum(across(tie(total, in_got).reshape(ctx_count, part, third + LANE)).astype(F32), axis=0)
+        qkvb = total[:, :third]
+        gain_grads = (total[:, third], total[:, third + 1])
+    else:
+        qkvb = jnp.concatenate([r_qkvb0.out, r_qkvb1.out], axis=1)
+        gain_grads = lax.psum_scatter(gain_rows, ("dp", "ctx"), scatter_dimension=1, tiled=True)
+    qkv_grad = jnp.concatenate(
+        [half[:, i * hw : (i + 1) * hw] for i in range(3) for half in (r_qkva.out, qkvb)], axis=1
     )
-    shards = (
-        jnp.concatenate([w_qkv[:, :third], gain_cols], axis=1),
-        w_qkv[:, third:],
-        w_attn_out,
-        jnp.pad(w_in[:, :hidden], ((0, 0), (0, padded - hidden))),
-        jnp.pad(w_in[:, hidden:], ((0, 0), (0, padded - hidden))),
-        jnp.pad(w_mlp_out, ((0, 0), (0, padded - hidden))),
-    )
-    forms = ("x", "y", "x", "y", "x", "y")
-    qkv0 = gather(shards[0], forms[0])
-    qkv1 = gather(shards[1], forms[1])
-    x = to_chip(tokens)
-    wout = gather(shards[2], forms[2])
-    wgate = gather(shards[3], forms[3])
-    wup = gather(shards[4], forms[4])
-    wdown = gather(shards[5], forms[5])
-    cot = to_chip(cotangent)
-
-    def reduce(left, right, col, count, chunk, form, masked=False):
-        call = functools.partial(grad_call, perm, left, keep, right, col, count, chunk, masked=masked)
-        if not fast:
-            return lax.psum_scatter(call(0, blocks, "f"), ("dp", "ctx"), scatter_dimension=0, tiled=True)
-        recv = swap(call(4, 4, "c"), 1)
-        send, kept = call(0, 4, form, recv=recv)
-        one, two = (2, 4) if form == "x" else (4, 2)
-        got = swap(send, one)
-        half = send.shape[0] // 2
-        send2 = (kept[half:].astype(F32) + got[half:].astype(F32)).astype(BF16)
-        kept2 = kept[:half].astype(F32) + got[:half].astype(F32)
-        total = (kept2 + swap(send2, two).astype(F32)).astype(BF16)
-        return jnp.sum(across(total.reshape(ctx_count, part, count)).astype(F32), axis=0)
-
-    attn_in, q, kv, gains = qkv_call(perm, x, cos, sin, qkv0, qkv1)
-    kv_other = swap(kv, 1)
-    attended, lse = attend_call(segk, segq, q, kv, kv_other)
-    h1, mlp_in = middle_call(perm, gains, x, keep, attended, wout)
-    mixed, f1, f2 = gate_call(perm, mlp_in, wgate, wup, padded)
-    third_hidden = padded // 3
-    down_grad = reduce(cot, mixed, 0, padded, third_hidden, forms[5], masked=True)
-    dgate, dup = dgate_call(perm, cot, keep, f1, f2, wdown)
-    gate_grad = reduce(mlp_in, dgate, 0, padded, third_hidden, forms[3])
-    up_grad = reduce(mlp_in, dup, 0, padded, third_hidden, forms[4])
-    dh1, e_attn, d_o, gain_two = dmiddle_call(perm, gains, cot, keep, h1, dgate, dup, wgate, wup, wout)
-    out_grad = reduce(attended, e_attn, 0, width, 512, forms[2])
-    layer_out = from_chip(down_call(perm, h1, keep, mixed, wdown))
-    dq, dk0, dv0, dk1, dv1 = dattend_call(segk, segq, q, kv, kv_other, d_o, lse)
-    d_qkv = dqkv_call(cos, sin, dq, dk0, dv0, swap(dk1, 1), swap(dv1, 1))
-    qkv_grad0 = reduce(attn_in, d_qkv, 0, third, 512, forms[0])
-    qkv_grad1 = reduce(attn_in, d_qkv, third, third, 512, forms[1])
-    input_rows, gain_one = dinput_call(perm, gains, x, dh1, d_qkv, qkv0, qkv1)
-    input_grad = from_chip(input_rows)
-
-    gain_rows = jnp.concatenate([gain_one, gain_two], axis=0)
-    if fast:
-        for bit in (1, 2, 4):
-            gain_rows = gain_rows + swap(gain_rows, bit)
-        mine = lax.dynamic_slice(gain_rows, (0, dp * LANE), (2, LANE))
-        mine = jnp.transpose(mine.reshape(2, ctx_count, part), (1, 0, 2))
-        gain_grads = jnp.sum(across(mine), axis=0)
-    else:
-        gain_grads = lax.psum_scatter(gain_rows, ("dp", "ctx"), scatter_dimension=1, tiled=True)
+    in_mine, in_other = split_back(in_got)
+    input_grad = join_back(in_mine, swap(in_other, 1))
+
     return (
         layer_out,
         input_grad,
         gain_grads[0],
-        jnp.concatenate([qkv_grad0, qkv_grad1], axis=1),
-        out_grad,
+        qkv_grad,
+        r_out.out,
         gain_grads[1],
-        jnp.concatenate([gate_grad[:, :hidden], up_grad[:, :hidden]], axis=1),
-        down_grad[:, :hidden],
+        jnp.concatenate([r_gate.out[:, :hidden], r_up.out[:, :hidden]], axis=1),
+        r_down.out[:, :hidden],
     )
 
 

time: 658 us -> 517 us (0.79)
  waiting for transfers between devices: 251 us -> 126 us
  starting transfers between devices: 113 us -> 68.7 us
  between operations: 2 us -> 15.5 us
  blocking collectives: 10.2 us -> 21.8 us
  Pallas kernels: 219 us -> 209 us
  local copies, waits for them, and re-layouts: 18.8 us -> 26.9 us
  other arithmetic: 33.9 us -> 41.1 us
    all_to_all x17 -> x6, waiting for transfers between devices: 113 us -> 28.8 us  [across(): return lax.all_to_all(v, 'ctx', split_axis=0, concat_axis=0, tiled=True)]
    ppermute x71, waiting for transfers between devices: 138 us -> 76.1 us  [swap(): return lax.ppermute(v, 'dp', [(i, i ^ bit) for i in range(dp_count)])]
    all_to_all x17 -> x6, starting transfers between devices: 71.6 us -> 25.2 us  [across(): return lax.all_to_all(v, 'ctx', split_axis=0, concat_axis=0, tiled=True)]
    all_gather x0 -> x1, blocking collectives: none -> 21.8 us  [gather_line(): return lax.all_gather(shard, 'ctx', axis=0, tiled=True)]
    reduce_scatter x0 -> x5, waiting for transfers between devices: none -> 16.9 us  [line(): lax.psum_scatter(self.three(), 'ctx', scatter_dimension=0, tiled=True)]
    pallas_call x16 -> x13, Pallas kernels: 158 us -> 142 us  [the longest x7 42.4 us: grad_call(): pl.pallas_call(functools.partial(grad_body, keep is not None, form), grid...]
    all_to_all x1 -> x0, blocking collectives: 10.2 us -> none  [across(): return lax.all_to_all(v, 'ctx', split_axis=0, concat_axis=0, tiled=True)]
    convert_element_type x12 -> x19, other arithmetic: 20.7 us -> 27.4 us  [the longest x7 13.1 us: three(): return did(total.astype(BF16))]
  transfers between devices with their start and end apart: 88 -> 83, of which waited for: 30 -> 29; matrix products, arithmetic and copies ran while one was open for 6% -> 10% of each run, Pallas kernels for 24% -> 36%
where the time goes in v2:
time: 517 us; the launch traced here: 509 us
  Pallas kernels  209 us (40%)
  waiting for transfers between devices  126 us (24%)
  starting transfers between devices  68.7 us (13%)
  other arithmetic  41.1 us (8%)
  local copies, waits for them, and re-layouts  26.9 us (5%)
  blocking collectives  21.8 us (4%)
  between operations  15.5 us (3%)
    ppermute x71, waiting for transfers between devices, swap(): return lax.ppermute(v, 'dp', [(i, i ^ bit) for i in range(dp_count)])  76.1 us
    ppermute x71, starting transfers between devices, swap(): return lax.ppermute(v, 'dp', [(i, i ^ bit) for i in range(dp_count)])  43.3 us
    pallas_call x7, Pallas kernels, grad_call(): pl.pallas_call(functools.partial(grad_body, keep is not None, form), grid...  42.4 us
    pallas_call x2, Pallas kernels, dattend_call(): pl.pallas_call(dattend_body, grid=(count,), out_shape=(sds((rows, count *...  36.4 us
    all_to_all x6, waiting for transfers between devices, across(): return lax.all_to_all(v, 'ctx', split_axis=0, concat_axis=0, tiled=True)  28.8 us
    pallas_call x2, Pallas kernels, attend_call(): pl.pallas_call(functools.partial(attend_body, len(given)), grid=(count,),...  28.3 us
    all_to_all x6, starting transfers between devices, across(): return lax.all_to_all(v, 'ctx', split_axis=0, concat_axis=0, tiled=True)  25.2 us
    all_gather x1, blocking collectives, gather_line(): return lax.all_gather(shard, 'ctx', axis=0, tiled=True)  21.8 us
  transfers between devices with their start and end apart: 83, of which 29 were waited for; matrix products, arithmetic and copies ran while one was open for 10% of the time, Pallas kernels for 36%

profile of v2, /device:TPU:0, one launch (start us, length us, event | category | flops | bytes accessed | tf_op | source)
XLA Modules:
  0.0 508.6 jit_solution(9716908397666446748)
XLA Ops:
  10.6 21.8 %all_gather.6 = bf16[128,3200]{1,0:T(8,128)(2,1)S(1)} all-gather(bf16[32,3200]{1,0:T(8,128)(2,1)S(1)} %concatenate.28), channel_id=1, replica_groups=mesh['dp'=8,'ctx'=4] {'ctx'}, dimensions={0}, use_global_device_ids=true | all-gather | bytes 1024000 | tf_op jit(solution)/shard_map/all_gather | solution.py:957
  36.8 9.7 %collective-permute-done.1.rest_10_ = bf16[128,1536]{1,0:T(8,128)(2,1)S(1)} collective-permute-done((bf16[128,1536]{1,0:T(8,128)(2,1)S(1)}, bf16[128,1536]{1,0:T(8,128)(2,1)S(1)}, u32[]{:S(2)}, u32[]{:S(2)}) %collective-permute-start.1) | collective-permute-done | bytes 393248 | tf_op jit(solution)/shard_map/ppermute | solution.py:887
  51.9 8.9 %collective-permute-done.4.rest_9_ = bf16[128,1536]{1,0:T(8,128)(2,1)} collective-permute-done((bf16[128,1536]{1,0:T(8,128)(2,1)S(1)}, bf16[128,1536]{1,0:T(8,128)(2,1)}, u32[]{:S(2)}, u32[]{:S(2)}) %collective-permute-start.4) | collective-permute-done | bytes 393248 | tf_op jit(solution)/shard_map/ppermute | solution.py:887
  83.5 17.0 %all-to-all-done = bf16[4,128,1024]{2,1,0:T(8,128)(2,1)S(1)} async-done(((bf16[4,128,1024]{2,1,0:T(8,128)(2,1)}), bf16[4,128,1024]{2,1,0:T(8,128)(2,1)S(1)}, u32[]{:S(2)}, u32[]{:S(2)}) %all-to-all-start) | async-done | bytes 1048608 | tf_op jit(solution)/shard_map/all_to_all | solution.py:893
  113.6 13.4 %qkv.1 = (bf16[512,1024]{1,0:T(8,128)(2,1)}, bf16[512,1024]{1,0:T(8,128)(2,1)}, bf16[512,2048]{1,0:T(8,128)(2,1)}, f32[8,1024]{1,0:T(8,128)}) custom-call(s32[8]{0:T(128)} %fusion.27.perm, bf16[512,1024]{1,0:T(8,128)(2,1)} %bitcast.162, f32[512,128]{1,0:T(8,128)} %get-tuple-element.284.cos_ref, f32[512,128]{1,0:T(8,128)} %get-tuple-element.285.sin_ref, ...), custom_call_target="tpu_custom_call" | custom-call | flops 1 | bytes 1 | tf_op jit(solution)/shard_map/qkv/pallas_call | solution.py:150
  150.2 14.1 %attend.2 = (bf16[512,1024]{1,0:T(8,128)(2,1)}, f32[8,8,512]{2,1,0:T(8,128)}) custom-call(s32[8]{0:T(128)} %fusion.27.perm, s32[1024,1]{1,0:T(8,128)} %copy.101.segk_ref, s32[1,512]{1,0:T(1,128)} %bitcast.179, bf16[512,1024]{1,0:T(8,128)(2,1)} %get-tuple-element.153.q_ref, bf16[512,2048]{1,0:T(8,128)(2,1)} %get-tuple-element.159.k0_ref.v0_ref, ...), custom_call_target="tpu_custom_call" | custom-call | flops 1 | bytes 1 | tf_op jit(solution)/shard_map/attend/pallas_call | solution.py:224
  164.4 14.2 %attend.3 = (bf16[512,1024]{1,0:T(8,128)(2,1)}, f32[8,8,512]{2,1,0:T(8,128)}) custom-call(s32[8]{0:T(128)} %fusion.27.perm, s32[1024,1]{1,0:T(8,128)} %copy.101.segk_ref, s32[1,512]{1,0:T(1,128)} %bitcast.180, bf16[512,1024]{1,0:T(8,128)(2,1)} %get-tuple-element.153.q_ref, ...), custom_call_target="tpu_custom_call", output_to_operand_aliasing={{0}: (8, {}), {1}: (9, {})} | custom-call | flops 1 | bytes 1 | tf_op jit(solution)/shard_map/attend/pallas_call | solution.py:224
  185.8 6.8 %middle.1 = (f32[512,1024]{1,0:T(8,128)}, bf16[512,1024]{1,0:T(8,128)(2,1)}) custom-call(s32[8]{0:T(128)} %fusion.27.perm, f32[8,1024]{1,0:T(8,128)} %get-tuple-element.165.gains_ref, bf16[512,1024]{1,0:T(8,128)(2,1)} %bitcast.163, f32[512,1]{1,0:T(8,128)} %copy.106.keep_ref.refs_2_, bf16[512,1024]{1,0:T(8,128)(2,1)} %get-tuple-element.184.o_ref.refs_0_, ...), custom_call_target="tpu_custom_call" | custom-call | flops 1 | bytes 1 | tf_op jit(solution)/shard_map/middle/pallas_call | solution.py:275
  192.7 15.2 %gate.1 = (bf16[512,2688]{1,0:T(8,128)(2,1)}, bf16[512,2688]{1,0:T(8,128)(2,1)}, bf16[512,2688]{1,0:T(8,128)(2,1)}) custom-call(s32[8]{0:T(128)} %fusion.27.perm, bf16[512,1024]{1,0:T(8,128)(2,1)} %get-tuple-element.182.b_ref.refs_0_, bf16[128,3712]{1,0:T(8,128)(2,1)} %copy-done.4, bf16[128,3712]{1,0:T(8,128)(2,1)} %copy-done.9, ...), custom_call_target="tpu_custom_call" | custom-call | flops 1 | bytes 1 | tf_op jit(solution)/shard_map/gate/pallas_call | solution.py:348
  214.9 11.2 %collective-permute-done.38.rest_3_ = bf16[128,2688]{1,0:T(8,128)(2,1)S(1)} collective-permute-done((bf16[128,2688]{1,0:T(8,128)(2,1)}, bf16[128,2688]{1,0:T(8,128)(2,1)S(1)}, u32[]{:S(2)}, u32[]{:S(2)}) %collective-permute-start.38) | collective-permute-done | bytes 688160 | tf_op jit(solution)/shard_map/ppermute | solution.py:887
  233.4 10.5 %dgate.1 = (bf16[512,2688]{1,0:T(8,128)(2,1)}, bf16[512,2688]{1,0:T(8,128)(2,1)}) custom-call(s32[8]{0:T(128)} %fusion.27.perm, bf16[512,1024]{1,0:T(8,128)(2,1)} %bitcast.166, f32[512,1]{1,0:T(8,128)} %copy.106.keep_ref.refs_2_, bf16[512,2688]{1,0:T(8,128)(2,1)} %get-tuple-element.186.f1_ref, bf16[512,2688]{1,0:T(8,128)(2,1)} %get-tuple-element.187.f2_ref, ...), custom_call_target="tpu_custom_call" | custom-call | flops 1 | bytes 1 | tf_op jit(solution)/shard_map/dgate/pallas_call | solution.py:409
  245.3 9.0 %grad_x.3 = (bf16[256,2688]{1,0:T(8,128)(2,1)}, bf16[256,2688]{1,0:T(8,128)(2,1)}) custom-call(s32[8]{0:T(128)} %fusion.27.perm, bf16[512,1024]{1,0:T(8,128)(2,1)} %bitcast.167, bf16[512,2688]{1,0:T(8,128)(2,1)} %get-tuple-element.180.refs_1_.m_ref, f32[512,1]{1,0:T(8,128)} %copy.106.keep_ref.refs_2_, bf16[512,1024]{1,0:T(8,128)(2,1)} %copy-done.47, ...), custom_call_target="tpu_custom_call" | custom-call | flops 1 | bytes 1 | tf_op jit(solution)/shard_map/grad_x/pallas_call | solution.py:849
  255.8 7.7 %grad_y.4 = (bf16[256,2688]{1,0:T(8,128)(2,1)}, bf16[256,2688]{1,0:T(8,128)(2,1)}) custom-call(s32[8]{0:T(128)} %fusion.27.perm, bf16[512,1024]{1,0:T(8,128)(2,1)} %get-tuple-element.182.b_ref.refs_0_, bf16[512,2688]{1,0:T(8,128)(2,1)} %get-tuple-element.193.refs_1_.dg_ref, bf16[512,1024]{1,0:T(8,128)(2,1)} %copy-done.15, ...), custom_call_target="tpu_custom_call" | custom-call | flops 1 | bytes 1 | tf_op jit(solution)/shard_map/grad_y/pallas_call | solution.py:849
  266.6 7.7 %grad_x.4 = (bf16[256,2688]{1,0:T(8,128)(2,1)}, bf16[256,2688]{1,0:T(8,128)(2,1)}) custom-call(s32[8]{0:T(128)} %fusion.27.perm, bf16[512,1024]{1,0:T(8,128)(2,1)} %get-tuple-element.182.b_ref.refs_0_, bf16[512,2688]{1,0:T(8,128)(2,1)} %get-tuple-element.199.refs_1_.du_ref, bf16[512,1024]{1,0:T(8,128)(2,1)} %copy-done.15, bf16[512,2688]{1,0:T(8,128)(2,1)} %copy-done.19), custom_call_target="tpu_custom_call" | custom-call | flops 1 | bytes 1 | tf_op jit(solution)/shard_map/grad_x/pallas_call | solution.py:849
  274.3 19.5 %dmiddle.1 = (f32[512,1024]{1,0:T(8,128)}, bf16[512,1024]{1,0:T(8,128)(2,1)}, bf16[512,1024]{1,0:T(8,128)(2,1)}, f32[1,1024]{1,0:T(1,128)}) custom-call(s32[8]{0:T(128)} %fusion.27.perm, f32[8,1024]{1,0:T(8,128)} %get-tuple-element.165.gains_ref, bf16[512,1024]{1,0:T(8,128)(2,1)} %bitcast.168, f32[512,1]{1,0:T(8,128)} %copy.106.keep_ref.refs_2_, ...), custom_call_target="tpu_custom_call" | custom-call | flops 1 | bytes 1 | tf_op jit(solution)/shard_map/dmiddle/pallas_call | solution.py:566
  294.4 9.4 %down.1 = bf16[512,1024]{1,0:T(8,128)(2,1)} custom-call(s32[8]{0:T(128)} %fusion.27.perm, f32[512,1024]{1,0:T(8,128)} %get-tuple-element.176.h1_ref, f32[512,1]{1,0:T(8,128)} %copy.106.keep_ref.refs_2_, bf16[512,2688]{1,0:T(8,128)(2,1)} %get-tuple-element.180.refs_1_.m_ref, bf16[128,2688]{1,0:T(8,128)(2,1)} %bitcast.14.rest_0_, ...), custom_call_target="tpu_custom_call" | custom-call | flops 1 | bytes 1 | tf_op jit(solution)/shard_map/down/pallas_call | solution.py:471
  319.5 18.2 %dattend.2 = (bf16[512,512]{1,0:T(8,128)(2,1)}, f32[512,512]{1,0:T(8,128)}, f32[512,512]{1,0:T(8,128)}, bf16[512,512]{1,0:T(8,128)(2,1)}, bf16[512,512]{1,0:T(8,128)(2,1)}) custom-call(s32[8]{0:T(128)} %fusion.27.perm, s32[1024,1]{1,0:T(8,128)} %copy.101.segk_ref, s32[1,512]{1,0:T(1,128)} %bitcast.181, bf16[512,1024]{1,0:T(8,128)(2,1)} %get-tuple-element.153.q_ref, ...), custom_call_target="tpu_custom_call" | custom-call | flops 1 | bytes 1 | tf_op jit(solution)/shard_map/dattend/pallas_call | solution.py:654
  345.6 6.5 %dqkv.2.refs_1_.da_ref = bf16[512,1536]{1,0:T(8,128)(2,1)} custom-call(s32[8]{0:T(128)} %fusion.27.perm, f32[512,128]{1,0:T(8,128)} %get-tuple-element.284.cos_ref, f32[512,128]{1,0:T(8,128)} %get-tuple-element.285.sin_ref, bf16[512,512]{1,0:T(8,128)(2,1)} %get-tuple-element.215.dq_ref, f32[512,512]{1,0:T(8,128)} %get-tuple-element.219.dk0_ref, ...), custom_call_target="tpu_custom_call" | custom-call | flops 1 | bytes 1 | tf_op jit(solution)/shard_map/dqkv/pallas_call | solution.py:704
  357.1 18.3 %dattend.3 = (bf16[512,512]{1,0:T(8,128)(2,1)}, f32[512,512]{1,0:T(8,128)}, f32[512,512]{1,0:T(8,128)}, bf16[512,512]{1,0:T(8,128)(2,1)}, bf16[512,512]{1,0:T(8,128)(2,1)}) custom-call(s32[8]{0:T(128)} %fusion.27.perm, s32[1024,1]{1,0:T(8,128)} %copy.101.segk_ref, s32[1,512]{1,0:T(1,128)} %bitcast.182, bf16[512,1024]{1,0:T(8,128)(2,1)} %get-tuple-element.153.q_ref, ...), custom_call_target="tpu_custom_call" | custom-call | flops 1 | bytes 1 | tf_op jit(solution)/shard_map/dattend/pallas_call | solution.py:654
  388.9 6.6 %dqkv.3.db_ref.refs_1_ = bf16[512,1536]{1,0:T(8,128)(2,1)} custom-call(s32[8]{0:T(128)} %fusion.27.perm, f32[512,128]{1,0:T(8,128)} %get-tuple-element.284.cos_ref, f32[512,128]{1,0:T(8,128)} %get-tuple-element.285.sin_ref, bf16[512,512]{1,0:T(8,128)(2,1)} %get-tuple-element.229.dq_ref, f32[512,512]{1,0:T(8,128)} %get-tuple-element.235.dk0_ref, ...), custom_call_target="tpu_custom_call" | custom-call | flops 1 | bytes 1 | tf_op jit(solution)/shard_map/dqkv/pallas_call | solution.py:704
  403.0 13.8 %dinput.1 = (bf16[512,1024]{1,0:T(8,128)(2,1)}, f32[1,1024]{1,0:T(1,128)}) custom-call(s32[8]{0:T(128)} %fusion.27.perm, f32[8,1024]{1,0:T(8,128)} %get-tuple-element.165.gains_ref, bf16[512,1024]{1,0:T(8,128)(2,1)} %bitcast.164, f32[512,1024]{1,0:T(8,128)} %get-tuple-element.202.dh1_ref, bf16[512,1536]{1,0:T(8,128)(2,1)} %dqkv.2.refs_1_.da_ref, ...), custom_call_target="tpu_custom_call" | custom-call | flops 1 | bytes 1 | tf_op jit(solution)/shard_map/dinput/pallas_call | solution.py:775
  437.9 11.6 %all-to-all-done.4 = bf16[4,128,1024]{2,1,0:T(8,128)(2,1)} async-done(((bf16[4,128,1024]{2,1,0:T(8,128)(2,1)}), bf16[4,128,1024]{2,1,0:T(8,128)(2,1)}, u32[]{:S(2)}, u32[]{:S(2)}) %all-to-all-start.4) | async-done | bytes 1048608 | tf_op jit(solution)/shard_map/all_to_all | solution.py:893
  456.1 9.4 %collective-permute-done.70 = f32[2,1024]{0,1:T(8,128)} collective-permute-done((f32[2,1024]{0,1:T(8,128)S(1)}, f32[2,1024]{0,1:T(8,128)}, u32[]{:S(2)}, u32[]{:S(2)}) %collective-permute-start.70) | collective-permute-done | bytes 8224 | tf_op jit(solution)/shard_map/ppermute | solution.py:887
  486.3 12.6 %reduce-scatter.10.cloned.1.call-done = bf16[32,1536]{1,0:T(8,128)(2,1)} async-done(((bf16[128,1536]{1,0:T(8,128)(2,1)}), bf16[32,1536]{1,0:T(8,128)(2,1)}) %reduce-scatter.10.cloned.1.call-update) | async-done | bytes 98320 | tf_op jit(solution)/shard_map/reduce_scatter | solution.py:1087
  (381 shorter events, 200.2 us)
Async XLA Ops:
  7.2 63.9 %all-gather.2.cloned.1.call-start = ((), (), s32[]{:S(2)}) async-start(), calls=%async_computation.11 | async-start | bytes 2048000 | tf_op jit(solution)/shard_map/all_gather | solution.py:957
  139.0 42.7 %all-to-all-start.2 = ((bf16[4,128,1024]{2,1,0:T(8,128)(2,1)}), bf16[4,128,1024]{2,1,0:T(8,128)(2,1)S(1)}, u32[]{:S(2)}, u32[]{:S(2)}) async-start(bf16[4,128,1024]{2,1,0:T(8,128)(2,1)} %bitcast.21), calls=%async_computation.2 | async-start | bytes 2097152 | tf_op jit(solution)/shard_map/all_to_all | solution.py:893
  144.0 34.6 %collective-permute-start.22 = (bf16[128,3712]{1,0:T(8,128)(2,1)S(1)}, bf16[128,3712]{1,0:T(8,128)(2,1)S(1)}, u32[]{:S(2)}, u32[]{:S(2)}) collective-permute-start(bf16[128,3712]{1,0:T(8,128)(2,1)S(1)} %collective-permute-done.10.rest_1_), channel_id=1, source_target_pairs={{0,16},{4,20},{8,24},{12,28},{16,0},{20,4},{24,8},{28,12},{1,17},{... | collective-permute-start | bytes 2850824 | tf_op jit(solution)/shard_map/ppermute | solution.py:887
  146.5 32.1 %collective-permute-start.23 = (bf16[128,2688]{1,0:T(8,128)(2,1)}, bf16[128,2688]{1,0:T(8,128)(2,1)}, u32[]{:S(2)}, u32[]{:S(2)}) collective-permute-start(bf16[128,2688]{1,0:T(8,128)(2,1)} %collective-permute-done.11.rest_10_), channel_id=1, source_target_pairs={{0,8},{4,12},{8,0},{12,4},{16,24},{20,28},{24,16},{28,20},{1,9},{5... | collective-permute-start | bytes 2064392 | tf_op jit(solution)/shard_map/ppermute | solution.py:887
  148.6 33.1 %collective-permute-start.25 = (bf16[128,2688]{1,0:T(8,128)(2,1)}, bf16[128,2688]{1,0:T(8,128)(2,1)}, u32[]{:S(2)}, u32[]{:S(2)}) collective-permute-start(bf16[128,2688]{1,0:T(8,128)(2,1)} %bitcast.14.rest_0_), channel_id=1, source_target_pairs={{0,16},{4,20},{8,24},{12,28},{16,0},{20,4},{24,8},{28,12},{1,17},{... | collective-permute-start | bytes 2064392 | tf_op jit(solution)/shard_map/ppermute | solution.py:887
  149.1 32.6 %collective-permute-start.30 = (bf16[128,2688]{1,0:T(8,128)(2,1)}, bf16[128,2688]{1,0:T(8,128)(2,1)}, u32[]{:S(2)}, u32[]{:S(2)}) collective-permute-start(bf16[128,2688]{1,0:T(8,128)(2,1)} %collective-permute-done.18.rest_9_), channel_id=1, source_target_pairs={{0,4},{4,0},{8,12},{12,8},{16,20},{20,16},{24,28},{28,24},{1,5},{5... | collective-permute-start | bytes 2064392 | tf_op jit(solution)/shard_map/ppermute | solution.py:887
  254.3 49.5 %collective-permute-start.46 = (bf16[256,2688]{1,0:T(8,128)(2,1)}, bf16[256,2688]{1,0:T(8,128)(2,1)S(1)}, u32[]{:S(2)}, u32[]{:S(2)}) collective-permute-start(bf16[256,2688]{1,0:T(8,128)(2,1)} %get-tuple-element.195), channel_id=1, source_target_pairs={{0,8},{4,12},{8,0},{12,4},{16,24},{20,28},{24,16},{28,20},{1,9},{5... | collective-permute-start | bytes 4128776 | tf_op jit(solution)/shard_map/ppermute | solution.py:887
  263.5 52.4 %collective-permute-start.45 = (bf16[256,2688]{1,0:T(8,128)(2,1)}, bf16[256,2688]{1,0:T(8,128)(2,1)}, u32[]{:S(2)}, u32[]{:S(2)}) collective-permute-start(bf16[256,2688]{1,0:T(8,128)(2,1)} %get-tuple-element.197), channel_id=1, source_target_pairs={{0,16},{4,20},{8,24},{12,28},{16,0},{20,4},{24,8},{28,12},{1,17},{... | collective-permute-start | bytes 4128776 | tf_op jit(solution)/shard_map/ppermute | solution.py:887
  293.8 43.9 %collective-permute-start.50 = (bf16[256,2688]{1,0:T(8,128)(2,1)}, bf16[256,2688]{1,0:T(8,128)(2,1)S(1)}, u32[]{:S(2)}, u32[]{:S(2)}) collective-permute-start(bf16[256,2688]{1,0:T(8,128)(2,1)} %get-tuple-element.200), channel_id=1, source_target_pairs={{0,8},{4,12},{8,0},{12,4},{16,24},{20,28},{24,16},{28,20},{1,9},{5... | collective-permute-start | bytes 4128776 | tf_op jit(solution)/shard_map/ppermute | solution.py:887
  305.2 32.8 %collective-permute-start.49 = (bf16[128,2688]{1,0:T(8,128)(2,1)}, bf16[128,2688]{1,0:T(8,128)(2,1)}, u32[]{:S(2)}, u32[]{:S(2)}) collective-permute-start(bf16[128,2688]{1,0:T(8,128)(2,1)} %add_convert_fusion.5), channel_id=1, source_target_pairs={{0,16},{4,20},{8,24},{12,28},{16,0},{20,4},{24,8},{28,12},{1,17},{... | collective-permute-start | bytes 2064392 | tf_op jit(solution)/shard_map/ppermute | solution.py:887
  305.7 46.4 %all-to-all-start.3 = ((bf16[4,128,1024]{2,1,0:T(8,128)(2,1)}), bf16[4,128,1024]{2,1,0:T(8,128)(2,1)S(1)}, u32[]{:S(2)}, u32[]{:S(2)}) async-start(bf16[4,128,1024]{2,1,0:T(8,128)(2,1)} %bitcast.24), calls=%async_computation.3 | async-start | bytes 2097152 | tf_op jit(solution)/shard_map/all_to_all | solution.py:893
  310.5 64.9 %reduce-scatter.6.cloned.1.call-start = ((), (), s32[]{:S(2)}) async-start(), calls=%async_computation.12 | async-start | bytes 860160 | tf_op jit(solution)/shard_map/reduce_scatter | solution.py:1087
  318.0 34.2 %collective-permute-start.48 = (bf16[128,2688]{1,0:T(8,128)(2,1)}, bf16[128,2688]{1,0:T(8,128)(2,1)}, u32[]{:S(2)}, u32[]{:S(2)}) collective-permute-start(bf16[128,2688]{1,0:T(8,128)(2,1)} %add_convert_fusion.4), channel_id=1, source_target_pairs={{0,8},{4,12},{8,0},{12,4},{16,24},{20,28},{24,16},{28,20},{1,9},{5... | collective-permute-start | bytes 2064392 | tf_op jit(solution)/shard_map/ppermute | solution.py:887
  341.8 47.1 %reduce-scatter.8.cloned.1.call-start = ((), (), s32[]{:S(2)}) async-start(), calls=%async_computation.13 | async-start | bytes 860160 | tf_op jit(solution)/shard_map/reduce_scatter | solution.py:1087
  354.9 70.2 %reduce-scatter.14.cloned.1.call-start = ((), (), s32[]{:S(2)}) async-start(), calls=%async_computation.16 | async-start | bytes 860160 | tf_op jit(solution)/shard_map/reduce_scatter | solution.py:1087
  356.6 38.9 %collective-permute-start.55 = (bf16[128,2688]{1,0:T(8,128)(2,1)S(1)}, bf16[128,2688]{1,0:T(8,128)(2,1)}, u32[]{:S(2)}, u32[]{:S(2)}) collective-permute-start(bf16[128,2688]{1,0:T(8,128)(2,1)S(1)} %add_convert_fusion.3), channel_id=1, source_target_pairs={{0,16},{4,20},{8,24},{12,28},{16,0},{20,4},{24,8},{28,12},{1,17},{... | collective-permute-start | bytes 2064392 | tf_op jit(solution)/shard_map/ppermute | solution.py:887
  400.0 51.0 %collective-permute-start.65 = (bf16[256,1536]{1,0:T(8,128)(2,1)}, bf16[256,1536]{1,0:T(8,128)(2,1)}, u32[]{:S(2)}, u32[]{:S(2)}) collective-permute-start(bf16[256,1536]{1,0:T(8,128)(2,1)} %get-tuple-element.232), channel_id=1, source_target_pairs={{0,16},{4,20},{8,24},{12,28},{16,0},{20,4},{24,8},{28,12},{1,17},{... | collective-permute-start | bytes 2359304 | tf_op jit(solution)/shard_map/ppermute | solution.py:887
  401.3 52.3 %collective-permute-start.62 = (bf16[128,1024]{1,0:T(8,128)(2,1)}, bf16[128,1024]{1,0:T(8,128)(2,1)}, u32[]{:S(2)}, u32[]{:S(2)}) collective-permute-start(bf16[128,1024]{1,0:T(8,128)(2,1)} %add_convert_fusion.9), channel_id=1, source_target_pairs={{0,8},{4,12},{8,0},{12,4},{16,24},{20,28},{24,16},{28,20},{1,9},{5... | collective-permute-start | bytes 786440 | tf_op jit(solution)/shard_map/ppermute | solution.py:887
  418.5 31.0 %all-to-all-start.4 = ((bf16[4,128,1024]{2,1,0:T(8,128)(2,1)}), bf16[4,128,1024]{2,1,0:T(8,128)(2,1)}, u32[]{:S(2)}, u32[]{:S(2)}) async-start(bf16[4,128,1024]{2,1,0:T(8,128)(2,1)} %bitcast.176), calls=%async_computation.6 | async-start | bytes 2097152 | tf_op jit(solution)/shard_map/all_to_all | solution.py:893
  422.8 62.0 %reduce-scatter.12.cloned.1.call-start = ((), (), s32[]{:S(2)}) async-start(), calls=%async_computation.15 | async-start | bytes 327680 | tf_op jit(solution)/shard_map/reduce_scatter | solution.py:1087
  431.7 34.6 %collective-permute-start.61 = (bf16[256,768]{1,0:T(8,128)(2,1)}, bf16[256,768]{1,0:T(8,128)(2,1)}, u32[]{:S(2)}, u32[]{:S(2)}) collective-permute-start(bf16[256,768]{1,0:T(8,128)(2,1)} %get-tuple-element.243), channel_id=1, source_target_pairs={{0,8},{4,12},{8,0},{12,4},{16,24},{20,28},{24,16},{28,20},{1,9},{5... | collective-permute-start | bytes 1179656 | tf_op jit(solution)/shard_map/ppermute | solution.py:887
  437.2 31.5 %collective-permute-start.68 = (bf16[256,768]{1,0:T(8,128)(2,1)}, bf16[256,768]{1,0:T(8,128)(2,1)}, u32[]{:S(2)}, u32[]{:S(2)}) collective-permute-start(bf16[256,768]{1,0:T(8,128)(2,1)} %get-tuple-element.249), channel_id=1, source_target_pairs={{0,16},{4,20},{8,24},{12,28},{16,0},{20,4},{24,8},{28,12},{1,17},{... | collective-permute-start | bytes 1179656 | tf_op jit(solution)/shard_map/ppermute | solution.py:887
  450.8 31.5 %collective-permute-start.59 = (bf16[2,128,1024]{2,1,0:T(8,128)(2,1)S(1)}, bf16[2,128,1024]{2,1,0:T(8,128)(2,1)S(1)}, u32[]{:S(2)}, u32[]{:S(2)}) collective-permute-start(bf16[2,128,1024]{2,1,0:T(8,128)(2,1)S(1)} %select_bitcast_fusion), channel_id=1, source_target_pairs={{0,4},{4,0},{8,12},{12,8},{16,20},{20,16},{24,28},{28,24},{1,5},{5... | collective-permute-start | bytes 1572872 | tf_op jit(solution)/shard_map/ppermute | solution.py:887
  456.0 42.8 %reduce-scatter.10.cloned.1.call-start = ((), (), s32[]{:S(2)}) async-start(), calls=%async_computation.14 | async-start | bytes 491520 | tf_op jit(solution)/shard_map/reduce_scatter | solution.py:1087
  (124 other events, 1495.6 us)
Sparse Core Ops, SparseCore 0:
  33.5 37.4 all-gather.1
  341.9 23.0 reduce-scatter.5
  367.4 21.4 reduce-scatter.7
  397.9 21.3 reduce-scatter.13
  456.2 18.4 reduce-scatter.11
  477.4 21.3 reduce-scatter.9

commit v3 on v2

v3 whole, which is shorter than its diff:
```python
import functools
import math

import jax
import jax.numpy as jnp
from jax import lax
from jax.experimental import pallas as pl
from jax.experimental.pallas import tpu as pltpu
from jax.sharding import PartitionSpec as P

HEADS = 16
HEAD = 64
LANE = 128

epsilon = 1e-05
rope_base = 160000.0
NEG = -1e30
LOG2E = math.log2(math.e)

COST = pl.CostEstimate(flops=1, transcendentals=0, bytes_accessed=1)
F32 = jnp.float32
BF16 = jnp.bfloat16
ANY = pl.BlockSpec(memory_space=pl.ANY)
SMEM = pl.BlockSpec(memory_space=pltpu.SMEM)


def params(*, mib=56):
    return pltpu.CompilerParams(vmem_limit_bytes=mib << 20)


def sds(shape, dtype):
    return jax.ShapeDtypeStruct(shape, dtype)


def nt(a, b):
    return lax.dot_general(a, b, (((1,), (1,)), ((), ())), preferred_element_type=F32)


def nn(a, b):
    return lax.dot_general(a, b, (((1,), (0,)), ((), ())), preferred_element_type=F32)


def lanes(perm, m):
    return pl.ds(pl.multiple_of(perm[m] * LANE, LANE), LANE)


def tn(a, b):
    return lax.dot_general(a, b, (((0,), (0,)), ((), ())), preferred_element_type=F32)


def chunks(count, size=1024):
    return [(c, min(size, count - c)) for c in range(0, count, size)]


class Copies:
    def __init__(self, sems):
        self.sems, self.used = sems, 0

    def start(self, source, target):
        copy = pltpu.make_async_copy(source, target, self.sems.at[self.used])
        self.used += 1
        copy.start()
        return [copy]

    def weight(self, pieces, col, count, target, to=None):
        out = []
        to = col if to is None else to
        for m, piece in enumerate(pieces):
            rows = piece.shape[0]
            out += self.start(piece.at[:, col : col + count], target.at[m * rows : (m + 1) * rows, to : to + count])
        return out


def wait(copies):
    for c in copies:
        c.wait()


def row_tiles(rows, tile, body):
    def step(i, carry):
        body(pl.ds(pl.multiple_of(i * tile, tile), tile))
        return carry

    lax.fori_loop(0, rows // tile, step, 0)


def call(body, perm, small, big, outs, scratch, copies, name):
    return pl.pallas_call(
        body,
        out_shape=tuple(outs),
        in_specs=[SMEM] + [pl.BlockSpec(memory_space=pltpu.VMEM)] * len(small) + [ANY] * len(big),
        out_specs=(ANY,) * len(outs),
        scratch_shapes=[*scratch, pltpu.SemaphoreType.DMA((copies,))],
        compiler_params=params(),
        cost_estimate=COST,
        name=name,
    )(perm, *small, *big)


def norm_rows(v):
    centered = v - jnp.mean(v, axis=-1, keepdims=True)
    inv = lax.rsqrt(jnp.mean(centered * centered, axis=-1, keepdims=True) + epsilon)
    return centered * inv, inv


def turn(u, cos, sin):
    first = lax.broadcasted_iota(jnp.int32, (1, LANE), 1) % HEAD < HEAD // 2
    out = []
    for h in range(u.shape[1] // LANE):
        b = u[:, h * LANE : (h + 1) * LANE]
        t = jnp.where(first, pltpu.roll(b, LANE - HEAD // 2, 1), pltpu.roll(b, HEAD // 2, 1))
        out.append(b * cos + t * sin)
    return jnp.concatenate(out, axis=1)


def qkv_body(n, perm, cos_ref, sin_ref, x_hbm, *rest):
    p0, p1 = rest[:n], rest[n : 2 * n]
    a_hbm, q_hbm, kv_hbm, gains_hbm, x, w, g, gains, a, ap, out, sems = rest[2 * n :]
    move = Copies(sems)
    rows, width = x.shape
    half = width // 2
    got_x = move.start(x_hbm, x)
    got_gains = move.weight(p0, 3 * half, LANE, g, 0)
    got = [move.weight(p, c * half, half, w, (3 * i + c) * half) for i, p in enumerate((p0, p1)) for c in range(3)]
    wait(got_gains)
    for m in range(width // LANE):
        gains[:, lanes(perm, m)] = g[m * LANE : (m + 1) * LANE, :].astype(F32).T[0:8, :]
    done = move.start(gains, gains_hbm)
    wait(got_x)

    def normalize(r):
        normed, _ = norm_rows(x[r, :].astype(F32))
        a[r, :] = (normed * gains[0:1, :]).astype(BF16)

    row_tiles(rows, LANE, normalize)
    done += move.start(a, a_hbm)
    for m in range(width // LANE):
        ap[:, m * LANE : (m + 1) * LANE] = a[:, lanes(perm, m)]
    for c in range(6):
        cols = slice(c * half, (c + 1) * half)
        kind, part = c % 3, c // 3
        wait(got[c])

        def project(r, cols=cols, kind=kind):
            u = nn(ap[r, :], w[:, cols])
            if kind < 2:
                u = turn(u, cos_ref[r, :], sin_ref[r, :])
            out[r, cols] = u.astype(BF16)

        row_tiles(rows, 256, project)
        if kind == 0:
            done += move.start(out.at[:, cols], q_hbm.at[:, part * half : (part + 1) * half])
        else:
            to = (kind - 1) * width + part * half
            done += move.start(out.at[:, cols], kv_hbm.at[:, to : to + half])
    wait(done)


def qkv_call(perm, x, cos, sin, p0, p1):
    rows, width = x.shape
    return call(
        functools.partial(qkv_body, len(p0)),
        perm,
        [cos, sin],
        [x, *p0, *p1],
        [sds((rows, width), BF16), sds((rows, width), BF16), sds((rows, 2 * width), BF16), sds((8, width), F32)],
        [
            pltpu.VMEM((rows, width), BF16),
            pltpu.VMEM((width, 3 * width), BF16),
            pltpu.VMEM((width, LANE), BF16),
            pltpu.VMEM((8, width), F32),
            pltpu.VMEM((rows, width), BF16),
            pltpu.VMEM((rows, width), BF16),
            pltpu.VMEM((rows, 3 * width), BF16),
        ],
        9 + 7 * len(p0),
        "qkv",
    )


def attend_body(given, perm, segk_ref, segq_ref, q_ref, k0_ref, k1_ref, v0_ref, v1_ref, *rest):
    o_ref, lse_ref, bias, vt = rest[given:]
    j = pl.program_id(0)
    rows = q_ref.shape[0]
    tile = 256

    @pl.when(j == 0)
    def _():
        bias[...] = jnp.where(segk_ref[...] == segq_ref[...], 0.0, NEG)

    for i in range(rows // LANE):
        r = slice(i * LANE, (i + 1) * LANE)
        vt[:, r] = v0_ref[r, :].astype(F32).T.astype(BF16)
        vt[:, rows + i * LANE : rows + (i + 1) * LANE] = v1_ref[r, :].astype(F32).T.astype(BF16)
    head_of = lax.broadcasted_iota(jnp.int32, (1, LANE), 1) // HEAD
    scale = LOG2E / math.sqrt(HEAD)
    for t in range(rows // tile):
        cols = slice(t * tile, (t + 1) * tile)
        q = q_ref[cols, :]
        parts = []
        for h in range(LANE // HEAD):
            qm = jnp.where(head_of == h, q, jnp.zeros_like(q))
            s = jnp.concatenate([nt(k0_ref[...], qm), nt(k1_ref[...], qm)], axis=0) * scale + bias[:, cols]
            top = jnp.max(s, axis=0, keepdims=True)
            e = jnp.exp2(s - top)
            total = jnp.sum(e, axis=0, keepdims=True)
            p = (e * (1.0 / total)).astype(BF16)
            ot = nn(vt[...], p)
            parts.append(ot[h * HEAD : (h + 1) * HEAD, :])
            lse_ref[0, h : h + 1, cols] = top + jnp.log2(total)
        o_ref[cols, :] = jnp.concatenate(parts, axis=0).T.astype(BF16)


def attend_call(perm, segk, segq, q, kv0, kv1, first, count, given=()):
    rows, width = q.shape
    pairs = width // LANE
    full = lambda j: (0, 0)
    at = lambda j: (0, first + j)
    vat = lambda j: (0, pairs + first + j)
    block = (rows, LANE)
    return pl.pallas_call(
        functools.partial(attend_body, len(given)),
        grid=(count,),
        out_shape=(sds((rows, width), BF16), sds((pairs, 8, rows), F32)),
        in_specs=[
            SMEM,
            pl.BlockSpec((2 * rows, 1), full),
            pl.BlockSpec((1, rows), full),
            pl.BlockSpec(block, at),
            pl.BlockSpec(block, at),
            pl.BlockSpec(block, at),
            pl.BlockSpec(block, vat),
            pl.BlockSpec(block, vat),
        ]
        + [ANY] * len(given),
        out_specs=(pl.BlockSpec(block, at), pl.BlockSpec((1, 8, rows), lambda j: (first + j, 0, 0))),
        scratch_shapes=[pltpu.VMEM((2 * rows, rows), F32), pltpu.VMEM((LANE, 2 * rows), BF16)],
        input_output_aliases={8 + i: i for i in range(len(given))},
        compiler_params=params(),
        cost_estimate=COST,
        name="attend",
    )(perm, segk, segq, q, kv0, kv1, kv0, kv1, *given)


def middle_body(n, perm, gains_ref, keep_ref, x_hbm, o_hbm, *rest):
    pieces = rest[:n]
    h1_hbm, b_hbm, x, o, op, w, h1, b, sems = rest[n:]
    move = Copies(sems)
    rows, width = x.shape
    got = move.start(o_hbm, o) + move.weight(pieces, 0, width, w) + move.start(x_hbm, x)
    wait(got[:1])
    for m in range(width // LANE):
        op[:, m * LANE : (m + 1) * LANE] = o[:, lanes(perm, m)]
    wait(got[1:])
    done = []
    for t in range(2):
        base = t * (rows // 2)

        def tile(i, carry, base=base):
            r = pl.ds(pl.multiple_of(base + i * LANE, LANE), LANE)
            v = x[r, :].astype(F32) + keep_ref[r, :] * nn(op[r, :], w[...])
            h1[r, :] = v
            normed, _ = norm_rows(v)
            b[r, :] = (normed * gains_ref[1:2, :]).astype(BF16)
            return carry

        lax.fori_loop(0, rows // 2 // LANE, tile, 0)
        part = slice(base, base + rows // 2)
        done += move.start(b.at[part, :], b_hbm.at[part, :]) + move.start(h1.at[part, :], h1_hbm.at[part, :])
    wait(done)


def middle_call(perm, gains, x, keep, o, pieces):
    rows, width = x.shape
    return call(
        functools.partial(middle_body, len(pieces)),
        perm,
        [gains, keep],
        [x, o, *pieces],
        [sds((rows, width), F32), sds((rows, width), BF16)],
        [
            pltpu.VMEM((rows, width), BF16),
            pltpu.VMEM((rows, width), BF16),
            pltpu.VMEM((rows, width), BF16),
            pltpu.VMEM((width, width), BF16),
            pltpu.VMEM((rows, width), F32),
            pltpu.VMEM((rows, width), BF16),
        ],
        6 + len(pieces),
        "middle",
    )


def gate_body(n, base, perm, b_hbm, *rest):
    pa, pb = rest[:n], rest[n : 2 * n]
    m_hbm, f1_hbm, f2_hbm, b, bp, wg, wu, mv, f1, f2, sems = rest[2 * n :]
    move = Copies(sems)
    rows, width = b.shape
    parts = chunks(mv.shape[1])
    got_b = move.start(b_hbm, b)
    got = [move.weight(pa, base + c, k, wg, c) + move.weight(pb, c, k, wu) for c, k in parts]
    wait(got_b)
    for m in range(width // LANE):
        bp[:, m * LANE : (m + 1) * LANE] = b[:, lanes(perm, m)]
    done = []
    for (c, k), g in zip(parts, got):
        cols = slice(c, c + k)
        wait(g)

        def tile(r, cols=cols):
            gate = nn(bp[r, :], wg[:, cols])
            up = nn(bp[r, :], wu[:, cols])
            cdf = 0.5 * (1.0 + lax.erf(gate * (1.0 / math.sqrt(2.0))))
            density = jnp.exp(-0.5 * gate * gate) * (1.0 / math.sqrt(2.0 * math.pi))
            act = gate * cdf
            mv[r, cols] = (act * up).astype(BF16)
            f1[r, cols] = (up * (cdf + gate * density)).astype(BF16)
            f2[r, cols] = act.astype(BF16)

        row_tiles(rows, LANE, tile)
        for v, to in ((mv, m_hbm), (f1, f1_hbm), (f2, f2_hbm)):
            done += move.start(v.at[:, cols], to.at[:, cols])
    wait(done)


def gate_call(perm, b, pa, pb, hidden, base):
    rows, width = b.shape
    return call(
        functools.partial(gate_body, len(pa), base),
        perm,
        [],
        [b, *pa, *pb],
        [sds((rows, hidden), BF16)] * 3,
        [pltpu.VMEM((rows, width), BF16)] * 2 + [pltpu.VMEM((width, hidden), BF16)] * 2 + [pltpu.VMEM((rows, hidden), BF16)] * 3,
        1 + len(chunks(hidden)) * (2 * len(pa) + 3),
        "gate",
    )


def dgate_body(n, perm, keep_ref, cot_hbm, f1_hbm, f2_hbm, *rest):
    pd = rest[:n]
    dg_hbm, du_hbm, cot, ep, wd, f1, f2, sems = rest[n:]
    move = Copies(sems)
    rows, width = cot.shape
    parts = chunks(f1.shape[1])
    got_cot = move.start(cot_hbm, cot)
    got = []
    for c, k in parts:
        cols = slice(c, c + k)
        got.append(
            move.weight(pd, c, k, wd)
            + move.start(f1_hbm.at[:, cols], f1.at[:, cols])
            + move.start(f2_hbm.at[:, cols], f2.at[:, cols])
        )
    wait(got_cot)
    for m in range(width // LANE):
        ep[:, m * LANE : (m + 1) * LANE] = (keep_ref[...] * cot[:, lanes(perm, m)].astype(F32)).astype(BF16)
    done = []
    for (c, k), g in zip(parts, got):
        cols = slice(c, c + k)
        wait(g)

        def tile(r, cols=cols):
            dm = nn(ep[r, :], wd[:, cols])
            f1[r, cols] = (dm * f1[r, cols].astype(F32)).astype(BF16)
            f2[r, cols] = (dm * f2[r, cols].astype(F32)).astype(BF16)

        row_tiles(rows, 256, tile)
        done += move.start(f1.at[:, cols], dg_hbm.at[:, cols]) + move.start(f2.at[:, cols], du_hbm.at[:, cols])
    wait(done)


def dgate_call(perm, cot, keep, f1, f2, pd):
    rows, width = cot.shape
    hidden = f1.shape[1]
    return call(
        functools.partial(dgate_body, len(pd)),
        perm,
        [keep],
        [cot, f1, f2, *pd],
        [sds((rows, hidden), BF16)] * 2,
        [pltpu.VMEM((rows, width), BF16)] * 2 + [pltpu.VMEM((width, hidden), BF16)] + [pltpu.VMEM((rows, hidden), BF16)] * 2,
        1 + len(chunks(hidden)) * (len(pd) + 4),
        "dgate",
    )


def down_body(n, perm, keep_ref, h1_hbm, m_hbm, *rest):
    pd = rest[:n]
    out_hbm, h1, mv, wd, acc, out, sems = rest[n:]
    move = Copies(sems)
    rows, width = h1.shape
    parts = chunks(mv.shape[1])
    got = [
        move.start(m_hbm.at[:, c : c + k], mv.at[:, c : c + k]) + move.weight(pd, c, k, wd) for c, k in parts
    ]
    got_h1 = move.start(h1_hbm, h1)
    for i, ((c, k), g) in enumerate(zip(parts, got)):
        cols = slice(c, c + k)
        wait(g)

        def tile(r, cols=cols, i=i):
            v = nt(mv[r, cols], wd[:, cols])
            acc[r, :] = v if i == 0 else acc[r, :] + v

        row_tiles(rows, 256, tile)
    wait(got_h1)
    for m in range(width // LANE):
        at = lanes(perm, m)
        out[:, at] = (h1[:, at] + keep_ref[...] * acc[:, m * LANE : (m + 1) * LANE]).astype(BF16)
    wait(move.start(out, out_hbm))


def down_call(perm, h1, keep, mixed, pd):
    rows, width = h1.shape
    hidden = mixed.shape[1]
    return call(
        functools.partial(down_body, len(pd)),
        perm,
        [keep],
        [h1, mixed, *pd],
        [sds((rows, width), BF16)],
        [
            pltpu.VMEM((rows, width), F32),
            pltpu.VMEM((rows, hidden), BF16),
            pltpu.VMEM((width, hidden), BF16),
            pltpu.VMEM((rows, width), F32),
            pltpu.VMEM((rows, width), BF16),
        ],
        2 + len(chunks(hidden)) * (len(pd) + 1),
        "down",
    )[0]


def norm_back(e, gain, normed, inv):
    scaled = e * gain
    return inv * (
        scaled
        - jnp.mean(scaled, axis=-1, keepdims=True)
        - normed * jnp.mean(scaled * normed, axis=-1, keepdims=True)
    )


def dmiddle_body(n, base, perm, gains_ref, keep_ref, cot_hbm, h1_hbm, dg_hbm, du_hbm, *rest):
    pa, pb = rest[:n], rest[n : 2 * n]
    dh1_hbm, e_hbm, do_hbm, gg_hbm, cot, h1, dg, du, wg, wu, wo, acc, db, e, do, gg, sems = rest[2 * n :]
    move = Copies(sems)
    rows, width = h1.shape
    parts = chunks(dg.shape[1])
    got = []
    for c, k in parts:
        cols = slice(c, c + k)
        got.append(move.start(dg_hbm.at[:, cols], dg.at[:, cols]) + move.weight(pa, base + c, k, wg, c))
        got.append(move.start(du_hbm.at[:, cols], du.at[:, cols]) + move.weight(pb, c, k, wu))
    got_rest = move.start(h1_hbm, h1) + move.start(cot_hbm, cot) + move.weight(pa, 0, width, wo)
    for i, g in enumerate(got):
        c, k = parts[i // 2]
        cols = slice(c, c + k)
        left, right = ((dg, wg), (du, wu))[i % 2]
        wait(g)

        def tile(r, cols=cols, left=left, right=right, i=i):
            v = nt(left[r, cols], right[:, cols])
            acc[r, :] = v if i == 0 else acc[r, :] + v

        row_tiles(rows, 256, tile)
    for m in range(width // LANE):
        db[:, lanes(perm, m)] = acc[:, m * LANE : (m + 1) * LANE]
    gg[...] = jnp.zeros_like(gg)
    wait(got_rest)
    done = []
    for t in range(2):
        at = t * (rows // 2)

        def back(i, carry, at=at):
            r = pl.ds(pl.multiple_of(at + i * LANE, LANE), LANE)
            normed, inv = norm_rows(h1[r, :])
            v = db[r, :]
            gg[...] += jnp.sum(v * normed, axis=0, keepdims=True)
            dh1 = cot[r, :].astype(F32) + norm_back(v, gains_ref[1:2, :], normed, inv)
            db[r, :] = dh1
            e[r, :] = (keep_ref[r, :] * dh1).astype(BF16)
            return carry

        lax.fori_loop(0, rows // 2 // LANE, back, 0)
        part = slice(at, at + rows // 2)
        done += move.start(db.at[part, :], dh1_hbm.at[part, :]) + move.start(e.at[part, :], e_hbm.at[part, :])
        d = nt(e[part, :], wo[...])
        for m in range(width // LANE):
            do[part, lanes(perm, m)] = d[:, m * LANE : (m + 1) * LANE].astype(BF16)
        done += move.start(do.at[part, :], do_hbm.at[part, :])
    done += move.start(gg, gg_hbm)
    wait(done)


def dmiddle_call(perm, gains, cot, keep, h1, dg, du, pa, pb, base):
    rows, width = h1.shape
    hidden = dg.shape[1]
    return call(
        functools.partial(dmiddle_body, len(pa), base),
        perm,
        [gains, keep],
        [cot, h1, dg, du, *pa, *pb],
        [sds((rows, width), F32), sds((rows, width), BF16), sds((rows, width), BF16), sds((1, width), F32)],
        [
            pltpu.VMEM((rows, width), BF16),
            pltpu.VMEM((rows, width), F32),
            pltpu.VMEM((rows, hidden), BF16),
            pltpu.VMEM((rows, hidden), BF16),
            pltpu.VMEM((width, hidden), BF16),
            pltpu.VMEM((width, hidden), BF16),
            pltpu.VMEM((width, width), BF16),
            pltpu.VMEM((rows, width), F32),
            pltpu.VMEM((rows, width), F32),
            pltpu.VMEM((rows, width), BF16),
            pltpu.VMEM((rows, width), BF16),
            pltpu.VMEM((1, width), F32),
        ],
        9 + len(pa) + len(chunks(hidden)) * 2 * (len(pa) + 1),
        "dmiddle",
    )


def dattend_body(perm, segk_ref, segq_ref, q_ref, k0_ref, k1_ref, v0_ref, v1_ref, do_ref, lse_ref, *rest):
    dq_ref, dk0_ref, dv0_ref, dk1_ref, dv1_ref, bias, kt, dk, dv = rest
    j = pl.program_id(0)
    rows = q_ref.shape[0]
    tile = 256

    @pl.when(j == 0)
    def _():
        bias[...] = jnp.where(segk_ref[...] == segq_ref[...], 0.0, NEG)

    for i in range(rows // LANE):
        r = slice(i * LANE, (i + 1) * LANE)
        kt[:, r] = k0_ref[r, :].astype(F32).T.astype(BF16)
        kt[:, rows + i * LANE : rows + (i + 1) * LANE] = k1_ref[r, :].astype(F32).T.astype(BF16)
    head_of = lax.broadcasted_iota(jnp.int32, (1, LANE), 1) // HEAD
    scale = LOG2E / math.sqrt(HEAD)
    back = 1.0 / math.sqrt(HEAD)
    for t in range(rows // tile):
        cols = slice(t * tile, (t + 1) * tile)
        q = q_ref[cols, :]
        do = do_ref[cols, :]
        parts = []
        for h in range(LANE // HEAD):
            qm = jnp.where(head_of == h, q, jnp.zeros_like(q))
            dom = jnp.where(head_of == h, do, jnp.zeros_like(do))
            s = jnp.concatenate([nt(k0_ref[...], qm), nt(k1_ref[...], qm)], axis=0) * scale + bias[:, cols]
            p = jnp.exp2(s - lse_ref[0, h : h + 1, cols])
            dp = jnp.concatenate([nt(v0_ref[...], dom), nt(v1_ref[...], dom)], axis=0)
            inner = jnp.sum(p * dp, axis=0, keepdims=True)
            ds = (p * (dp - inner)).astype(BF16)
            dv_new = nn(p.astype(BF16), dom)
            dk_new = nn(ds, qm)
            if t == 0 and h == 0:
                dv[...] = dv_new
                dk[...] = dk_new
            else:
                dv[...] += dv_new
                dk[...] += dk_new
            parts.append(nn(kt[...], ds)[h * HEAD : (h + 1) * HEAD, :])
        dq_ref[cols, :] = (jnp.concatenate(parts, axis=0).T * back).astype(BF16)
    dk0_ref[...] = dk[:rows, :]
    dv0_ref[...] = dv[:rows, :]
    dk1_ref[...] = dk[rows:, :].astype(BF16)
    dv1_ref[...] = dv[rows:, :].astype(BF16)


def dattend_call(perm, segk, segq, q, kv0, kv1, do, lse, first, count):
    rows, width = q.shape
    pairs = width // LANE
    full = lambda j: (0, 0)
    at = lambda j: (0, first + j)
    vat = lambda j: (0, pairs + first + j)
    block = (rows, LANE)
    return pl.pallas_call(
        dattend_body,
        grid=(count,),
        out_shape=(
            sds((rows, count * LANE), BF16),
            sds((rows, count * LANE), F32),
            sds((rows, count * LANE), F32),
            sds((rows, count * LANE), BF16),
            sds((rows, count * LANE), BF16),
        ),
        in_specs=[
            SMEM,
            pl.BlockSpec((2 * rows, 1), full),
            pl.BlockSpec((1, rows), full),
            pl.BlockSpec(block, at),
            pl.BlockSpec(block, at),
            pl.BlockSpec(block, at),
            pl.BlockSpec(block, vat),
            pl.BlockSpec(block, vat),
            pl.BlockSpec(block, at),
            pl.BlockSpec((1, 8, rows), lambda j: (first + j, 0, 0)),
        ],
        out_specs=(pl.BlockSpec(block, lambda j: (0, j)),) * 5,
        scratch_shapes=[
            pltpu.VMEM((2 * rows, rows), F32),
            pltpu.VMEM((LANE, 2 * rows), BF16),
            pltpu.VMEM((2 * rows, LANE), F32),
            pltpu.VMEM((2 * rows, LANE), F32),
        ],
        compiler_params=params(),
        cost_estimate=COST,
        name="dattend",
    )(perm, segk, segq, q, kv0, kv1, kv0, kv1, do, lse)


def dqkv_body(perm, cos_ref, sin_ref, dq_ref, dk0_ref, dv0_ref, dk1_ref, dv1_ref, out_ref):
    width = dq_ref.shape[1]
    cos = cos_ref[...]
    sin = -sin_ref[...]
    out_ref[:, :width] = turn(dq_ref[...].astype(F32), cos, sin).astype(BF16)
    key = ((dk0_ref[...] + dk1_ref[...].astype(F32)) * (1.0 / math.sqrt(HEAD))).astype(BF16)
    out_ref[:, width : 2 * width] = turn(key.astype(F32), cos, sin).astype(BF16)
    out_ref[:, 2 * width :] = (dv0_ref[...] + dv1_ref[...].astype(F32)).astype(BF16)


def dqkv_call(perm, cos, sin, dq, dk0, dv0, dk1, dv1):
    rows, width = dq.shape
    tile = 64
    row = lambda i: (i, 0)
    block = pl.BlockSpec((tile, width), row)
    return pl.pallas_call(
        dqkv_body,
        grid=(rows // tile,),
        out_shape=sds((rows, 3 * width), BF16),
        in_specs=[SMEM] + [pl.BlockSpec((tile, LANE), row)] * 2 + [block] * 5,
        out_specs=pl.BlockSpec((tile, 3 * width), row),
        compiler_params=params(),
        cost_estimate=COST,
        name="dqkv",
    )(perm, cos, sin, dq, dk0, dv0, dk1, dv1)


def dinput_body(n, perm, gains_ref, x_hbm, dh1_hbm, da_hbm, db_hbm, *rest):
    p0, p1 = rest[:n], rest[n : 2 * n]
    out_hbm, gg_hbm, x, dh1, d, w, acc, e, out, gg, sems = rest[2 * n :]
    move = Copies(sems)
    rows, width = x.shape
    part = 3 * width // 2
    got = []
    for i, (source, pieces) in enumerate(((da_hbm, p0), (db_hbm, p1))):
        for c, k in chunks(part, part // 2):
            to = slice(i * part + c, i * part + c + k)
            got.append((to, move.start(source.at[:, c : c + k], d.at[:, to]) + move.weight(pieces, c, k, w, i * part + c)))
    got_rest = move.start(x_hbm, x) + move.start(dh1_hbm, dh1)
    for i, (cols, g) in enumerate(got):
        wait(g)

        def tile(r, cols=cols, i=i):
            v = nt(d[r, cols], w[:, cols])
            acc[r, :] = v if i == 0 else acc[r, :] + v

        row_tiles(rows, 256, tile)
    for m in range(width // LANE):
        e[:, lanes(perm, m)] = acc[:, m * LANE : (m + 1) * LANE]
    gg[...] = jnp.zeros_like(gg)
    wait(got_rest)
    done = []
    for t in range(2):
        at = t * (rows // 2)

        def back(i, carry, at=at):
            r = pl.ds(pl.multiple_of(at + i * LANE, LANE), LANE)
            normed, inv = norm_rows(x[r, :].astype(F32))
            v = e[r, :]
            gg[...] += jnp.sum(v * normed, axis=0, keepdims=True)
            out[r, :] = (dh1[r, :] + norm_back(v, gains_ref[0:1, :], normed, inv)).astype(BF16)
            return carry

        lax.fori_loop(0, rows // 2 // LANE, back, 0)
        here = slice(at, at + rows // 2)
        done += move.start(out.at[here, :], out_hbm.at[here, :])
    done += move.start(gg, gg_hbm)
    wait(done)


def dinput_call(perm, gains, x, dh1, da, db, p0, p1):
    rows, width = x.shape
    return call(
        functools.partial(dinput_body, len(p0)),
        perm,
        [gains],
        [x, dh1, da, db, *p0, *p1],
        [sds((rows, width), BF16), sds((1, width), F32)],
        [
            pltpu.VMEM((rows, width), BF16),
            pltpu.VMEM((rows, width), F32),
            pltpu.VMEM((rows, 3 * width), BF16),
            pltpu.VMEM((width, 3 * width), BF16),
            pltpu.VMEM((rows, width), F32),
            pltpu.VMEM((rows, width), F32),
            pltpu.VMEM((rows, width), BF16),
            pltpu.VMEM((1, width), F32),
        ],
        9 + 4 * len(p0),
        "dinput",
    )


def grad_body(masked, form, col, perm, *refs):
    count = 2 if form != "f" else 1
    keeps = refs[: count if masked else 0]
    refs = refs[len(keeps) :]
    lefts, rights = refs[:count], refs[count : 2 * count]
    outs = refs[2 * count : -4]
    left, right, out, sems = refs[-4:]
    move = Copies(sems)
    height, width = left.shape[2], right.shape[2]
    parts = chunks(width)
    got_left, got = [], [[] for _ in parts]
    for s in range(count):
        got_left.append([])
        for i in range(height // LANE):
            got_left[s] += move.start(lefts[s].at[:, lanes(perm, i)], left.at[s, :, i * LANE : (i + 1) * LANE])
        got[0] += move.start(rights[s].at[:, col : col + parts[0][1]], right.at[s, :, : parts[0][1]])
    for p, (c, k) in list(enumerate(parts))[1:]:
        for s in range(count):
            got[p] += move.start(rights[s].at[:, col + c : col + c + k], right.at[s, :, c : c + k])
    for s in range(count):
        wait(got_left[s])
        if masked:
            left[s] = (left[s].astype(F32) * keeps[s][...]).astype(BF16)
    done = []
    for (c, k), g in zip(parts, got):
        cols = slice(c, c + k)
        wait(g)
        for t in range(height // 256):
            rows = slice(t * 256, (t + 1) * 256)
            v = tn(left[0, :, rows], right[0, :, cols])
            for s in range(1, count):
                v = v + tn(left[s, :, rows], right[s, :, cols])
            if form == "f":
                out[0, rows, cols] = v
            elif form == "x":
                here = slice(t * LANE, (t + 1) * LANE)
                out[0, here, cols] = v[LANE:, :].astype(BF16)
                out[1, here, cols] = v[:LANE, :].astype(BF16)
            else:
                out[1 - t, :, cols] = v.astype(BF16)
        for i, to in enumerate(outs):
            done += move.start(out.at[i, :, cols], to.at[:, cols])
    wait(done)


def grad_call(perm, sources, col, count, form):
    rows, width = sources[0][0].shape
    keeps = [k for _, _, k in sources if k is not None]
    height = width if form == "f" else width // 2
    outs = [sds((height, count), F32)] if form == "f" else [sds((height // 2, count), BF16)] * 2
    parts = len(chunks(count))
    got = call(
        functools.partial(grad_body, bool(keeps), form, col),
        perm,
        keeps,
        [s[0] for s in sources] + [s[1] for s in sources],
        outs,
        [
            pltpu.VMEM((len(sources), rows, height), BF16),
            pltpu.VMEM((len(sources), rows, count), BF16),
            pltpu.VMEM((len(outs), outs[0].shape[0], count), outs[0].dtype),
        ],
        len(sources) * (height // LANE + parts) + len(outs) * parts,
        "grad_" + form,
    )
    return got[0] if form == "f" else got


def rotary_tables(positions):
    half = HEAD // 2
    exponent = jnp.arange(half, dtype=F32) * (2.0 / HEAD)
    frequency = jnp.exp(-exponent * math.log(rope_base))
    angles = positions.astype(F32)[:, None] * frequency[None, :]
    cos, sin = jnp.cos(angles), jnp.sin(angles)
    return jnp.concatenate([cos, cos, cos, cos], axis=-1), jnp.concatenate([-sin, sin, -sin, sin], axis=-1)


def on_device(tokens, segments, cotangent, attn_gain, w_qkv, w_attn_out, mlp_gain, w_in, w_mlp_out):
    micro_count, seq_count, local_len, width = tokens.shape
    hidden = w_mlp_out.shape[1]
    padded = -(-hidden // LANE) * LANE
    dp_count = lax.axis_size("dp")
    ctx_count = lax.axis_size("ctx")
    part = width // (dp_count * ctx_count)
    blocks = width // LANE
    half_len = local_len // 2
    rows = ctx_count * half_len
    assert seq_count == 1 and ctx_count == 2 * micro_count and dp_count % 2 == 0
    fast = dp_count == 8 and ctx_count * part == LANE
    dp = lax.axis_index("dp")
    low = dp % 2

    def swap(v, bit):
        return lax.ppermute(v, "dp", [(i, i ^ bit) for i in range(dp_count)])

    def tie(v, *after):
        return lax.optimization_barrier((v, *after))[0] if after else v

    def across(v):
        return lax.all_to_all(v, "ctx", split_axis=0, concat_axis=0, tiled=True)

    def pick(zero, one):
        return jnp.where(low == 0, zero, one)

    def spread(shard):
        return jnp.broadcast_to(shard[None], (ctx_count, *shard.shape))

    def flat(v):
        return v.reshape(v.shape[0] * v.shape[1], v.shape[2])

    def halves_out(v):
        halves = v.reshape(micro_count, 2, half_len, width)
        return pick(halves[:, 0], halves[:, 1]), pick(halves[:, 1], halves[:, 0])

    def join_in(mine, other):
        both = jnp.stack([pick(mine, other), pick(other, mine)], axis=1)
        return both.reshape(ctx_count, half_len, width)

    def split_back(got):
        got = got.reshape(micro_count, 2, half_len, width)
        return pick(got[:, 0], got[:, 1]), pick(got[:, 1], got[:, 0])

    def join_back(mine, other):
        both = jnp.stack([pick(mine, other), pick(other, mine)], axis=1)
        return both.reshape(micro_count, 1, local_len, width)

    step = jnp.arange(rows, dtype=jnp.int32)
    positions = step // half_len * local_len + low * half_len + step % half_len
    cos, sin = rotary_tables(positions)

    index = jnp.arange(blocks, dtype=jnp.int32)
    if fast:
        turned = (index // 4) + 4 * (index // 2 % 2) + 2 * (index % 2)
        perm = jnp.bitwise_xor(turned, dp.astype(jnp.int32))
    else:
        perm = index

    third = 3 * width // 2
    seg = segments.reshape(micro_count, local_len)
    seg_cols = micro_count * local_len // part
    gain_cols = jnp.concatenate(
        [
            attn_gain[:, None],
            mlp_gain[:, None],
            seg.astype(BF16).reshape(part, seg_cols) if fast else jnp.zeros((part, 0), BF16),
            jnp.zeros((part, LANE - 2 - (seg_cols if fast else 0)), BF16),
        ],
        axis=1,
    )
    pad = ((0, 0), (0, padded - hidden))
    first_cols = third + LANE
    hw = width // 2
    thirds = [w_qkv[:, i * hw : (i + 1) * hw] for i in range(6)]
    shard_qkv = jnp.concatenate(thirds[0::2] + [gain_cols] + thirds[1::2], axis=1)
    shard_rest = jnp.concatenate([w_attn_out, jnp.pad(w_in[:, :hidden], pad), jnp.pad(w_in[:, hidden:], pad)], axis=1)
    shard_down = jnp.pad(w_mlp_out, pad)
    cut = width + padded

    def gather_all(shard):
        return lax.all_gather(shard, ("dp", "ctx"), axis=0, tiled=True)

    def gather_line(shard):
        return lax.all_gather(shard, "ctx", axis=0, tiled=True)

    last = []

    def order(v, *after):
        return tie(v, *last, *after)

    def did(out):
        last[:] = [jax.tree.leaves(out)[0]]
        return out

    mine, other = halves_out(tokens)
    cot_mine, cot_other = halves_out(cotangent)
    live = {}

    def sync(**more):
        live.update(more)
        names, leaves = zip(*live.items())
        live.update(zip(names, lax.optimization_barrier(leaves)))
        return [live[k] for k in more]

    if fast:
        other = swap(other, 1)
        own1 = gather_line(shard_qkv)
        a1, b1, other, mine = sync(a1=own1[:, :first_cols], b1=own1[:, first_cols:], other=other, mine=mine)
        (rest_in,) = sync(rest_in=shard_rest)
        own2 = gather_line(rest_in)
        sync(cos=cos, sin=sin, perm=perm, down_in=spread(shard_down))
        xa1, yb1, ca1, cb1 = sync(xa1=swap(a1, 2), yb1=swap(b1, 4), ca1=swap(a1, 1), cb1=swap(b1, 1))
        a1, b1 = live["a1"], live["b1"]
        sync(ya1=swap(a1, 4), yxa1=swap(xa1, 4), xb1=swap(b1, 2), xyb1=swap(yb1, 2), cxa1=swap(xa1, 1), cyb1=swap(yb1, 1))
        sync(own2=own2, **{"c" + k: swap(live[k], 1) for k in ("ya1", "yxa1", "xb1", "xyb1")})
        a2, b2 = live["own2"][:, :cut], live["own2"][:, cut:]
        x_in = across(join_in(live["mine"], live["other"]))
        sync(xa2=swap(a2, 2), yb2=swap(b2, 4), x_in=x_in, a2=a2, b2=b2)
        qkv0 = [live[k] for k in ("a1", "xa1", "ya1", "yxa1", "ca1", "cxa1", "cya1", "cyxa1")]
        qkv1 = [live[k] for k in ("b1", "xb1", "yb1", "xyb1", "cb1", "cxb1", "cyb1", "cxyb1")]
        cos, sin, perm = live["cos"], live["sin"], live["perm"]
        x = flat(live["x_in"])
        seg_at = slice(third + 2, third + 2 + seg_cols)
        z = lax.axis_index("ctx")
        seg_from = jnp.where(z % 2 == low, qkv0[0][:, seg_at], qkv0[4][:, seg_at])
        seg_from = seg_from.reshape(ctx_count, micro_count, local_len)
        seg_all = lax.dynamic_index_in_dim(seg_from, z // 2, 1, False).astype(jnp.int32)
    else:
        qkv0, qkv1 = [gather_all(shard_qkv[:, :first_cols])], [gather_all(shard_qkv[:, first_cols:])]
        rest_a, rest_b = [gather_all(shard_rest[:, :cut])], [gather_all(shard_rest[:, cut:])]
        wdown = [gather_all(shard_down)]
        x = flat(across(join_in(mine, swap(other, 1))))
        cot = flat(across(join_in(cot_mine, swap(cot_other, 1))))
        seg_other = swap(seg, 1)
        seg_all = across(jnp.stack([pick(seg, seg_other), pick(seg_other, seg)], axis=1).reshape(ctx_count, local_len))

    seg_halves = seg_all.reshape(ctx_count, 2, half_len)
    seg_mine = pick(seg_halves[:, 0], seg_halves[:, 1]).reshape(rows)
    seg_theirs = pick(seg_halves[:, 1], seg_halves[:, 0]).reshape(rows)
    segq = seg_mine.reshape(1, rows)
    segk = jnp.concatenate([seg_mine, seg_theirs]).reshape(2 * rows, 1)
    keep = (seg_mine != 0).astype(F32).reshape(rows, 1)
    keep_theirs = (seg_theirs != 0).astype(F32).reshape(rows, 1)

    attn_in, q, kv, gains = qkv_call(perm, x, cos, sin, qkv0, qkv1)
    kv_other = swap(kv, 1)
    part_one = blocks // 2
    if fast:
        own3 = flat(across(live["down_in"]))
        sync(
            attn_in=attn_in, q=q, kv=kv, gains=gains, kv_other=kv_other, segq=segq, segk=segk, keep=keep,
            keep_theirs=keep_theirs, own3=own3, ya2=swap(live["a2"], 4), xb2=swap(live["b2"], 2),
            ca2=swap(live["a2"], 1), cb2=swap(live["b2"], 1),
        )
        attn_in, q, kv, gains, kv_other = (live[k] for k in ("attn_in", "q", "kv", "gains", "kv_other"))
        segq, segk, perm = live["segq"], live["segk"], live["perm"]
    some = attend_call(perm, segk, segq, q, kv, kv_other, 0, part_one)
    if fast:
        sync(yxa2=swap(live["xa2"], 4), xyb2=swap(live["yb2"], 2), some=some[0], some_lse=some[1], **{"c" + k: swap(live[k], 1) for k in ("xa2", "yb2")})
        some = (live["some"], live["some_lse"])
        attn_in, q, kv, gains, kv_other = (live[k] for k in ("attn_in", "q", "kv", "gains", "kv_other"))
        segq, segk, perm = live["segq"], live["segk"], live["perm"]
    attended, lse = attend_call(perm, segk, segq, q, kv, kv_other, part_one, blocks - part_one, some)
    if fast:
        cores = {"c" + k: swap(live[k], 1) for k in ("ya2", "xb2", "yxa2")}
        cot_in = join_in(cot_mine, swap(tie(cot_other, live["own3"]), 1))
        sync(attended=attended, lse=lse, xd=swap(live["own3"], 2), yd=swap(live["own3"], 4), cot_in=cot_in, x=x, **cores)
        rest_a = [live[k] for k in ("a2", "xa2", "ya2", "yxa2", "ca2", "cxa2", "cya2", "cyxa2")]
        rest_b = [live[k] for k in ("b2", "xb2", "yb2", "xyb2", "cb2", "cxb2", "cyb2")]
        rest_b.append(swap(live["xyb2"], 1))
        attn_in, q, kv, gains, kv_other, x = (live[k] for k in ("attn_in", "q", "kv", "gains", "kv_other", "x"))
        segq, segk, perm, attended, lse = (live[k] for k in ("segq", "segk", "perm", "attended", "lse"))
        keep, keep_theirs = live["keep"], live["keep_theirs"]
        own3, xd, yd = live["own3"], live["xd"], live["yd"]
        cot = flat(across(live["cot_in"]))
        xyd = swap(yd, 2)
        cores = [swap(v, 1) for v in (own3, xd, yd)]

    def pair(v, *after):
        return (v, swap(tie(v, *after), 1) if fast else None)

    h1, mlp_in = middle_call(perm, gains, x, keep, attended, rest_a)
    mixed, f1, f2 = gate_call(perm, mlp_in, rest_a, rest_b, padded, width)
    if fast:
        h1, mlp_in, mixed, f1, f2, cot, xyd, *cores = sync(
            h1=h1, mlp_in=mlp_in, mixed=mixed, f1=f1, f2=f2, cot=cot, xyd=xyd,
            **{"cores%d" % i: v for i, v in enumerate(cores)},
        )
        attn_in, gains, x, attended, keep, perm = (live[k] for k in ("attn_in", "gains", "x", "attended", "keep", "perm"))
        own3, xd, yd = (live[k] for k in ("own3", "xd", "yd"))
        wdown = [own3, xd, yd, xyd, *cores, swap(xyd, 1)]
        others = [swap(tie(v, wdown[-1]), 1) for v in (mixed, cot, mlp_in, attn_in, attended)]
    dgate, dup = did(dgate_call(perm, cot, keep, f1, f2, wdown))
    if fast:
        dgate, dup, mixed_other, cot_other, mlp_other, a_other, o_other = sync(
            dgate=dgate, dup=dup, **{"other%d" % i: v for i, v in enumerate(others)}
        )
        perm, cot, mixed, keep, keep_theirs, mlp_in = (
            live[k] for k in ("perm", "cot", "mixed", "keep", "keep_theirs", "mlp_in")
        )
        cot_pair, mixed_pair, mlp_pair = (cot, cot_other), (mixed, mixed_other), (mlp_in, mlp_other)
        in_pair, o_pair = (attn_in, a_other), (attended, o_other)
    else:
        cot_pair, mixed_pair, mlp_pair, in_pair, o_pair = ((v, None) for v in (cot, mixed, mlp_in, attn_in, attended))
    dgate_pair, dup_pair = pair(dgate), pair(dup)

    class Reduce:
        def __init__(self, left, right, keeps, col, count, form):
            self.count = count
            if not fast:
                g = did(grad_call(order(perm), [(left[0], right[0], keeps[0])], col, count, "f"))
                self.out = lax.psum_scatter(g, ("dp", "ctx"), scatter_dimension=0, tiled=True)
                return
            sources = [(left[i], right[i], keeps[i]) for i in range(2)]
            leave, self.kept = did(grad_call(order(perm), sources, col, count, form))
            self.first, self.second = (2, 4) if form == "x" else (4, 2)
            self.half = leave.shape[0] // 2
            self.got = swap(leave, self.first)

        def two(self):
            if fast:
                h = self.half
                kept = order(self.kept)
                leave = did((kept[h:].astype(F32) + self.got[h:].astype(F32)).astype(BF16))
                self.got2 = swap(leave, self.second)

        def three(self):
            got2 = order(self.got2)
            h = self.half
            total = self.kept[:h].astype(F32) + self.got[:h].astype(F32) + got2.astype(F32)
            return did(total.astype(BF16))

        def line(self, other=None):
            if fast:
                total = self.three()
                if other is not None:
                    total = did(jnp.concatenate([total, other.three()], axis=1))
                total = lax.psum_scatter(total, "ctx", scatter_dimension=0, tiled=True).astype(F32)
                self.out = total[:, : self.count]
                if other is not None:
                    other.out = total[:, self.count :]

    none = (None, None)
    r_down = Reduce(cot_pair, mixed_pair, (keep, keep_theirs), 0, padded, "x")
    r_gate = Reduce(mlp_pair, dgate_pair, none, 0, padded, "y")
    r_up = Reduce(mlp_pair, dup_pair, none, 0, padded, "x")
    dh1, e_attn, d_o, gain_two = did(dmiddle_call(order(perm), gains, cot, keep, h1, dgate, dup, rest_a, rest_b, width))
    e_pair = pair(e_attn)
    rows_out = did(down_call(order(perm), h1, keep, mixed, wdown))
    out_got = across(rows_out.reshape(ctx_count, half_len, width))
    r_down.two()
    r_out = Reduce(o_pair, e_pair, none, 0, width, "y")
    r_gate.two()
    back = lambda first, count: did(dattend_call(order(perm), segk, segq, q, kv, kv_other, d_o, lse, first, count))
    dq, dk0, dv0, dk1, dv1 = back(0, part_one)
    dk_got, dv_got = swap(dk1, 1), swap(dv1, 1)
    r_up.two()
    r_down.line()
    da = did(dqkv_call(order(perm), cos, sin, dq, dk0, dv0, dk_got, dv_got))
    da_pair = pair(da, out_got)
    r_gate.line()
    dq, dk0, dv0, dk1, dv1 = back(part_one, blocks - part_one)
    dk_got, dv_got = swap(tie(dk1, *((r_down.out,) if fast else ())), 1), swap(dv1, 1)
    r_qkva = Reduce(in_pair, da_pair, none, 0, third, "y")
    r_out.two()
    out_mine, out_other = split_back(out_got)
    layer_out = join_back(out_mine, swap(tie(out_other, dk_got), 1))
    db = did(dqkv_call(order(perm, *((r_gate.out,) if fast else ())), cos, sin, dq, dk0, dv0, dk_got, dv_got))
    db_pair = pair(db)
    r_up.line(r_out)
    r_qkva.two()
    input_rows, gain_one = did(dinput_call(order(perm), gains, x, dh1, da, db, qkv0, qkv1))
    in_got = across(input_rows.reshape(ctx_count, half_len, width))
    gain_rows = jnp.concatenate([gain_one, gain_two], axis=0)
    sub = third // 2
    if fast:
        gain_got = swap(gain_rows, 2)
    r_qkvb0 = Reduce(in_pair, db_pair, none, 0, sub, "x")
    if fast:
        gain_rows = did(order(gain_rows) + gain_got)
        gain_got = swap(gain_rows, 4)
    r_qkvb1 = Reduce(in_pair, db_pair, none, sub, sub, "y")
    r_qkva.line()
    if fast:
        gain_rows = did(order(gain_rows) + gain_got)
        gain_got = swap(gain_rows, 1)
    r_qkvb0.two()
    r_qkvb1.two()
    if fast:
        gain_rows = gain_rows + gain_got
        ours = lax.dynamic_slice(gain_rows, (0, dp * LANE), (2, LANE)).T.astype(BF16)
        total = jnp.concatenate([r_qkvb0.three(), r_qkvb1.three(), ours, jnp.zeros((LANE, LANE - 2), BF16)], axis=1)
        total = jnp.sum(across(tie(total, in_got).reshape(ctx_count, part, third + LANE)).astype(F32), axis=0)
        qkvb = total[:, :third]
        gain_grads = (total[:, third], total[:, third + 1])
    else:
        qkvb = jnp.concatenate([r_qkvb0.out, r_qkvb1.out], axis=1)
        gain_grads = lax.psum_scatter(gain_rows, ("dp", "ctx"), scatter_dimension=1, tiled=True)
    qkv_grad = jnp.concatenate(
        [half[:, i * hw : (i + 1) * hw] for i in range(3) for half in (r_qkva.out, qkvb)], axis=1
    )
    in_mine, in_other = split_back(order(in_got))
    input_grad = join_back(in_mine, swap(in_other, 1))

    return (
        layer_out,
        input_grad,
        gain_grads[0],
        qkv_grad,
        r_out.out,
        gain_grads[1],
        jnp.concatenate([r_gate.out[:, :hidden], r_up.out[:, :hidden]], axis=1),
        r_down.out[:, :hidden],
    )


def solution(mesh):
    return jax.shard_map(
        on_device,
        mesh=mesh,
        in_specs=(
            P(None, "dp", "ctx", None),
            P(None, "dp", "ctx"),
            P(None, "dp", "ctx", None),
            P(("dp", "ctx")),
            P(("dp", "ctx"), None),
            P(("dp", "ctx"), None),
            P(("dp", "ctx")),
            P(("dp", "ctx"), None),
            P(("dp", "ctx"), None),
        ),
        out_specs=(
            P(None, "dp", "ctx", None),
            P(None, "dp", "ctx", None),
            P(("dp", "ctx")),
            P(("dp", "ctx"), None),
            P(("dp", "ctx"), None),
            P(("dp", "ctx")),
            P(("dp", "ctx"), None),
            P(("dp", "ctx"), None),
        ),
        check_vma=False,
    )
```

time: 517 us -> 494 us (0.956)
  waiting for transfers between devices: 126 us -> 99.4 us
  local copies, waits for them, and re-layouts: 26.9 us -> 39.6 us
  Pallas kernels: 209 us -> 199 us
    reduce_scatter x5 -> x4, waiting for transfers between devices: 16.9 us -> 2.23 us  [line(): lax.psum_scatter(total, 'ctx', scatter_dimension=0, tiled=True).astype(F32)]
    all_to_all x6, waiting for transfers between devices: 28.8 us -> 16.4 us  [across(): return lax.all_to_all(v, 'ctx', split_axis=0, concat_axis=0, tiled=True)]
    pallas_call x14, Pallas kernels: 131 us -> 121 us  [call(): pl.pallas_call(body, out_shape=tuple(outs), in_specs=[SMEM] + [pl.BlockSp...]
    unnamed x135, local copies, waits for them, and re-layouts: 10.3 us -> 17.9 us
    optimization_barrier x0 -> x7, local copies, waits for them, and re-layouts: none -> 6.51 us  [sync(): live.update(zip(names, lax.optimization_barrier(leaves)))]
  transfers between devices with their start and end apart: 83 -> 82, of which waited for: 29 -> 24; matrix products, arithmetic and copies ran while one was open for 10% -> 13% of each run, Pallas kernels for 36% -> 38%
where the time goes in v3:
time: 494 us; the launch traced here: 486 us
  Pallas kernels  199 us (40%)
  waiting for transfers between devices  99.4 us (20%)
  starting transfers between devices  67.8 us (14%)
  other arithmetic  43.1 us (9%)
  local copies, waits for them, and re-layouts  39.6 us (8%)
  blocking collectives  21.3 us (4%)
  between operations  15.3 us (3%)
    pallas_call x14, Pallas kernels, call(): pl.pallas_call(body, out_shape=tuple(outs), in_specs=[SMEM] + [pl.BlockSp...  121 us
    ppermute x71, waiting for transfers between devices, swap(): return lax.ppermute(v, 'dp', [(i, i ^ bit) for i in range(dp_count)])  80.6 us
    ppermute x71, starting transfers between devices, swap(): return lax.ppermute(v, 'dp', [(i, i ^ bit) for i in range(dp_count)])  42.2 us
    pallas_call x2, Pallas kernels, dattend_call(): pl.pallas_call(dattend_body, grid=(count,), out_shape=(sds((rows, count *...  36.5 us
    pallas_call x2, Pallas kernels, attend_call(): pl.pallas_call(functools.partial(attend_body, len(given)), grid=(count,),...  28.4 us
    all_to_all x6, starting transfers between devices, across(): return lax.all_to_all(v, 'ctx', split_axis=0, concat_axis=0, tiled=True)  25.2 us
    all_gather x1, blocking collectives, gather_line(): return lax.all_gather(shard, 'ctx', axis=0, tiled=True)  21.3 us
    unnamed x135, local copies, waits for them, and re-layouts  17.9 us
  transfers between devices with their start and end apart: 82, of which 24 were waited for; matrix products, arithmetic and copies ran while one was open for 13% of the time, Pallas kernels for 38%

profile of v3, /device:TPU:0, one launch (start us, length us, event | category | flops | bytes accessed | tf_op | source)
XLA Modules:
  0.0 485.8 jit_solution(11013509689976994660)
XLA Ops:
  9.6 21.3 %all_gather.6 = bf16[128,3200]{1,0:T(8,128)(2,1)S(1)} all-gather(bf16[32,3200]{1,0:T(8,128)(2,1)S(1)} %concatenate.30), channel_id=1, replica_groups=mesh['dp'=8,'ctx'=4] {'ctx'}, dimensions={0}, use_global_device_ids=true | all-gather | bytes 1024000 | tf_op jit(solution)/shard_map/all_gather | solution.py:867
  51.2 9.9 %collective-permute-done.7.rest_9_ = bf16[128,1536]{1,0:T(8,128)(2,1)S(1)} collective-permute-done((bf16[128,1536]{1,0:T(8,128)(2,1)S(1)}, bf16[128,1536]{1,0:T(8,128)(2,1)S(1)}, u32[]{:S(2)}, u32[]{:S(2)}) %collective-permute-start.7) | collective-permute-done | bytes 393248 | tf_op jit(solution)/shard_map/ppermute | solution.py:798
  61.1 8.0 %collective-permute-done.8.rest_11_ = bf16[128,1536]{1,0:T(8,128)(2,1)S(1)} collective-permute-done((bf16[128,1536]{1,0:T(8,128)(2,1)S(1)}, bf16[128,1536]{1,0:T(8,128)(2,1)S(1)}, u32[]{:S(2)}, u32[]{:S(2)}) %collective-permute-start.8) | collective-permute-done | bytes 393248 | tf_op jit(solution)/shard_map/ppermute | solution.py:798
  84.2 15.7 %collective-permute-done.16.rest_10_ = bf16[128,2688]{1,0:T(8,128)(2,1)S(1)} collective-permute-done((bf16[128,2688]{1,0:T(8,128)(2,1)S(1)}, bf16[128,2688]{1,0:T(8,128)(2,1)S(1)}, u32[]{:S(2)}, u32[]{:S(2)}) %collective-permute-start.16) | collective-permute-done | bytes 688160 | tf_op jit(solution)/shard_map/ppermute | solution.py:798
  106.8 12.5 %qkv.1 = (bf16[512,1024]{1,0:T(8,128)(2,1)}, bf16[512,1024]{1,0:T(8,128)(2,1)}, bf16[512,2048]{1,0:T(8,128)(2,1)}, f32[8,1024]{1,0:T(8,128)}) custom-call(s32[8]{0:T(128)} %fusion.25.perm, f32[512,128]{1,0:T(8,128)} %get-tuple-element.370.cos_ref, f32[512,128]{1,0:T(8,128)} %get-tuple-element.371.sin_ref, bf16[512,1024]{1,0:T(8,128)(2,1)} %bitcast.149, ...), custom_call_target="tpu_custom_call" | custom-call | flops 1 | bytes 1 | tf_op jit(solution)/shard_map/qkv/pallas_call | solution.py:88
  127.2 12.0 %collective-permute-done.19.rest_9_ = bf16[128,2688]{1,0:T(8,128)(2,1)} collective-permute-done((bf16[128,2688]{1,0:T(8,128)(2,1)}, bf16[128,2688]{1,0:T(8,128)(2,1)}, u32[]{:S(2)}, u32[]{:S(2)}) %collective-permute-start.19) | collective-permute-done | bytes 688160 | tf_op jit(solution)/shard_map/ppermute | solution.py:798
  150.5 14.2 %attend.2 = (bf16[512,1024]{1,0:T(8,128)(2,1)}, f32[8,8,512]{2,1,0:T(8,128)}) custom-call(s32[8]{0:T(128)} %fusion.25.perm, s32[1024,1]{1,0:T(8,128)} %copy.101.segk_ref, s32[1,512]{1,0:T(1,128)} %bitcast.168, bf16[512,1024]{1,0:T(8,128)(2,1)} %get-tuple-element.452.q_ref, bf16[512,2048]{1,0:T(8,128)(2,1)} %get-tuple-element.453.k0_ref.v0_ref, ...), custom_call_target="tpu_custom_call" | custom-call | flops 1 | bytes 1 | tf_op jit(solution)/shard_map/attend/pallas_call | solution.py:221
  174.6 14.2 %attend.3 = (bf16[512,1024]{1,0:T(8,128)(2,1)}, f32[8,8,512]{2,1,0:T(8,128)}) custom-call(s32[8]{0:T(128)} %fusion.25.perm, s32[1024,1]{1,0:T(8,128)} %copy.102.segk_ref, s32[1,512]{1,0:T(1,128)} %bitcast.169, bf16[512,1024]{1,0:T(8,128)(2,1)} %get-tuple-element.452.q_ref, ...), custom_call_target="tpu_custom_call", output_to_operand_aliasing={{0}: (8, {}), {1}: (9, {})} | custom-call | flops 1 | bytes 1 | tf_op jit(solution)/shard_map/attend/pallas_call | solution.py:221
  198.7 7.2 %middle.1 = (f32[512,1024]{1,0:T(8,128)}, bf16[512,1024]{1,0:T(8,128)(2,1)}) custom-call(s32[8]{0:T(128)} %fusion.25.perm, f32[8,1024]{1,0:T(8,128)} %get-tuple-element.485.gains_ref, f32[512,1]{1,0:T(8,128)} %copy.106.keep_ref, bf16[512,1024]{1,0:T(8,128)(2,1)} %bitcast.150, bf16[512,1024]{1,0:T(8,128)(2,1)} %get-tuple-element.509.o_hbm.refs_0_, ...), custom_call_target="tpu_custom_call" | custom-call | flops 1 | bytes 1 | tf_op jit(solution)/shard_map/middle/pallas_call | solution.py:88
  206.7 13.9 %gate.1 = (bf16[512,2688]{1,0:T(8,128)(2,1)}, bf16[512,2688]{1,0:T(8,128)(2,1)}, bf16[512,2688]{1,0:T(8,128)(2,1)}) custom-call(s32[8]{0:T(128)} %fusion.25.perm, bf16[512,1024]{1,0:T(8,128)(2,1)} %get-tuple-element.520.b_hbm.refs_0_, bf16[128,3712]{1,0:T(8,128)(2,1)} %copy-done.4, bf16[128,3712]{1,0:T(8,128)(2,1)} %copy-done.6, ...), custom_call_target="tpu_custom_call" | custom-call | flops 1 | bytes 1 | tf_op jit(solution)/shard_map/gate/pallas_call | solution.py:88
  227.1 9.5 %dgate.1 = (bf16[512,2688]{1,0:T(8,128)(2,1)}, bf16[512,2688]{1,0:T(8,128)(2,1)}) custom-call(s32[8]{0:T(128)} %fusion.25.perm, f32[512,1]{1,0:T(8,128)} %copy.107.keep_ref, bf16[512,1024]{1,0:T(8,128)(2,1)} %bitcast.153, bf16[512,2688]{1,0:T(8,128)(2,1)} %get-tuple-element.496.f1_hbm, bf16[512,2688]{1,0:T(8,128)(2,1)} %get-tuple-element.497.f2_hbm, ...), custom_call_target="tpu_custom_call" | custom-call | flops 1 | bytes 1 | tf_op jit(solution)/shard_map/dgate/pallas_call | solution.py:88
  239.0 7.7 %grad_x.3 = (bf16[256,2688]{1,0:T(8,128)(2,1)}, bf16[256,2688]{1,0:T(8,128)(2,1)}) custom-call(s32[8]{0:T(128)} %fusion.25.perm, f32[512,1]{1,0:T(8,128)} %copy.108.refs_0_.keep_ref, f32[512,1]{1,0:T(8,128)} %copy.109.refs_1_, bf16[512,1024]{1,0:T(8,128)(2,1)} %bitcast.154, bf16[512,1024]{1,0:T(8,128)(2,1)} %collective-permute-done.39.refs_3_, ...), custom_call_target="tpu_custom_call" | custom-call | flops 1 | bytes 1 | tf_op jit(solution)/shard_map/grad_x/pallas_call | solution.py:88
  247.6 7.3 %grad_y.4 = (bf16[256,2688]{1,0:T(8,128)(2,1)}, bf16[256,2688]{1,0:T(8,128)(2,1)}) custom-call(s32[8]{0:T(128)} %fusion.25.perm, bf16[512,1024]{1,0:T(8,128)(2,1)} %get-tuple-element.520.b_hbm.refs_0_, bf16[512,1024]{1,0:T(8,128)(2,1)} %collective-permute-done.40.refs_1_, bf16[512,2688]{1,0:T(8,128)(2,1)} %get-tuple-element.522.refs_2_.dg_hbm, ...), custom_call_target="tpu_custom_call" | custom-call | flops 1 | bytes 1 | tf_op jit(solution)/shard_map/grad_y/pallas_call | solution.py:88
  257.7 7.3 %grad_x.4 = (bf16[256,2688]{1,0:T(8,128)(2,1)}, bf16[256,2688]{1,0:T(8,128)(2,1)}) custom-call(s32[8]{0:T(128)} %fusion.25.perm, bf16[512,1024]{1,0:T(8,128)(2,1)} %get-tuple-element.520.b_hbm.refs_0_, bf16[512,1024]{1,0:T(8,128)(2,1)} %collective-permute-done.40.refs_1_, bf16[512,2688]{1,0:T(8,128)(2,1)} %get-tuple-element.525.refs_2_.du_hbm, ...), custom_call_target="tpu_custom_call" | custom-call | flops 1 | bytes 1 | tf_op jit(solution)/shard_map/grad_x/pallas_call | solution.py:88
  265.1 16.6 %dmiddle.1 = (f32[512,1024]{1,0:T(8,128)}, bf16[512,1024]{1,0:T(8,128)(2,1)}, bf16[512,1024]{1,0:T(8,128)(2,1)}, f32[1,1024]{1,0:T(1,128)}) custom-call(s32[8]{0:T(128)} %fusion.25.perm, f32[8,1024]{1,0:T(8,128)} %get-tuple-element.485.gains_ref, f32[512,1]{1,0:T(8,128)} %copy.108.refs_0_.keep_ref, bf16[512,1024]{1,0:T(8,128)(2,1)} %bitcast.155, ...), custom_call_target="tpu_custom_call" | custom-call | flops 1 | bytes 1 | tf_op jit(solution)/shard_map/dmiddle/pallas_call | solution.py:88
  284.3 9.1 %down.1 = bf16[512,1024]{1,0:T(8,128)(2,1)} custom-call(s32[8]{0:T(128)} %fusion.25.perm, f32[512,1]{1,0:T(8,128)} %copy.108.refs_0_.keep_ref, f32[512,1024]{1,0:T(8,128)} %get-tuple-element.493.h1_hbm, bf16[512,2688]{1,0:T(8,128)(2,1)} %get-tuple-element.516.refs_4_.m_hbm, bf16[128,2688]{1,0:T(8,128)(2,1)} %bitcast.16.rest_0_, ...), custom_call_target="tpu_custom_call" | custom-call | flops 1 | bytes 1 | tf_op jit(solution)/shard_map/down/pallas_call | solution.py:88
  308.7 18.2 %dattend.2 = (bf16[512,512]{1,0:T(8,128)(2,1)}, f32[512,512]{1,0:T(8,128)}, f32[512,512]{1,0:T(8,128)}, bf16[512,512]{1,0:T(8,128)(2,1)}, bf16[512,512]{1,0:T(8,128)(2,1)}) custom-call(s32[8]{0:T(128)} %fusion.25.perm, s32[1024,1]{1,0:T(8,128)} %copy.114.segk_ref, s32[1,512]{1,0:T(1,128)} %bitcast.170, bf16[512,1024]{1,0:T(8,128)(2,1)} %get-tuple-element.452.q_ref, ...), custom_call_target="tpu_custom_call" | custom-call | flops 1 | bytes 1 | tf_op jit(solution)/shard_map/dattend/pallas_call | solution.py:577
  335.0 6.5 %dqkv.2.refs_2_.da_hbm = bf16[512,1536]{1,0:T(8,128)(2,1)} custom-call(s32[8]{0:T(128)} %fusion.25.perm, f32[512,128]{1,0:T(8,128)} %get-tuple-element.370.cos_ref, f32[512,128]{1,0:T(8,128)} %get-tuple-element.371.sin_ref, bf16[512,512]{1,0:T(8,128)(2,1)} %get-tuple-element.541.dq_ref, f32[512,512]{1,0:T(8,128)} %get-tuple-element.545.dk0_ref, ...), custom_call_target="tpu_custom_call" | custom-call | flops 1 | bytes 1 | tf_op jit(solution)/shard_map/dqkv/pallas_call | solution.py:627
  346.5 18.4 %dattend.3 = (bf16[512,512]{1,0:T(8,128)(2,1)}, f32[512,512]{1,0:T(8,128)}, f32[512,512]{1,0:T(8,128)}, bf16[512,512]{1,0:T(8,128)(2,1)}, bf16[512,512]{1,0:T(8,128)(2,1)}) custom-call(s32[8]{0:T(128)} %fusion.25.perm, s32[1024,1]{1,0:T(8,128)} %copy.114.segk_ref, s32[1,512]{1,0:T(1,128)} %bitcast.171, bf16[512,1024]{1,0:T(8,128)(2,1)} %get-tuple-element.452.q_ref, ...), custom_call_target="tpu_custom_call" | custom-call | flops 1 | bytes 1 | tf_op jit(solution)/shard_map/dattend/pallas_call | solution.py:577
  366.6 5.7 %grad_y.6 = (bf16[256,1536]{1,0:T(8,128)(2,1)}, bf16[256,1536]{1,0:T(8,128)(2,1)}) custom-call(s32[8]{0:T(128)} %fusion.25.perm, bf16[512,1024]{1,0:T(8,128)(2,1)} %get-tuple-element.508.refs_0_, bf16[512,1024]{1,0:T(8,128)(2,1)} %collective-permute-done.41.refs_1_, bf16[512,1536]{1,0:T(8,128)(2,1)} %dqkv.2.refs_2_.da_hbm, bf16[512,1536]{1,0:T(8,128)(2,1)} %copy-done.33), custom_call_target="tpu_custom_call" | custom-call | flops 1 | bytes 1 | tf_op jit(solution)/shard_map/grad_y/pallas_call | solution.py:88
  378.8 6.6 %dqkv.3.db_hbm.refs_2_ = bf16[512,1536]{1,0:T(8,128)(2,1)} custom-call(s32[8]{0:T(128)} %fusion.25.perm, f32[512,128]{1,0:T(8,128)} %get-tuple-element.370.cos_ref, f32[512,128]{1,0:T(8,128)} %get-tuple-element.371.sin_ref, bf16[512,512]{1,0:T(8,128)(2,1)} %get-tuple-element.554.dq_ref, f32[512,512]{1,0:T(8,128)} %get-tuple-element.563.dk0_ref, ...), custom_call_target="tpu_custom_call" | custom-call | flops 1 | bytes 1 | tf_op jit(solution)/shard_map/dqkv/pallas_call | solution.py:627
  397.9 10.5 %dinput.1 = (bf16[512,1024]{1,0:T(8,128)(2,1)}, f32[1,1024]{1,0:T(1,128)}) custom-call(s32[8]{0:T(128)} %fusion.25.perm, f32[8,1024]{1,0:T(8,128)} %get-tuple-element.485.gains_ref, bf16[512,1024]{1,0:T(8,128)(2,1)} %bitcast.151, f32[512,1024]{1,0:T(8,128)} %get-tuple-element.528.dh1_hbm, bf16[512,1536]{1,0:T(8,128)(2,1)} %dqkv.2.refs_2_.da_hbm, ...), custom_call_target="tpu_custom_call" | custom-call | flops 1 | bytes 1 | tf_op jit(solution)/shard_map/dinput/pallas_call | solution.py:88
  435.1 5.1 %collective-permute-done.65 = f32[2,1024]{0,1:T(8,128)} collective-permute-done((f32[2,1024]{0,1:T(8,128)S(1)}, f32[2,1024]{0,1:T(8,128)}, u32[]{:S(2)}, u32[]{:S(2)}) %collective-permute-start.65) | collective-permute-done | bytes 8224 | tf_op jit(solution)/shard_map/ppermute | solution.py:798
  466.7 10.7 %all-to-all-done.5 = bf16[4,32,1664]{2,1,0:T(8,128)(2,1)S(1)} async-done(((bf16[4,32,1664]{2,1,0:T(8,128)(2,1)}), bf16[4,32,1664]{2,1,0:T(8,128)(2,1)S(1)}, u32[]{:S(2)}, u32[]{:S(2)}) %all-to-all-start.5) | async-done | bytes 426016 | tf_op jit(solution)/shard_map/all_to_all | solution.py:804
  (383 shorter events, 202.4 us)
Async XLA Ops:
  7.2 66.3 %all-gather.2.cloned.1.call-start = ((), (), s32[]{:S(2)}) async-start(), calls=%async_computation.10 | async-start | bytes 2048000 | tf_op jit(solution)/shard_map/all_gather | solution.py:867
  8.6 23.9 %collective-permute-start = (bf16[2,128,1024]{2,1,0:T(8,128)(2,1)S(1)}, bf16[2,128,1024]{2,1,0:T(8,128)(2,1)S(1)}, u32[]{:S(2)}, u32[]{:S(2)}) collective-permute-start(bf16[2,128,1024]{2,1,0:T(8,128)(2,1)S(1)} %get-tuple-element.601), channel_id=1, source_target_pairs={{0,4},{4,0},{8,12},{12,8},{16,20},{20,16},{24,28},{28,24},{1,5},{5... | collective-permute-start | bytes 1572872 | tf_op jit(solution)/shard_map/ppermute | solution.py:798
  76.0 29.8 %all-to-all-start = ((bf16[4,128,1024]{2,1,0:T(8,128)(2,1)}), bf16[4,128,1024]{2,1,0:T(8,128)(2,1)S(1)}, u32[]{:S(2)}, u32[]{:S(2)}) async-start(bf16[4,128,1024]{2,1,0:T(8,128)(2,1)} %bitcast.7), calls=%async_computation | async-start | bytes 2097152 | tf_op jit(solution)/shard_map/all_to_all | solution.py:804
  119.3 25.8 %collective-permute-start.17 = (bf16[512,2048]{1,0:T(8,128)(2,1)}, bf16[512,2048]{1,0:T(8,128)(2,1)S(1)}, u32[]{:S(2)}, u32[]{:S(2)}) collective-permute-start(bf16[512,2048]{1,0:T(8,128)(2,1)} %get-tuple-element.453.k0_ref.v0_ref), channel_id=1, source_target_pairs={{0,4},{4,0},{8,12},{12,8},{16,20},{20,16},{24,28},{28,24},{1,5},{5... | collective-permute-start | bytes 6291464 | tf_op jit(solution)/shard_map/ppermute | solution.py:798
  119.5 23.6 %collective-permute-start.18 = (bf16[128,3712]{1,0:T(8,128)(2,1)S(1)}, bf16[128,3712]{1,0:T(8,128)(2,1)}, u32[]{:S(2)}, u32[]{:S(2)}) collective-permute-start(bf16[128,3712]{1,0:T(8,128)(2,1)S(1)} %slice.221.rest_0_), channel_id=1, source_target_pairs={{0,16},{4,20},{8,24},{12,28},{16,0},{20,4},{24,8},{28,12},{1,17},{... | collective-permute-start | bytes 2850824 | tf_op jit(solution)/shard_map/ppermute | solution.py:798
  121.8 23.3 %all-to-all-start.1 = ((bf16[4,32,2688]{2,1,0:T(8,128)(2,1)}), bf16[4,32,2688]{2,1,0:T(8,128)(2,1)}, u32[]{:S(2)}, u32[]{:S(2)}) async-start(bf16[4,32,2688]{2,1,0:T(8,128)(2,1)} %broadcast_in_dim.23), calls=%async_computation.1 | async-start | bytes 1376256 | tf_op jit(solution)/shard_map/all_to_all | solution.py:804
  192.1 30.4 %all-to-all-start.2 = ((bf16[4,128,1024]{2,1,0:T(8,128)(2,1)}), bf16[4,128,1024]{2,1,0:T(8,128)(2,1)S(1)}, u32[]{:S(2)}, u32[]{:S(2)}) async-start(bf16[4,128,1024]{2,1,0:T(8,128)(2,1)} %bitcast.162), calls=%async_computation.2 | async-start | bytes 2097152 | tf_op jit(solution)/shard_map/all_to_all | solution.py:804
  196.4 24.2 %collective-permute-start.33 = (bf16[128,2688]{1,0:T(8,128)(2,1)}, bf16[128,2688]{1,0:T(8,128)(2,1)}, u32[]{:S(2)}, u32[]{:S(2)}) collective-permute-start(bf16[128,2688]{1,0:T(8,128)(2,1)} %collective-permute-done.27.rest_2_), channel_id=1, source_target_pairs={{0,8},{4,12},{8,0},{12,4},{16,24},{20,28},{24,16},{28,20},{1,9},{5... | collective-permute-start | bytes 2064392 | tf_op jit(solution)/shard_map/ppermute | solution.py:798
  246.6 46.7 %collective-permute-start.46 = (bf16[256,2688]{1,0:T(8,128)(2,1)}, bf16[256,2688]{1,0:T(8,128)(2,1)}, u32[]{:S(2)}, u32[]{:S(2)}) collective-permute-start(bf16[256,2688]{1,0:T(8,128)(2,1)} %get-tuple-element.518), channel_id=1, source_target_pairs={{0,8},{4,12},{8,0},{12,4},{16,24},{20,28},{24,16},{28,20},{1,9},{5... | collective-permute-start | bytes 4128776 | tf_op jit(solution)/shard_map/ppermute | solution.py:798
  254.9 50.8 %collective-permute-start.45 = (bf16[256,2688]{1,0:T(8,128)(2,1)}, bf16[256,2688]{1,0:T(8,128)(2,1)}, u32[]{:S(2)}, u32[]{:S(2)}) collective-permute-start(bf16[256,2688]{1,0:T(8,128)(2,1)} %get-tuple-element.523), channel_id=1, source_target_pairs={{0,16},{4,20},{8,24},{12,28},{16,0},{20,4},{24,8},{28,12},{1,17},{... | collective-permute-start | bytes 4128776 | tf_op jit(solution)/shard_map/ppermute | solution.py:798
  282.8 44.1 %collective-permute-start.50 = (bf16[256,2688]{1,0:T(8,128)(2,1)}, bf16[256,2688]{1,0:T(8,128)(2,1)S(1)}, u32[]{:S(2)}, u32[]{:S(2)}) collective-permute-start(bf16[256,2688]{1,0:T(8,128)(2,1)} %get-tuple-element.526), channel_id=1, source_target_pairs={{0,8},{4,12},{8,0},{12,4},{16,24},{20,28},{24,16},{28,20},{1,9},{5... | collective-permute-start | bytes 4128776 | tf_op jit(solution)/shard_map/ppermute | solution.py:798
  295.5 31.6 %collective-permute-start.49 = (bf16[128,2688]{1,0:T(8,128)(2,1)}, bf16[128,2688]{1,0:T(8,128)(2,1)}, u32[]{:S(2)}, u32[]{:S(2)}) collective-permute-start(bf16[128,2688]{1,0:T(8,128)(2,1)} %add_convert_fusion.5), channel_id=1, source_target_pairs={{0,16},{4,20},{8,24},{12,28},{16,0},{20,4},{24,8},{28,12},{1,17},{... | collective-permute-start | bytes 2064392 | tf_op jit(solution)/shard_map/ppermute | solution.py:798
  296.1 45.5 %all-to-all-start.3 = ((bf16[4,128,1024]{2,1,0:T(8,128)(2,1)}), bf16[4,128,1024]{2,1,0:T(8,128)(2,1)S(1)}, u32[]{:S(2)}, u32[]{:S(2)}) async-start(bf16[4,128,1024]{2,1,0:T(8,128)(2,1)} %bitcast.24), calls=%async_computation.3 | async-start | bytes 2097152 | tf_op jit(solution)/shard_map/all_to_all | solution.py:804
  299.6 65.4 %reduce-scatter.5.cloned.1.call-start = ((), (), s32[]{:S(2)}) async-start(), calls=%async_computation.11 | async-start | bytes 860160 | tf_op jit(solution)/shard_map/reduce_scatter | solution.py:1021
  307.8 33.9 %collective-permute-start.48 = (bf16[128,2688]{1,0:T(8,128)(2,1)}, bf16[128,2688]{1,0:T(8,128)(2,1)}, u32[]{:S(2)}, u32[]{:S(2)}) collective-permute-start(bf16[128,2688]{1,0:T(8,128)(2,1)} %add_convert_fusion.4), channel_id=1, source_target_pairs={{0,8},{4,12},{8,0},{12,4},{16,24},{20,28},{24,16},{28,20},{1,9},{5... | collective-permute-start | bytes 2064392 | tf_op jit(solution)/shard_map/ppermute | solution.py:798
  331.2 47.6 %reduce-scatter.7.cloned.1.call-start = ((), (), s32[]{:S(2)}) async-start(), calls=%async_computation.12 | async-start | bytes 860160 | tf_op jit(solution)/shard_map/reduce_scatter | solution.py:1021
  341.5 24.0 %collective-permute-start.55 = (bf16[512,1536]{1,0:T(8,128)(2,1)}, bf16[512,1536]{1,0:T(8,128)(2,1)S(1)}, u32[]{:S(2)}, u32[]{:S(2)}) collective-permute-start(bf16[512,1536]{1,0:T(8,128)(2,1)} %dqkv.2.refs_2_.da_hbm), channel_id=1, source_target_pairs={{0,4},{4,0},{8,12},{12,8},{16,20},{20,16},{24,28},{28,24},{1,5},{5... | collective-permute-start | bytes 4718600 | tf_op jit(solution)/shard_map/ppermute | solution.py:798
  344.4 110.1 %reduce-scatter.11.cloned.1.call-start = ((), (), s32[]{:S(2)}) async-start(), calls=%async_computation.14 | async-start | bytes 1187840 | tf_op jit(solution)/shard_map/reduce_scatter | solution.py:1021
  344.4 29.3 %collective-permute-start.57 = (bf16[256,1024]{1,0:T(8,128)(2,1)}, bf16[256,1024]{1,0:T(8,128)(2,1)}, u32[]{:S(2)}, u32[]{:S(2)}) collective-permute-start(bf16[256,1024]{1,0:T(8,128)(2,1)} %get-tuple-element.536), channel_id=1, source_target_pairs={{0,16},{4,20},{8,24},{12,28},{16,0},{20,4},{24,8},{28,12},{1,17},{... | collective-permute-start | bytes 1572872 | tf_op jit(solution)/shard_map/ppermute | solution.py:798
  345.8 39.6 %collective-permute-start.56 = (bf16[128,2688]{1,0:T(8,128)(2,1)S(1)}, bf16[128,2688]{1,0:T(8,128)(2,1)}, u32[]{:S(2)}, u32[]{:S(2)}) collective-permute-start(bf16[128,2688]{1,0:T(8,128)(2,1)S(1)} %add_convert_fusion.3), channel_id=1, source_target_pairs={{0,16},{4,20},{8,24},{12,28},{16,0},{20,4},{24,8},{28,12},{1,17},{... | collective-permute-start | bytes 2064392 | tf_op jit(solution)/shard_map/ppermute | solution.py:798
  385.4 32.8 %collective-permute-start.61 = (bf16[512,1536]{1,0:T(8,128)(2,1)}, bf16[512,1536]{1,0:T(8,128)(2,1)S(1)}, u32[]{:S(2)}, u32[]{:S(2)}) collective-permute-start(bf16[512,1536]{1,0:T(8,128)(2,1)} %dqkv.3.db_hbm.refs_2_), channel_id=1, source_target_pairs={{0,4},{4,0},{8,12},{12,8},{16,20},{20,16},{24,28},{28,24},{1,5},{5... | collective-permute-start | bytes 4718600 | tf_op jit(solution)/shard_map/ppermute | solution.py:798
  394.1 39.0 %collective-permute-start.64 = (bf16[128,1536]{1,0:T(8,128)(2,1)}, bf16[128,1536]{1,0:T(8,128)(2,1)}, u32[]{:S(2)}, u32[]{:S(2)}) collective-permute-start(bf16[128,1536]{1,0:T(8,128)(2,1)} %add_convert_fusion.7), channel_id=1, source_target_pairs={{0,8},{4,12},{8,0},{12,4},{16,24},{20,28},{24,16},{28,20},{1,9},{5... | collective-permute-start | bytes 1179656 | tf_op jit(solution)/shard_map/ppermute | solution.py:798
  413.0 43.6 %all-to-all-start.4 = ((bf16[4,128,1024]{2,1,0:T(8,128)(2,1)}), bf16[4,128,1024]{2,1,0:T(8,128)(2,1)S(1)}, u32[]{:S(2)}, u32[]{:S(2)}) async-start(bf16[4,128,1024]{2,1,0:T(8,128)(2,1)} %bitcast.164), calls=%async_computation.6 | async-start | bytes 2097152 | tf_op jit(solution)/shard_map/all_to_all | solution.py:804
  418.0 46.7 %reduce-scatter.9.cloned.1.call-start = ((), (), s32[]{:S(2)}) async-start(), calls=%async_computation.13 | async-start | bytes 491520 | tf_op jit(solution)/shard_map/reduce_scatter | solution.py:1021
  (122 other events, 1366.3 us)
Sparse Core Ops, SparseCore 0:
  32.7 37.9 all-gather.1
  331.3 23.5 reduce-scatter.4
  357.3 21.3 reduce-scatter.6
  389.2 24.5 reduce-scatter.10
  442.8 21.8 reduce-scatter.8

commit v4 on v3

--- a/solution.py
+++ b/solution.py
@@ -178,15 +178,14 @@
     )
 
 
-def attend_body(given, perm, segk_ref, segq_ref, q_ref, k0_ref, k1_ref, v0_ref, v1_ref, *rest):
-    o_ref, lse_ref, bias, vt = rest[given:]
+def attend_body(perm, segk_ref, segq_ref, q_ref, k0_ref, k1_ref, v0_ref, v1_ref, o_ref, p_ref, bias, vt):
     j = pl.program_id(0)
     rows = q_ref.shape[0]
-    tile = 256
+    tile = min(512, rows)
 
     @pl.when(j == 0)
     def _():
-        bias[...] = jnp.where(segk_ref[...] == segq_ref[...], 0.0, NEG)
+        bias[...] = jnp.where(segk_ref[:, :1] == segq_ref[...], 0.0, NEG)
 
     for i in range(rows // LANE):
         r = slice(i * LANE, (i + 1) * LANE)
@@ -205,60 +204,63 @@
             e = jnp.exp2(s - top)
             total = jnp.sum(e, axis=0, keepdims=True)
             p = (e * (1.0 / total)).astype(BF16)
-            ot = nn(vt[...], p)
-            parts.append(ot[h * HEAD : (h + 1) * HEAD, :])
-            lse_ref[0, h : h + 1, cols] = top + jnp.log2(total)
+            p_ref[0, h, :, cols] = p
+            parts.append(nn(vt[...], p)[h * HEAD : (h + 1) * HEAD, :])
         o_ref[cols, :] = jnp.concatenate(parts, axis=0).T.astype(BF16)
 
 
-def attend_call(perm, segk, segq, q, kv0, kv1, first, count, given=()):
+def attend_call(perm, segk, segq, q, kv0, kv1, first, count):
     rows, width = q.shape
     pairs = width // LANE
     full = lambda j: (0, 0)
     at = lambda j: (0, first + j)
     vat = lambda j: (0, pairs + first + j)
     block = (rows, LANE)
+    heads = LANE // HEAD
     return pl.pallas_call(
-        functools.partial(attend_body, len(given)),
+        attend_body,
         grid=(count,),
-        out_shape=(sds((rows, width), BF16), sds((pairs, 8, rows), F32)),
+        out_shape=(sds((rows, count * LANE), BF16), sds((count, heads, 2 * rows, rows), BF16)),
         in_specs=[
             SMEM,
-            pl.BlockSpec((2 * rows, 1), full),
+            pl.BlockSpec((2 * rows, LANE), full),
             pl.BlockSpec((1, rows), full),
             pl.BlockSpec(block, at),
             pl.BlockSpec(block, at),
             pl.BlockSpec(block, at),
             pl.BlockSpec(block, vat),
             pl.BlockSpec(block, vat),
-        ]
-        + [ANY] * len(given),
-        out_specs=(pl.BlockSpec(block, at), pl.BlockSpec((1, 8, rows), lambda j: (first + j, 0, 0))),
+        ],
+        out_specs=(
+            pl.BlockSpec(block, lambda j: (0, j)),
+            pl.BlockSpec((1, heads, 2 * rows, rows), lambda j: (j, 0, 0, 0)),
+        ),
         scratch_shapes=[pltpu.VMEM((2 * rows, rows), F32), pltpu.VMEM((LANE, 2 * rows), BF16)],
-        input_output_aliases={8 + i: i for i in range(len(given))},
         compiler_params=params(),
         cost_estimate=COST,
         name="attend",
-    )(perm, segk, segq, q, kv0, kv1, kv0, kv1, *given)
-
-
-def middle_body(n, perm, gains_ref, keep_ref, x_hbm, o_hbm, *rest):
+    )(perm, segk, segq, q, kv0, kv1, kv0, kv1)
+
+
+def middle_body(n, perm, gains_ref, keep_ref, x_hbm, oa_hbm, ob_hbm, *rest):
     pieces = rest[:n]
-    h1_hbm, b_hbm, x, o, op, w, h1, b, sems = rest[n:]
+    h1_hbm, b_hbm, o_hbm, x, o, op, w, h1, b, sems = rest[n:]
     move = Copies(sems)
     rows, width = x.shape
-    got = move.start(o_hbm, o) + move.weight(pieces, 0, width, w) + move.start(x_hbm, x)
-    wait(got[:1])
+    half = width // 2
+    got = move.start(oa_hbm, o.at[:, :half]) + move.start(ob_hbm, o.at[:, half:])
+    got += move.weight(pieces, 0, width, w) + move.start(x_hbm, x)
+    wait(got[:2])
+    done = move.start(o, o_hbm)
     for m in range(width // LANE):
         op[:, m * LANE : (m + 1) * LANE] = o[:, lanes(perm, m)]
-    wait(got[1:])
-    done = []
+    wait(got[2:])
     for t in range(2):
         base = t * (rows // 2)
 
         def tile(i, carry, base=base):
             r = pl.ds(pl.multiple_of(base + i * LANE, LANE), LANE)
-            v = x[r, :].astype(F32) + keep_ref[r, :] * nn(op[r, :], w[...])
+            v = x[r, :].astype(F32) + keep_ref[r, :1] * nn(op[r, :], w[...])
             h1[r, :] = v
             normed, _ = norm_rows(v)
             b[r, :] = (normed * gains_ref[1:2, :]).astype(BF16)
@@ -270,14 +272,14 @@
     wait(done)
 
 
-def middle_call(perm, gains, x, keep, o, pieces):
+def middle_call(perm, gains, x, keep, oa, ob, pieces):
     rows, width = x.shape
     return call(
         functools.partial(middle_body, len(pieces)),
         perm,
         [gains, keep],
-        [x, o, *pieces],
-        [sds((rows, width), F32), sds((rows, width), BF16)],
+        [x, oa, ob, *pieces],
+        [sds((rows, width), F32), sds((rows, width), BF16), sds((rows, width), BF16)],
         [
             pltpu.VMEM((rows, width), BF16),
             pltpu.VMEM((rows, width), BF16),
@@ -286,7 +288,7 @@
             pltpu.VMEM((rows, width), F32),
             pltpu.VMEM((rows, width), BF16),
         ],
-        6 + len(pieces),
+        8 + len(pieces),
         "middle",
     )
 
@@ -337,14 +339,14 @@
     )
 
 
-def dgate_body(n, perm, keep_ref, cot_hbm, f1_hbm, f2_hbm, *rest):
+def dgate_body(n, perm, keep_ref, cot_hbm, f1_hbm, f2_hbm, h1_hbm, m_hbm, *rest):
     pd = rest[:n]
-    dg_hbm, du_hbm, cot, ep, wd, f1, f2, sems = rest[n:]
+    dg_hbm, du_hbm, out_hbm, cot, ep, wd, f1, f2, h1, mv, acc, out, sems = rest[n:]
     move = Copies(sems)
     rows, width = cot.shape
     parts = chunks(f1.shape[1])
     got_cot = move.start(cot_hbm, cot)
-    got = []
+    got, got_m = [], []
     for c, k in parts:
         cols = slice(c, c + k)
         got.append(
@@ -352,6 +354,9 @@
             + move.start(f1_hbm.at[:, cols], f1.at[:, cols])
             + move.start(f2_hbm.at[:, cols], f2.at[:, cols])
         )
+    for c, k in parts:
+        got_m.append(move.start(m_hbm.at[:, c : c + k], mv.at[:, c : c + k]))
+    got_h1 = move.start(h1_hbm, h1)
     wait(got_cot)
     for m in range(width // LANE):
         ep[:, m * LANE : (m + 1) * LANE] = (keep_ref[...] * cot[:, lanes(perm, m)].astype(F32)).astype(BF16)
@@ -367,69 +372,44 @@
 
         row_tiles(rows, 256, tile)
         done += move.start(f1.at[:, cols], dg_hbm.at[:, cols]) + move.start(f2.at[:, cols], du_hbm.at[:, cols])
+    for i, ((c, k), g) in enumerate(zip(parts, got_m)):
+        cols = slice(c, c + k)
+        wait(g)
+
+        def add(r, cols=cols, i=i):
+            v = nt(mv[r, cols], wd[:, cols])
+            acc[r, :] = v if i == 0 else acc[r, :] + v
+
+        row_tiles(rows, 256, add)
+    wait(got_h1)
+    for m in range(width // LANE):
+        at = lanes(perm, m)
+        out[:, at] = (h1[:, at] + keep_ref[...] * acc[:, m * LANE : (m + 1) * LANE]).astype(BF16)
+    done += move.start(out, out_hbm)
     wait(done)
 
 
-def dgate_call(perm, cot, keep, f1, f2, pd):
+def dgate_call(perm, cot, keep, f1, f2, h1, mixed, pd):
     rows, width = cot.shape
     hidden = f1.shape[1]
     return call(
         functools.partial(dgate_body, len(pd)),
         perm,
         [keep],
-        [cot, f1, f2, *pd],
-        [sds((rows, hidden), BF16)] * 2,
-        [pltpu.VMEM((rows, width), BF16)] * 2 + [pltpu.VMEM((width, hidden), BF16)] + [pltpu.VMEM((rows, hidden), BF16)] * 2,
-        1 + len(chunks(hidden)) * (len(pd) + 4),
+        [cot, f1, f2, h1, mixed, *pd],
+        [sds((rows, hidden), BF16)] * 2 + [sds((rows, width), BF16)],
+        [pltpu.VMEM((rows, width), BF16)] * 2
+        + [pltpu.VMEM((width, hidden), BF16)]
+        + [pltpu.VMEM((rows, hidden), BF16)] * 2
+        + [
+            pltpu.VMEM((rows, width), F32),
+            pltpu.VMEM((rows, hidden), BF16),
+            pltpu.VMEM((rows, width), F32),
+            pltpu.VMEM((rows, width), BF16),
+        ],
+        3 + len(chunks(hidden)) * (len(pd) + 5),
         "dgate",
     )
-
-
-def down_body(n, perm, keep_ref, h1_hbm, m_hbm, *rest):
-    pd = rest[:n]
-    out_hbm, h1, mv, wd, acc, out, sems = rest[n:]
-    move = Copies(sems)
-    rows, width = h1.shape
-    parts = chunks(mv.shape[1])
-    got = [
-        move.start(m_hbm.at[:, c : c + k], mv.at[:, c : c + k]) + move.weight(pd, c, k, wd) for c, k in parts
-    ]
-    got_h1 = move.start(h1_hbm, h1)
-    for i, ((c, k), g) in enumerate(zip(parts, got)):
-        cols = slice(c, c + k)
-        wait(g)
-
-        def tile(r, cols=cols, i=i):
-            v = nt(mv[r, cols], wd[:, cols])
-            acc[r, :] = v if i == 0 else acc[r, :] + v
-
-        row_tiles(rows, 256, tile)
-    wait(got_h1)
-    for m in range(width // LANE):
-        at = lanes(perm, m)
-        out[:, at] = (h1[:, at] + keep_ref[...] * acc[:, m * LANE : (m + 1) * LANE]).astype(BF16)
-    wait(move.start(out, out_hbm))
-
-
-def down_call(perm, h1, keep, mixed, pd):
-    rows, width = h1.shape
-    hidden = mixed.shape[1]
-    return call(
-        functools.partial(down_body, len(pd)),
-        perm,
-        [keep],
-        [h1, mixed, *pd],
-        [sds((rows, width), BF16)],
-        [
-            pltpu.VMEM((rows, width), F32),
-            pltpu.VMEM((rows, hidden), BF16),
-            pltpu.VMEM((width, hidden), BF16),
-            pltpu.VMEM((rows, width), F32),
-            pltpu.VMEM((rows, width), BF16),
-        ],
-        2 + len(chunks(hidden)) * (len(pd) + 1),
-        "down",
-    )[0]
 
 
 def norm_back(e, gain, normed, inv):
@@ -479,7 +459,7 @@
             gg[...] += jnp.sum(v * normed, axis=0, keepdims=True)
             dh1 = cot[r, :].astype(F32) + norm_back(v, gains_ref[1:2, :], normed, inv)
             db[r, :] = dh1
-            e[r, :] = (keep_ref[r, :] * dh1).astype(BF16)
+            e[r, :] = (keep_ref[r, :1] * dh1).astype(BF16)
             return carry
 
         lax.fori_loop(0, rows // 2 // LANE, back, 0)
@@ -521,22 +501,16 @@
     )
 
 
-def dattend_body(perm, segk_ref, segq_ref, q_ref, k0_ref, k1_ref, v0_ref, v1_ref, do_ref, lse_ref, *rest):
-    dq_ref, dk0_ref, dv0_ref, dk1_ref, dv1_ref, bias, kt, dk, dv = rest
-    j = pl.program_id(0)
+def dattend_body(
+    perm, q_ref, k0_ref, k1_ref, v0_ref, v1_ref, do_ref, p_ref, dq_ref, dk0_ref, dv0_ref, dk1_ref, dv1_ref, kt, dk, dv
+):
     rows = q_ref.shape[0]
-    tile = 256
-
-    @pl.when(j == 0)
-    def _():
-        bias[...] = jnp.where(segk_ref[...] == segq_ref[...], 0.0, NEG)
-
+    tile = min(512, rows)
     for i in range(rows // LANE):
         r = slice(i * LANE, (i + 1) * LANE)
         kt[:, r] = k0_ref[r, :].astype(F32).T.astype(BF16)
         kt[:, rows + i * LANE : rows + (i + 1) * LANE] = k1_ref[r, :].astype(F32).T.astype(BF16)
     head_of = lax.broadcasted_iota(jnp.int32, (1, LANE), 1) // HEAD
-    scale = LOG2E / math.sqrt(HEAD)
     back = 1.0 / math.sqrt(HEAD)
     for t in range(rows // tile):
         cols = slice(t * tile, (t + 1) * tile)
@@ -546,12 +520,12 @@
         for h in range(LANE // HEAD):
             qm = jnp.where(head_of == h, q, jnp.zeros_like(q))
             dom = jnp.where(head_of == h, do, jnp.zeros_like(do))
-            s = jnp.concatenate([nt(k0_ref[...], qm), nt(k1_ref[...], qm)], axis=0) * scale + bias[:, cols]
-            p = jnp.exp2(s - lse_ref[0, h : h + 1, cols])
+            p = p_ref[0, h, :, cols]
+            pf = p.astype(F32)
             dp = jnp.concatenate([nt(v0_ref[...], dom), nt(v1_ref[...], dom)], axis=0)
-            inner = jnp.sum(p * dp, axis=0, keepdims=True)
-            ds = (p * (dp - inner)).astype(BF16)
-            dv_new = nn(p.astype(BF16), dom)
+            inner = jnp.sum(pf * dp, axis=0, keepdims=True)
+            ds = (pf * (dp - inner)).astype(BF16)
+            dv_new = nn(p, dom)
             dk_new = nn(ds, qm)
             if t == 0 and h == 0:
                 dv[...] = dv_new
@@ -567,10 +541,10 @@
     dv1_ref[...] = dv[rows:, :].astype(BF16)
 
 
-def dattend_call(perm, segk, segq, q, kv0, kv1, do, lse, first, count):
+def dattend_call(perm, q, kv0, kv1, do, p, first):
     rows, width = q.shape
     pairs = width // LANE
-    full = lambda j: (0, 0)
+    count = p.shape[0]
     at = lambda j: (0, first + j)
     vat = lambda j: (0, pairs + first + j)
     block = (rows, LANE)
@@ -586,19 +560,16 @@
         ),
         in_specs=[
             SMEM,
-            pl.BlockSpec((2 * rows, 1), full),
-            pl.BlockSpec((1, rows), full),
             pl.BlockSpec(block, at),
             pl.BlockSpec(block, at),
             pl.BlockSpec(block, at),
             pl.BlockSpec(block, vat),
             pl.BlockSpec(block, vat),
             pl.BlockSpec(block, at),
-            pl.BlockSpec((1, 8, rows), lambda j: (first + j, 0, 0)),
+            pl.BlockSpec((1, *p.shape[1:]), lambda j: (j, 0, 0, 0)),
         ],
         out_specs=(pl.BlockSpec(block, lambda j: (0, j)),) * 5,
         scratch_shapes=[
-            pltpu.VMEM((2 * rows, rows), F32),
             pltpu.VMEM((LANE, 2 * rows), BF16),
             pltpu.VMEM((2 * rows, LANE), F32),
             pltpu.VMEM((2 * rows, LANE), F32),
@@ -606,7 +577,7 @@
         compiler_params=params(),
         cost_estimate=COST,
         name="dattend",
-    )(perm, segk, segq, q, kv0, kv1, kv0, kv1, do, lse)
+    )(perm, q, kv0, kv1, kv0, kv1, do, p)
 
 
 def dqkv_body(perm, cos_ref, sin_ref, dq_ref, dk0_ref, dv0_ref, dk1_ref, dv1_ref, out_ref):
@@ -621,7 +592,7 @@
 
 def dqkv_call(perm, cos, sin, dq, dk0, dv0, dk1, dv1):
     rows, width = dq.shape
-    tile = 64
+    tile = 256
     row = lambda i: (i, 0)
     block = pl.BlockSpec((tile, width), row)
     return pl.pallas_call(
@@ -702,72 +673,74 @@
     )
 
 
-def grad_body(masked, form, col, perm, *refs):
-    count = 2 if form != "f" else 1
+def grad_body(masked, forms, col, perm, *refs):
+    count = 2 if forms[0] != "f" else 1
     keeps = refs[: count if masked else 0]
     refs = refs[len(keeps) :]
-    lefts, rights = refs[:count], refs[count : 2 * count]
-    outs = refs[2 * count : -4]
+    lefts, rights = refs[:count], refs[count : count * (1 + len(forms))]
+    outs = refs[count * (1 + len(forms)) : -4]
     left, right, out, sems = refs[-4:]
+    per = len(outs) // len(forms)
     move = Copies(sems)
     height, width = left.shape[2], right.shape[2]
     parts = chunks(width)
-    got_left, got = [], [[] for _ in parts]
-    for s in range(count):
-        got_left.append([])
-        for i in range(height // LANE):
-            got_left[s] += move.start(lefts[s].at[:, lanes(perm, i)], left.at[s, :, i * LANE : (i + 1) * LANE])
-        got[0] += move.start(rights[s].at[:, col : col + parts[0][1]], right.at[s, :, : parts[0][1]])
-    for p, (c, k) in list(enumerate(parts))[1:]:
-        for s in range(count):
-            got[p] += move.start(rights[s].at[:, col + c : col + c + k], right.at[s, :, c : c + k])
+    got_left, got = [[] for _ in range(count)], [[[] for _ in parts] for _ in forms]
+    for f in range(len(forms)):
+        for p, (c, k) in enumerate(parts):
+            for s in range(count):
+                if f == 0 and p == 0:
+                    for i in range(height // LANE):
+                        block = left.at[s, :, i * LANE : (i + 1) * LANE]
+                        got_left[s] += move.start(lefts[s].at[:, lanes(perm, i)], block)
+                source = rights[f * count + s].at[:, col + c : col + c + k]
+                got[f][p] += move.start(source, right.at[f * count + s, :, c : c + k])
     for s in range(count):
         wait(got_left[s])
         if masked:
-            left[s] = (left[s].astype(F32) * keeps[s][...]).astype(BF16)
+            left[s] = (left[s].astype(F32) * keeps[s][:, :1]).astype(BF16)
     done = []
-    for (c, k), g in zip(parts, got):
-        cols = slice(c, c + k)
-        wait(g)
-        for t in range(height // 256):
-            rows = slice(t * 256, (t + 1) * 256)
-            v = tn(left[0, :, rows], right[0, :, cols])
-            for s in range(1, count):
-                v = v + tn(left[s, :, rows], right[s, :, cols])
-            if form == "f":
-                out[0, rows, cols] = v
-            elif form == "x":
-                here = slice(t * LANE, (t + 1) * LANE)
-                out[0, here, cols] = v[LANE:, :].astype(BF16)
-                out[1, here, cols] = v[:LANE, :].astype(BF16)
-            else:
-                out[1 - t, :, cols] = v.astype(BF16)
-        for i, to in enumerate(outs):
-            done += move.start(out.at[i, :, cols], to.at[:, cols])
+    for f, form in enumerate(forms):
+        for (c, k), g in zip(parts, got[f]):
+            cols = slice(c, c + k)
+            wait(g)
+            for t in range(height // 256):
+                rows = slice(t * 256, (t + 1) * 256)
+                v = tn(left[0, :, rows], right[f * count, :, cols])
+                for s in range(1, count):
+                    v = v + tn(left[s, :, rows], right[f * count + s, :, cols])
+                if form == "f":
+                    out[f, rows, cols] = v
+                elif form == "x":
+                    here = slice(t * LANE, (t + 1) * LANE)
+                    out[2 * f, here, cols] = v[LANE:, :].astype(BF16)
+                    out[2 * f + 1, here, cols] = v[:LANE, :].astype(BF16)
+                else:
+                    out[2 * f + 1 - t, :, cols] = v.astype(BF16)
+            for i in range(per * f, per * (f + 1)):
+                done += move.start(out.at[i, :, cols], outs[i].at[:, cols])
     wait(done)
 
 
-def grad_call(perm, sources, col, count, form):
-    rows, width = sources[0][0].shape
-    keeps = [k for _, _, k in sources if k is not None]
-    height = width if form == "f" else width // 2
-    outs = [sds((height, count), F32)] if form == "f" else [sds((height // 2, count), BF16)] * 2
+def grad_call(perm, lefts, rights, keeps, col, count, forms):
+    rows, width = lefts[0].shape
+    full = forms[0] == "f"
+    height = width if full else width // 2
+    outs = ([sds((height, count), F32)] if full else [sds((height // 2, count), BF16)] * 2) * len(forms)
     parts = len(chunks(count))
-    got = call(
-        functools.partial(grad_body, bool(keeps), form, col),
+    return call(
+        functools.partial(grad_body, bool(keeps), forms, col),
         perm,
         keeps,
-        [s[0] for s in sources] + [s[1] for s in sources],
+        [*lefts, *(r for group in rights for r in group)],
         outs,
         [
-            pltpu.VMEM((len(sources), rows, height), BF16),
-            pltpu.VMEM((len(sources), rows, count), BF16),
+            pltpu.VMEM((len(lefts), rows, height), BF16),
+            pltpu.VMEM((len(lefts) * len(forms), rows, count), BF16),
             pltpu.VMEM((len(outs), outs[0].shape[0], count), outs[0].dtype),
         ],
-        len(sources) * (height // LANE + parts) + len(outs) * parts,
-        "grad_" + form,
+        len(lefts) * (height // LANE + parts * len(forms)) + len(outs) * parts,
+        "grad_" + "".join(forms),
     )
-    return got[0] if form == "f" else got
 
 
 def rotary_tables(positions):
@@ -921,38 +894,38 @@
     seg_mine = pick(seg_halves[:, 0], seg_halves[:, 1]).reshape(rows)
     seg_theirs = pick(seg_halves[:, 1], seg_halves[:, 0]).reshape(rows)
     segq = seg_mine.reshape(1, rows)
-    segk = jnp.concatenate([seg_mine, seg_theirs]).reshape(2 * rows, 1)
-    keep = (seg_mine != 0).astype(F32).reshape(rows, 1)
-    keep_theirs = (seg_theirs != 0).astype(F32).reshape(rows, 1)
+    wide = lambda v: jnp.broadcast_to(v[:, None], (v.shape[0], LANE))
+    segk = wide(jnp.concatenate([seg_mine, seg_theirs]))
+    keep, keep_theirs = wide((seg_mine != 0).astype(F32)), wide((seg_theirs != 0).astype(F32))
 
     attn_in, q, kv, gains = qkv_call(perm, x, cos, sin, qkv0, qkv1)
-    kv_other = swap(kv, 1)
     part_one = blocks // 2
     if fast:
         own3 = flat(across(live["down_in"]))
         sync(
-            attn_in=attn_in, q=q, kv=kv, gains=gains, kv_other=kv_other, segq=segq, segk=segk, keep=keep,
+            attn_in=attn_in, q=q, kv=kv, gains=gains, segq=segq, segk=segk, keep=keep,
             keep_theirs=keep_theirs, own3=own3, ya2=swap(live["a2"], 4), xb2=swap(live["b2"], 2),
             ca2=swap(live["a2"], 1), cb2=swap(live["b2"], 1),
         )
+        attn_in, q, kv, gains = (live[k] for k in ("attn_in", "q", "kv", "gains"))
+        segq, segk, perm = live["segq"], live["segk"], live["perm"]
+    kv_other = swap(kv, 1)
+    oa, pa = attend_call(perm, segk, segq, q, kv, kv_other, 0, part_one)
+    if fast:
+        sync(kv_other=kv_other, yxa2=swap(live["xa2"], 4), xyb2=swap(live["yb2"], 2), oa=oa, **{"c" + k: swap(live[k], 1) for k in ("xa2", "yb2")})
+        oa = live["oa"]
         attn_in, q, kv, gains, kv_other = (live[k] for k in ("attn_in", "q", "kv", "gains", "kv_other"))
         segq, segk, perm = live["segq"], live["segk"], live["perm"]
-    some = attend_call(perm, segk, segq, q, kv, kv_other, 0, part_one)
-    if fast:
-        sync(yxa2=swap(live["xa2"], 4), xyb2=swap(live["yb2"], 2), some=some[0], some_lse=some[1], **{"c" + k: swap(live[k], 1) for k in ("xa2", "yb2")})
-        some = (live["some"], live["some_lse"])
-        attn_in, q, kv, gains, kv_other = (live[k] for k in ("attn_in", "q", "kv", "gains", "kv_other"))
-        segq, segk, perm = live["segq"], live["segk"], live["perm"]
-    attended, lse = attend_call(perm, segk, segq, q, kv, kv_other, part_one, blocks - part_one, some)
+    ob, pb = attend_call(perm, segk, segq, q, kv, kv_other, part_one, blocks - part_one)
     if fast:
         cores = {"c" + k: swap(live[k], 1) for k in ("ya2", "xb2", "yxa2")}
         cot_in = join_in(cot_mine, swap(tie(cot_other, live["own3"]), 1))
-        sync(attended=attended, lse=lse, xd=swap(live["own3"], 2), yd=swap(live["own3"], 4), cot_in=cot_in, x=x, **cores)
+        sync(ob=ob, xd=swap(live["own3"], 2), yd=swap(live["own3"], 4), cot_in=cot_in, x=x, **cores)
         rest_a = [live[k] for k in ("a2", "xa2", "ya2", "yxa2", "ca2", "cxa2", "cya2", "cyxa2")]
         rest_b = [live[k] for k in ("b2", "xb2", "yb2", "xyb2", "cb2", "cxb2", "cyb2")]
         rest_b.append(swap(live["xyb2"], 1))
         attn_in, q, kv, gains, kv_other, x = (live[k] for k in ("attn_in", "q", "kv", "gains", "kv_other", "x"))
-        segq, segk, perm, attended, lse = (live[k] for k in ("segq", "segk", "perm", "attended", "lse"))
+        perm, oa, ob = live["perm"], live["oa"], live["ob"]
         keep, keep_theirs = live["keep"], live["keep_theirs"]
         own3, xd, yd = live["own3"], live["xd"], live["yd"]
         cot = flat(across(live["cot_in"]))
@@ -962,21 +935,21 @@
     def pair(v, *after):
         return (v, swap(tie(v, *after), 1) if fast else None)
 
-    h1, mlp_in = middle_call(perm, gains, x, keep, attended, rest_a)
+    h1, mlp_in, attended = middle_call(perm, gains, x, keep, oa, ob, rest_a)
     mixed, f1, f2 = gate_call(perm, mlp_in, rest_a, rest_b, padded, width)
     if fast:
-        h1, mlp_in, mixed, f1, f2, cot, xyd, *cores = sync(
-            h1=h1, mlp_in=mlp_in, mixed=mixed, f1=f1, f2=f2, cot=cot, xyd=xyd,
+        attended, h1, mlp_in, mixed, f1, f2, cot, xyd, *cores = sync(
+            attended=attended, h1=h1, mlp_in=mlp_in, mixed=mixed, f1=f1, f2=f2, cot=cot, xyd=xyd,
             **{"cores%d" % i: v for i, v in enumerate(cores)},
         )
-        attn_in, gains, x, attended, keep, perm = (live[k] for k in ("attn_in", "gains", "x", "attended", "keep", "perm"))
+        attn_in, gains, x, keep, perm = (live[k] for k in ("attn_in", "gains", "x", "keep", "perm"))
         own3, xd, yd = (live[k] for k in ("own3", "xd", "yd"))
         wdown = [own3, xd, yd, xyd, *cores, swap(xyd, 1)]
         others = [swap(tie(v, wdown[-1]), 1) for v in (mixed, cot, mlp_in, attn_in, attended)]
-    dgate, dup = did(dgate_call(perm, cot, keep, f1, f2, wdown))
+    dgate, dup, rows_out = did(dgate_call(perm, cot, keep, f1, f2, h1, mixed, wdown))
     if fast:
-        dgate, dup, mixed_other, cot_other, mlp_other, a_other, o_other = sync(
-            dgate=dgate, dup=dup, **{"other%d" % i: v for i, v in enumerate(others)}
+        dgate, dup, rows_out, mixed_other, cot_other, mlp_other, a_other, o_other = sync(
+            dgate=dgate, dup=dup, rows_out=rows_out, **{"other%d" % i: v for i, v in enumerate(others)}
         )
         perm, cot, mixed, keep, keep_theirs, mlp_in = (
             live[k] for k in ("perm", "cot", "mixed", "keep", "keep_theirs", "mlp_in")
@@ -988,17 +961,15 @@
     dgate_pair, dup_pair = pair(dgate), pair(dup)
 
     class Reduce:
-        def __init__(self, left, right, keeps, col, count, form):
+        def __init__(self, count, form, grads):
             self.count = count
             if not fast:
-                g = did(grad_call(order(perm), [(left[0], right[0], keeps[0])], col, count, "f"))
-                self.out = lax.psum_scatter(g, ("dp", "ctx"), scatter_dimension=0, tiled=True)
+                self.out = lax.psum_scatter(grads[0], ("dp", "ctx"), scatter_dimension=0, tiled=True)
                 return
-            sources = [(left[i], right[i], keeps[i]) for i in range(2)]
-            leave, self.kept = did(grad_call(order(perm), sources, col, count, form))
-            self.first, self.second = (2, 4) if form == "x" else (4, 2)
+            leave, self.kept = grads
+            first, self.second = (2, 4) if form == "x" else (4, 2)
             self.half = leave.shape[0] // 2
-            self.got = swap(leave, self.first)
+            self.got = swap(leave, first)
 
         def two(self):
             if fast:
@@ -1013,76 +984,85 @@
             total = self.kept[:h].astype(F32) + self.got[:h].astype(F32) + got2.astype(F32)
             return did(total.astype(BF16))
 
-        def line(self, other=None):
-            if fast:
-                total = self.three()
-                if other is not None:
-                    total = did(jnp.concatenate([total, other.three()], axis=1))
-                total = lax.psum_scatter(total, "ctx", scatter_dimension=0, tiled=True).astype(F32)
-                self.out = total[:, : self.count]
-                if other is not None:
-                    other.out = total[:, self.count :]
-
-    none = (None, None)
-    r_down = Reduce(cot_pair, mixed_pair, (keep, keep_theirs), 0, padded, "x")
-    r_gate = Reduce(mlp_pair, dgate_pair, none, 0, padded, "y")
-    r_up = Reduce(mlp_pair, dup_pair, none, 0, padded, "x")
+    def finish(first, *some):
+        return tie(first, *(r.out for r in some)) if fast else first
+
+    def reductions(left, rights, keeps, col, count, forms, tied=None):
+        if not fast:
+            got = [did(grad_call(order(perm), left[:1], [r[:1]], keeps[:1], col, count, ("f",))) for r in rights]
+            return [Reduce(count, None, g) for g in got]
+        got = did(grad_call(order(perm) if tied is None else tied, left, rights, keeps, col, count, forms))
+        return [Reduce(count, form, got[2 * i : 2 * i + 2]) for i, form in enumerate(forms)]
+
+    def line(*some):
+        if fast:
+            totals = [r.three() for r in some]
+            total = did(jnp.concatenate(totals, axis=1)) if len(some) > 1 else totals[0]
+            total = lax.psum_scatter(total, "ctx", scatter_dimension=0, tiled=True).astype(F32)
+            at = 0
+            for r in some:
+                r.out = total[:, at : at + r.count]
+                at += r.count
+
+    out_got = across(rows_out.reshape(ctx_count, half_len, width))
+    (r_down,) = reductions(cot_pair, [mixed_pair], [keep, keep_theirs], 0, padded, ("x",))
+    r_gate, r_up = reductions(mlp_pair, [dgate_pair, dup_pair], [], 0, padded, ("y", "x"))
     dh1, e_attn, d_o, gain_two = did(dmiddle_call(order(perm), gains, cot, keep, h1, dgate, dup, rest_a, rest_b, width))
     e_pair = pair(e_attn)
-    rows_out = did(down_call(order(perm), h1, keep, mixed, wdown))
-    out_got = across(rows_out.reshape(ctx_count, half_len, width))
     r_down.two()
-    r_out = Reduce(o_pair, e_pair, none, 0, width, "y")
+    (r_out,) = reductions(o_pair, [e_pair], [], 0, width, ("y",))
+
+    tied, out_got = lax.optimization_barrier((order(perm), out_got))
+    dq, dk0, dv0, dk1, dv1 = did(dattend_call(tied, q, kv, kv_other, d_o, pa, 0))
+    dk_got, dv_got = swap(dk1, 1), swap(dv1, 1)
     r_gate.two()
-    back = lambda first, count: did(dattend_call(order(perm), segk, segq, q, kv, kv_other, d_o, lse, first, count))
-    dq, dk0, dv0, dk1, dv1 = back(0, part_one)
+    da = did(dqkv_call(order(perm), cos, sin, dq, dk0, dv0, dk_got, dv_got))
+    da_pair = pair(da)
+    r_up.two()
+    line(r_down)
+    (r_qkva,) = reductions(in_pair, [da_pair], [], 0, third, ("y",))
+    dq, dk0, dv0, dk1, dv1 = did(dattend_call(order(perm), q, kv, kv_other, d_o, pb, part_one))
     dk_got, dv_got = swap(dk1, 1), swap(dv1, 1)
-    r_up.two()
-    r_down.line()
-    da = did(dqkv_call(order(perm), cos, sin, dq, dk0, dv0, dk_got, dv_got))
-    da_pair = pair(da, out_got)
-    r_gate.line()
-    dq, dk0, dv0, dk1, dv1 = back(part_one, blocks - part_one)
-    dk_got, dv_got = swap(tie(dk1, *((r_down.out,) if fast else ())), 1), swap(dv1, 1)
-    r_qkva = Reduce(in_pair, da_pair, none, 0, third, "y")
     r_out.two()
-    out_mine, out_other = split_back(out_got)
-    layer_out = join_back(out_mine, swap(tie(out_other, dk_got), 1))
-    db = did(dqkv_call(order(perm, *((r_gate.out,) if fast else ())), cos, sin, dq, dk0, dv0, dk_got, dv_got))
+    line(r_gate)
+    db = did(dqkv_call(finish(order(perm), r_down), cos, sin, dq, dk0, dv0, dk_got, dv_got))
     db_pair = pair(db)
-    r_up.line(r_out)
-    r_qkva.two()
+    line(r_up, r_out)
     input_rows, gain_one = did(dinput_call(order(perm), gains, x, dh1, da, db, qkv0, qkv1))
     in_got = across(input_rows.reshape(ctx_count, half_len, width))
+    sub = third // 2
     gain_rows = jnp.concatenate([gain_one, gain_two], axis=0)
-    sub = third // 2
     if fast:
         gain_got = swap(gain_rows, 2)
-    r_qkvb0 = Reduce(in_pair, db_pair, none, 0, sub, "x")
+    (r_qkvb0,) = reductions(in_pair, [db_pair], [], 0, sub, ("x",), finish(order(perm), r_gate))
     if fast:
         gain_rows = did(order(gain_rows) + gain_got)
         gain_got = swap(gain_rows, 4)
-    r_qkvb1 = Reduce(in_pair, db_pair, none, sub, sub, "y")
-    r_qkva.line()
+    (r_qkvb1,) = reductions(in_pair, [db_pair], [], sub, sub, ("y",))
+    r_qkva.two()
     if fast:
         gain_rows = did(order(gain_rows) + gain_got)
         gain_got = swap(gain_rows, 1)
+        r_qkvb0.kept = tie(r_qkvb0.kept, in_got)
     r_qkvb0.two()
+    if fast:
+        r_qkvb1.kept = finish(r_qkvb1.kept, r_up)
     r_qkvb1.two()
+    line(r_qkva, r_qkvb0, r_qkvb1)
+    out_mine, out_other = split_back(out_got)
+    layer_out = join_back(out_mine, swap(out_other, 1))
     if fast:
         gain_rows = gain_rows + gain_got
-        ours = lax.dynamic_slice(gain_rows, (0, dp * LANE), (2, LANE)).T.astype(BF16)
-        total = jnp.concatenate([r_qkvb0.three(), r_qkvb1.three(), ours, jnp.zeros((LANE, LANE - 2), BF16)], axis=1)
-        total = jnp.sum(across(tie(total, in_got).reshape(ctx_count, part, third + LANE)).astype(F32), axis=0)
-        qkvb = total[:, :third]
-        gain_grads = (total[:, third], total[:, third + 1])
+        for bit in (1, 2):
+            gain_rows = gain_rows + lax.ppermute(gain_rows, "ctx", [(i, i ^ bit) for i in range(ctx_count)])
+        gain_grads = lax.dynamic_slice(gain_rows, (0, (dp * ctx_count + lax.axis_index("ctx")) * part), (2, part))
     else:
-        qkvb = jnp.concatenate([r_qkvb0.out, r_qkvb1.out], axis=1)
         gain_grads = lax.psum_scatter(gain_rows, ("dp", "ctx"), scatter_dimension=1, tiled=True)
+    qkvb = jnp.concatenate([r_qkvb0.out, r_qkvb1.out], axis=1)
     qkv_grad = jnp.concatenate(
         [half[:, i * hw : (i + 1) * hw] for i in range(3) for half in (r_qkva.out, qkvb)], axis=1
     )
-    in_mine, in_other = split_back(order(in_got))
+    in_mine, in_other = split_back(in_got)
     input_grad = join_back(in_mine, swap(in_other, 1))
 
     return (

time: 494 us -> 441 us (0.89)
  Pallas kernels: 199 us -> 172 us
  local copies, waits for them, and re-layouts: 39.6 us -> 29.1 us
  other arithmetic: 43.1 us -> 35 us
  waiting for transfers between devices: 99.4 us -> 92.6 us
    ppermute x71, waiting for transfers between devices: 80.6 us -> 57.9 us  [swap(): return lax.ppermute(v, 'dp', [(i, i ^ bit) for i in range(dp_count)])]
    reduce_scatter x4, waiting for transfers between devices: 2.23 us -> 20.3 us  [line(): lax.psum_scatter(total, 'ctx', scatter_dimension=0, tiled=True).astype(F32)]
    pallas_call x14 -> x12, Pallas kernels: 121 us -> 113 us  [call(): pl.pallas_call(body, out_shape=tuple(outs), in_specs=[SMEM] + [pl.BlockSp...]
    pallas_call x2, Pallas kernels: 36.5 us -> 28.4 us  [dattend_call(): pl.pallas_call(dattend_body, grid=(count,), out_shape=(sds((rows, count *...]
    optimization_barrier x8 -> x0, local copies, waits for them, and re-layouts: 6.73 us -> none  [the longest x7 6.51 us: sync(): live.update(zip(names, lax.optimization_barrier(leaves)))]
    pallas_call x2, Pallas kernels: 13.1 us -> 7.38 us  [dqkv_call(): pl.pallas_call(dqkv_body, grid=(rows // tile,), out_shape=sds((rows, 3 *...]
    all_to_all x6 -> x5, waiting for transfers between devices: 16.4 us -> 11.5 us  [across(): return lax.all_to_all(v, 'ctx', split_axis=0, concat_axis=0, tiled=True)]
    unnamed x135 -> x155, local copies, waits for them, and re-layouts: 17.9 us -> 15.6 us
  transfers between devices with their start and end apart: 82 -> 83, of which waited for: 24 -> 26; matrix products, arithmetic and copies ran while one was open for 13% -> 9% of each run, Pallas kernels for 38% -> 40%
where the time goes in v4:
time: 441 us; the launch traced here: 435 us
  Pallas kernels  172 us (39%)
  waiting for transfers between devices  92.6 us (21%)
  starting transfers between devices  69.6 us (16%)
  other arithmetic  35 us (8%)
  local copies, waits for them, and re-layouts  29.1 us (7%)
  blocking collectives  21.3 us (5%)
  between operations  15.2 us (3%)
    pallas_call x12, Pallas kernels, call(): pl.pallas_call(body, out_shape=tuple(outs), in_specs=[SMEM] + [pl.BlockSp...  113 us
    ppermute x71, waiting for transfers between devices, swap(): return lax.ppermute(v, 'dp', [(i, i ^ bit) for i in range(dp_count)])  57.9 us
    ppermute x71, starting transfers between devices, swap(): return lax.ppermute(v, 'dp', [(i, i ^ bit) for i in range(dp_count)])  43.8 us
    pallas_call x2, Pallas kernels, dattend_call(): pl.pallas_call(dattend_body, grid=(count,), out_shape=(sds((rows, count *...  28.4 us
    pallas_call x2, Pallas kernels, attend_call(): pl.pallas_call(attend_body, grid=(count,), out_shape=(sds((rows, count *...  23.9 us
    all_to_all x5, starting transfers between devices, across(): return lax.all_to_all(v, 'ctx', split_axis=0, concat_axis=0, tiled=True)  23.3 us
    all_gather x1, blocking collectives, gather_line(): return lax.all_gather(shard, 'ctx', axis=0, tiled=True)  21.3 us
    reduce_scatter x4, waiting for transfers between devices, line(): lax.psum_scatter(total, 'ctx', scatter_dimension=0, tiled=True).astype(F32)  20.3 us
  transfers between devices with their start and end apart: 83, of which 26 were waited for; matrix products, arithmetic and copies ran while one was open for 9% of the time, Pallas kernels for 40%

profile of v4, /device:TPU:0, one launch (start us, length us, event | category | flops | bytes accessed | tf_op | source)
XLA Modules:
  0.0 435.2 jit_solution(15913338782382149486)
XLA Ops:
  9.6 21.3 %all_gather.6 = bf16[128,3200]{1,0:T(8,128)(2,1)S(1)} all-gather(bf16[32,3200]{1,0:T(8,128)(2,1)S(1)} %concatenate.31), channel_id=1, replica_groups=mesh['dp'=8,'ctx'=4] {'ctx'}, dimensions={0}, use_global_device_ids=true | all-gather | bytes 1024000 | tf_op jit(solution)/shard_map/all_gather | solution.py:840
  48.6 6.2 %collective-permute-done.7.rest_9_ = bf16[128,1536]{1,0:T(8,128)(2,1)S(1)} collective-permute-done((bf16[128,1536]{1,0:T(8,128)(2,1)S(1)}, bf16[128,1536]{1,0:T(8,128)(2,1)S(1)}, u32[]{:S(2)}, u32[]{:S(2)}) %collective-permute-start.7) | collective-permute-done | bytes 393248 | tf_op jit(solution)/shard_map/ppermute | solution.py:771
  54.8 6.2 %collective-permute-done.8.rest_11_ = bf16[128,1536]{1,0:T(8,128)(2,1)S(1)} collective-permute-done((bf16[128,1536]{1,0:T(8,128)(2,1)S(1)}, bf16[128,1536]{1,0:T(8,128)(2,1)S(1)}, u32[]{:S(2)}, u32[]{:S(2)}) %collective-permute-start.8) | collective-permute-done | bytes 393248 | tf_op jit(solution)/shard_map/ppermute | solution.py:771
  82.0 15.4 %collective-permute-done.16.rest_10_ = bf16[128,2688]{1,0:T(8,128)(2,1)S(1)} collective-permute-done((bf16[128,2688]{1,0:T(8,128)(2,1)S(1)}, bf16[128,2688]{1,0:T(8,128)(2,1)S(1)}, u32[]{:S(2)}, u32[]{:S(2)}) %collective-permute-start.16) | collective-permute-done | bytes 688160 | tf_op jit(solution)/shard_map/ppermute | solution.py:771
  110.8 12.6 %qkv.1 = (bf16[512,1024]{1,0:T(8,128)(2,1)}, bf16[512,1024]{1,0:T(8,128)(2,1)}, bf16[512,2048]{1,0:T(8,128)(2,1)}, f32[8,1024]{1,0:T(8,128)}) custom-call(s32[8]{0:T(128)} %fusion.22.perm, f32[512,128]{1,0:T(8,128)} %get-tuple-element.367.cos_ref, f32[512,128]{1,0:T(8,128)} %get-tuple-element.368.sin_ref, bf16[512,1024]{1,0:T(8,128)(2,1)} %bitcast.149, ...), custom_call_target="tpu_custom_call" | custom-call | flops 1 | bytes 1 | tf_op jit(solution)/shard_map/qkv/pallas_call | solution.py:88
  137.3 11.9 %attend.2 = (bf16[512,512]{1,0:T(8,128)(2,1)}, bf16[4,2,1024,512]{3,2,1,0:T(8,128)(2,1)}) custom-call(s32[8]{0:T(128)} %fusion.22.perm, s32[1024,128]{1,0:T(8,128)} %broadcast_in_dim.18.segk_ref, s32[1,512]{1,0:T(1,128)} %bitcast.167, bf16[512,1024]{1,0:T(8,128)(2,1)} %get-tuple-element.445.q_ref, bf16[512,2048]{1,0:T(8,128)(2,1)} %get-tuple-element.446.k0_ref.v0_ref, ...), custom_call_target="tpu_custom_call" | custom-call | flops 1 | bytes 1 | tf_op jit(solution)/shard_map/attend/pallas_call | solution.py:220
  158.7 11.9 %attend.3 = (bf16[512,512]{1,0:T(8,128)(2,1)}, bf16[4,2,1024,512]{3,2,1,0:T(8,128)(2,1)}) custom-call(s32[8]{0:T(128)} %fusion.22.perm, s32[1024,128]{1,0:T(8,128)} %broadcast_in_dim.18.segk_ref, s32[1,512]{1,0:T(1,128)} %bitcast.168, bf16[512,1024]{1,0:T(8,128)(2,1)} %get-tuple-element.445.q_ref, bf16[512,2048]{1,0:T(8,128)(2,1)} %get-tuple-element.446.k0_ref.v0_ref, ...), custom_call_target="tpu_custom_call" | custom-call | flops 1 | bytes 1 | tf_op jit(solution)/shard_map/attend/pallas_call | solution.py:220
  176.2 5.2 %all-to-all-start.2 = ((bf16[4,128,1024]{2,1,0:T(8,128)(2,1)}), bf16[4,128,1024]{2,1,0:T(8,128)(2,1)S(1)}, u32[]{:S(2)}, u32[]{:S(2)}) async-start(bf16[4,128,1024]{2,1,0:T(8,128)(2,1)} %bitcast.19), calls=%async_computation.2 | async-start | bytes 2097152 | tf_op jit(solution)/shard_map/all_to_all | solution.py:777
  182.8 7.3 %middle.1 = (f32[512,1024]{1,0:T(8,128)}, bf16[512,1024]{1,0:T(8,128)(2,1)}, bf16[512,1024]{1,0:T(8,128)(2,1)}) custom-call(s32[8]{0:T(128)} %fusion.22.perm, f32[8,1024]{1,0:T(8,128)} %get-tuple-element.477.gains_ref, f32[512,128]{1,0:T(8,128)} %broadcast_in_dim.19.keep_ref.refs_0_, bf16[512,1024]{1,0:T(8,128)(2,1)} %bitcast.150, ...), custom_call_target="tpu_custom_call" | custom-call | flops 1 | bytes 1 | tf_op jit(solution)/shard_map/middle/pallas_call | solution.py:88
  191.0 13.9 %gate.1 = (bf16[512,2688]{1,0:T(8,128)(2,1)}, bf16[512,2688]{1,0:T(8,128)(2,1)}, bf16[512,2688]{1,0:T(8,128)(2,1)}) custom-call(s32[8]{0:T(128)} %fusion.22.perm, bf16[512,1024]{1,0:T(8,128)(2,1)} %get-tuple-element.514.b_hbm.refs_0_, bf16[128,3712]{1,0:T(8,128)(2,1)} %copy-done.3, bf16[128,3712]{1,0:T(8,128)(2,1)} %copy-done.6, ...), custom_call_target="tpu_custom_call" | custom-call | flops 1 | bytes 1 | tf_op jit(solution)/shard_map/gate/pallas_call | solution.py:88
  210.7 13.7 %dgate.1 = (bf16[512,2688]{1,0:T(8,128)(2,1)}, bf16[512,2688]{1,0:T(8,128)(2,1)}, bf16[512,1024]{1,0:T(8,128)(2,1)}) custom-call(s32[8]{0:T(128)} %fusion.22.perm, f32[512,128]{1,0:T(8,128)} %broadcast_in_dim.19.keep_ref.refs_0_, bf16[512,1024]{1,0:T(8,128)(2,1)} %bitcast.153, bf16[512,2688]{1,0:T(8,128)(2,1)} %get-tuple-element.488.f1_hbm, ...), custom_call_target="tpu_custom_call" | custom-call | flops 1 | bytes 1 | tf_op jit(solution)/shard_map/dgate/pallas_call | solution.py:88
  225.9 7.6 %grad_x.2 = (bf16[256,2688]{1,0:T(8,128)(2,1)}, bf16[256,2688]{1,0:T(8,128)(2,1)}) custom-call(s32[8]{0:T(128)} %fusion.22.perm, f32[512,128]{1,0:T(8,128)} %broadcast_in_dim.19.keep_ref.refs_0_, f32[512,128]{1,0:T(8,128)} %broadcast_in_dim.20.refs_1_, bf16[512,1024]{1,0:T(8,128)(2,1)} %bitcast.154, bf16[512,1024]{1,0:T(8,128)(2,1)} %collective-permute-done.39.refs_3_, ...), custom_call_target="tpu_custom_call" | custom-call | flops 1 | bytes 1 | tf_op jit(solution)/shard_map/grad_x/pallas_call | solution.py:88
  235.1 5.1 %all-to-all-start.3 = ((bf16[4,128,1024]{2,1,0:T(8,128)(2,1)}), bf16[4,128,1024]{2,1,0:T(8,128)(2,1)S(1)}, u32[]{:S(2)}, u32[]{:S(2)}) async-start(bf16[4,128,1024]{2,1,0:T(8,128)(2,1)} %bitcast.21), calls=%async_computation.3 | async-start | bytes 2097152 | tf_op jit(solution)/shard_map/all_to_all | solution.py:777
  240.4 11.0 %grad_yx.1 = (bf16[256,2688]{1,0:T(8,128)(2,1)}, bf16[256,2688]{1,0:T(8,128)(2,1)}, bf16[256,2688]{1,0:T(8,128)(2,1)}, bf16[256,2688]{1,0:T(8,128)(2,1)}) custom-call(s32[8]{0:T(128)} %fusion.22.perm, bf16[512,1024]{1,0:T(8,128)(2,1)} %get-tuple-element.514.b_hbm.refs_0_, bf16[512,1024]{1,0:T(8,128)(2,1)} %collective-permute-done.40.refs_1_, ...), custom_call_target="tpu_custom_call" | custom-call | flops 1 | bytes 1 | tf_op jit(solution)/shard_map/grad_yx/pallas_call | solution.py:88
  252.9 16.4 %dmiddle.1 = (f32[512,1024]{1,0:T(8,128)}, bf16[512,1024]{1,0:T(8,128)(2,1)}, bf16[512,1024]{1,0:T(8,128)(2,1)}, f32[1,1024]{1,0:T(1,128)}) custom-call(s32[8]{0:T(128)} %fusion.22.perm, f32[8,1024]{1,0:T(8,128)} %get-tuple-element.477.gains_ref, f32[512,128]{1,0:T(8,128)} %broadcast_in_dim.19.keep_ref.refs_0_, bf16[512,1024]{1,0:T(8,128)(2,1)} %bitcast.155, ...), custom_call_target="tpu_custom_call" | custom-call | flops 1 | bytes 1 | tf_op jit(solution)/shard_map/dmiddle/pallas_call | solution.py:88
  273.7 5.0 %grad_y.3 = (bf16[256,1024]{1,0:T(8,128)(2,1)}, bf16[256,1024]{1,0:T(8,128)(2,1)}) custom-call(s32[8]{0:T(128)} %fusion.22.perm, bf16[512,1024]{1,0:T(8,128)(2,1)} %get-tuple-element.502.refs_0_, bf16[512,1024]{1,0:T(8,128)(2,1)} %collective-permute-done.42.refs_1_, bf16[512,1024]{1,0:T(8,128)(2,1)} %get-tuple-element.524.refs_2_, bf16[512,1024]{1,0:T(8,128)(2,1)} %copy-done.45), custom_call_target="tpu_custom_call" | custom-call | flops 1 | bytes 1 | tf_op jit(solution)/shard_map/grad_y/pallas_call | solution.py:88
  280.2 14.2 %dattend.2 = (bf16[512,512]{1,0:T(8,128)(2,1)}, f32[512,512]{1,0:T(8,128)}, f32[512,512]{1,0:T(8,128)}, bf16[512,512]{1,0:T(8,128)(2,1)}, bf16[512,512]{1,0:T(8,128)(2,1)}) custom-call(s32[8]{0:T(128)} %fusion.22.perm, bf16[512,1024]{1,0:T(8,128)(2,1)} %get-tuple-element.445.q_ref, bf16[512,2048]{1,0:T(8,128)(2,1)} %get-tuple-element.446.k0_ref.v0_ref, ...), custom_call_target="tpu_custom_call" | custom-call | flops 1 | bytes 1 | tf_op jit(solution)/shard_map/dattend/pallas_call | solution.py:551
  309.3 5.7 %grad_y.4 = (bf16[256,1536]{1,0:T(8,128)(2,1)}, bf16[256,1536]{1,0:T(8,128)(2,1)}) custom-call(s32[8]{0:T(128)} %fusion.22.perm, bf16[512,1024]{1,0:T(8,128)(2,1)} %get-tuple-element.501.refs_0_, bf16[512,1024]{1,0:T(8,128)(2,1)} %copy-done.5, bf16[512,1536]{1,0:T(8,128)(2,1)} %dqkv.2.refs_2_.da_hbm, bf16[512,1536]{1,0:T(8,128)(2,1)} %copy-done.36), custom_call_target="tpu_custom_call" | custom-call | flops 1 | bytes 1 | tf_op jit(solution)/shard_map/grad_y/pallas_call | solution.py:88
  316.6 14.3 %dattend.3 = (bf16[512,512]{1,0:T(8,128)(2,1)}, f32[512,512]{1,0:T(8,128)}, f32[512,512]{1,0:T(8,128)}, bf16[512,512]{1,0:T(8,128)(2,1)}, bf16[512,512]{1,0:T(8,128)(2,1)}) custom-call(s32[8]{0:T(128)} %fusion.22.perm, bf16[512,1024]{1,0:T(8,128)(2,1)} %get-tuple-element.445.q_ref, bf16[512,2048]{1,0:T(8,128)(2,1)} %get-tuple-element.446.k0_ref.v0_ref, ...), custom_call_target="tpu_custom_call" | custom-call | flops 1 | bytes 1 | tf_op jit(solution)/shard_map/dattend/pallas_call | solution.py:551
  344.6 10.5 %dinput.1 = (bf16[512,1024]{1,0:T(8,128)(2,1)}, f32[1,1024]{1,0:T(1,128)}) custom-call(s32[8]{0:T(128)} %fusion.22.perm, f32[8,1024]{1,0:T(8,128)} %get-tuple-element.477.gains_ref, bf16[512,1024]{1,0:T(8,128)(2,1)} %bitcast.151, f32[512,1024]{1,0:T(8,128)} %get-tuple-element.520.dh1_hbm, bf16[512,1536]{1,0:T(8,128)(2,1)} %dqkv.2.refs_2_.da_hbm, ...), custom_call_target="tpu_custom_call" | custom-call | flops 1 | bytes 1 | tf_op jit(solution)/shard_map/dinput/pallas_call | solution.py:88
  355.1 5.1 %all-to-all-start.4 = ((bf16[4,128,1024]{2,1,0:T(8,128)(2,1)}), bf16[4,128,1024]{2,1,0:T(8,128)(2,1)S(1)}, u32[]{:S(2)}, u32[]{:S(2)}) async-start(bf16[4,128,1024]{2,1,0:T(8,128)(2,1)} %bitcast.163), calls=%async_computation.5 | async-start | bytes 2097152 | tf_op jit(solution)/shard_map/all_to_all | solution.py:777
  361.9 4.5 %grad_x.3 = (bf16[256,768]{1,0:T(8,128)(2,1)}, bf16[256,768]{1,0:T(8,128)(2,1)}) custom-call(s32[8]{0:T(128)} %fusion.22.perm, bf16[512,1024]{1,0:T(8,128)(2,1)} %get-tuple-element.501.refs_0_, bf16[512,1024]{1,0:T(8,128)(2,1)} %copy-done.5, bf16[512,1536]{1,0:T(8,128)(2,1)} %dqkv.3.db_hbm.refs_2_, bf16[512,1536]{1,0:T(8,128)(2,1)} %collective-permute-done.61.refs_3_), custom_call_target="tpu_custom_call" | custom-call | flops 1 | bytes 1 | tf_op jit(solution)/shard_map/grad_x/pallas_call | solution.py:88
  381.4 9.7 %all-to-all-done.4 = bf16[4,128,1024]{2,1,0:T(8,128)(2,1)S(1)} async-done(((bf16[4,128,1024]{2,1,0:T(8,128)(2,1)}), bf16[4,128,1024]{2,1,0:T(8,128)(2,1)S(1)}, u32[]{:S(2)}, u32[]{:S(2)}) %all-to-all-start.4) | async-done | bytes 1048608 | tf_op jit(solution)/shard_map/all_to_all | solution.py:777
  407.6 19.0 %reduce-scatter.9.cloned.1.call-done = bf16[32,3072]{1,0:T(8,128)(2,1)} async-done(((bf16[128,3072]{1,0:T(8,128)(2,1)}), bf16[32,3072]{1,0:T(8,128)(2,1)}) %reduce-scatter.9.cloned.1.call-update) | async-done | bytes 196624 | tf_op jit(solution)/shard_map/reduce_scatter | solution.py:1001
  (396 shorter events, 166.4 us)
Async XLA Ops:
  7.2 63.4 %all-gather.2.cloned.1.call-start = ((), (), s32[]{:S(2)}) async-start(), calls=%async_computation.9 | async-start | bytes 2048000 | tf_op jit(solution)/shard_map/all_gather | solution.py:840
  8.6 23.9 %collective-permute-start = (bf16[2,128,1024]{2,1,0:T(8,128)(2,1)S(1)}, bf16[2,128,1024]{2,1,0:T(8,128)(2,1)S(1)}, u32[]{:S(2)}, u32[]{:S(2)}) collective-permute-start(bf16[2,128,1024]{2,1,0:T(8,128)(2,1)S(1)} %get-tuple-element.595), channel_id=1, source_target_pairs={{0,4},{4,0},{8,12},{12,8},{16,20},{20,16},{24,28},{28,24},{1,5},{5... | collective-permute-start | bytes 1572872 | tf_op jit(solution)/shard_map/ppermute | solution.py:771
  72.9 29.4 %all-to-all-start = ((bf16[4,128,1024]{2,1,0:T(8,128)(2,1)}), bf16[4,128,1024]{2,1,0:T(8,128)(2,1)S(1)}, u32[]{:S(2)}, u32[]{:S(2)}) async-start(bf16[4,128,1024]{2,1,0:T(8,128)(2,1)} %bitcast.7), calls=%async_computation | async-start | bytes 2097152 | tf_op jit(solution)/shard_map/all_to_all | solution.py:777
  77.7 22.8 %collective-permute-start.15 = (bf16[128,3712]{1,0:T(8,128)(2,1)S(1)}, bf16[128,3712]{1,0:T(8,128)(2,1)S(1)}, u32[]{:S(2)}, u32[]{:S(2)}) collective-permute-start(bf16[128,3712]{1,0:T(8,128)(2,1)S(1)} %slice.227.rest_0_), channel_id=1, source_target_pairs={{0,8},{4,12},{8,0},{12,4},{16,24},{20,28},{24,16},{28,20},{1,9},{5... | collective-permute-start | bytes 2850824 | tf_op jit(solution)/shard_map/ppermute | solution.py:771
  102.4 26.6 %all-to-all-start.1 = ((bf16[4,32,2688]{2,1,0:T(8,128)(2,1)}), bf16[4,32,2688]{2,1,0:T(8,128)(2,1)}, u32[]{:S(2)}, u32[]{:S(2)}) async-start(bf16[4,32,2688]{2,1,0:T(8,128)(2,1)} %broadcast_in_dim.17), calls=%async_computation.1 | async-start | bytes 1376256 | tf_op jit(solution)/shard_map/all_to_all | solution.py:777
  131.6 23.5 %collective-permute-start.22 = (bf16[128,3712]{1,0:T(8,128)(2,1)S(1)}, bf16[128,3712]{1,0:T(8,128)(2,1)S(1)}, u32[]{:S(2)}, u32[]{:S(2)}) collective-permute-start(bf16[128,3712]{1,0:T(8,128)(2,1)S(1)} %collective-permute-done.15.rest_1_), channel_id=1, source_target_pairs={{0,16},{4,20},{8,24},{12,28},{16,0},{20,4},{24,8},{28,12},{1,17},{... | collective-permute-start | bytes 2850824 | tf_op jit(solution)/shard_map/ppermute | solution.py:771
  176.2 30.6 %all-to-all-start.2 = ((bf16[4,128,1024]{2,1,0:T(8,128)(2,1)}), bf16[4,128,1024]{2,1,0:T(8,128)(2,1)S(1)}, u32[]{:S(2)}, u32[]{:S(2)}) async-start(bf16[4,128,1024]{2,1,0:T(8,128)(2,1)} %bitcast.19), calls=%async_computation.2 | async-start | bytes 2097152 | tf_op jit(solution)/shard_map/all_to_all | solution.py:777
  181.5 23.4 %collective-permute-start.33 = (bf16[128,2688]{1,0:T(8,128)(2,1)}, bf16[128,2688]{1,0:T(8,128)(2,1)S(1)}, u32[]{:S(2)}, u32[]{:S(2)}) collective-permute-start(bf16[128,2688]{1,0:T(8,128)(2,1)} %collective-permute-done.27.rest_2_), channel_id=1, source_target_pairs={{0,8},{4,12},{8,0},{12,4},{16,24},{20,28},{24,16},{28,20},{1,9},{5... | collective-permute-start | bytes 2064392 | tf_op jit(solution)/shard_map/ppermute | solution.py:771
  182.6 24.2 %collective-permute-start.36 = (bf16[128,2688]{1,0:T(8,128)(2,1)}, bf16[128,2688]{1,0:T(8,128)(2,1)}, u32[]{:S(2)}, u32[]{:S(2)}) collective-permute-start(bf16[128,2688]{1,0:T(8,128)(2,1)} %collective-permute-done.27.rest_2_), channel_id=1, source_target_pairs={{0,4},{4,0},{8,12},{12,8},{16,20},{20,16},{24,28},{28,24},{1,5},{5... | collective-permute-start | bytes 2064392 | tf_op jit(solution)/shard_map/ppermute | solution.py:771
  233.6 36.4 %collective-permute-start.45 = (bf16[256,2688]{1,0:T(8,128)(2,1)}, bf16[256,2688]{1,0:T(8,128)(2,1)}, u32[]{:S(2)}, u32[]{:S(2)}) collective-permute-start(bf16[256,2688]{1,0:T(8,128)(2,1)} %get-tuple-element.512), channel_id=1, source_target_pairs={{0,8},{4,12},{8,0},{12,4},{16,24},{20,28},{24,16},{28,20},{1,9},{5... | collective-permute-start | bytes 4128776 | tf_op jit(solution)/shard_map/ppermute | solution.py:771
  235.1 45.1 %all-to-all-start.3 = ((bf16[4,128,1024]{2,1,0:T(8,128)(2,1)}), bf16[4,128,1024]{2,1,0:T(8,128)(2,1)S(1)}, u32[]{:S(2)}, u32[]{:S(2)}) async-start(bf16[4,128,1024]{2,1,0:T(8,128)(2,1)} %bitcast.21), calls=%async_computation.3 | async-start | bytes 2097152 | tf_op jit(solution)/shard_map/all_to_all | solution.py:777
  240.2 95.9 %reduce-scatter.5.cloned.1.call-start = ((), (), s32[]{:S(2)}) async-start(), calls=%async_computation.10 | async-start | bytes 860160 | tf_op jit(solution)/shard_map/reduce_scatter | solution.py:1001
  251.4 43.1 %collective-permute-start.49 = (bf16[256,2688]{1,0:T(8,128)(2,1)}, bf16[256,2688]{1,0:T(8,128)(2,1)S(1)}, u32[]{:S(2)}, u32[]{:S(2)}) collective-permute-start(bf16[256,2688]{1,0:T(8,128)(2,1)} %get-tuple-element.518), channel_id=1, source_target_pairs={{0,16},{4,20},{8,24},{12,28},{16,0},{20,4},{24,8},{28,12},{1,17},{... | collective-permute-start | bytes 4128776 | tf_op jit(solution)/shard_map/ppermute | solution.py:771
  269.4 33.4 %collective-permute-start.48 = (bf16[256,2688]{1,0:T(8,128)(2,1)}, bf16[256,2688]{1,0:T(8,128)(2,1)}, u32[]{:S(2)}, u32[]{:S(2)}) collective-permute-start(bf16[256,2688]{1,0:T(8,128)(2,1)} %get-tuple-element.530), channel_id=1, source_target_pairs={{0,8},{4,12},{8,0},{12,4},{16,24},{20,28},{24,16},{28,20},{1,9},{5... | collective-permute-start | bytes 4128776 | tf_op jit(solution)/shard_map/ppermute | solution.py:771
  272.1 32.9 %collective-permute-start.54 = (bf16[128,2688]{1,0:T(8,128)(2,1)}, bf16[128,2688]{1,0:T(8,128)(2,1)S(1)}, u32[]{:S(2)}, u32[]{:S(2)}) collective-permute-start(bf16[128,2688]{1,0:T(8,128)(2,1)} %add_convert_fusion.5), channel_id=1, source_target_pairs={{0,16},{4,20},{8,24},{12,28},{16,0},{20,4},{24,8},{28,12},{1,17},{... | collective-permute-start | bytes 2064392 | tf_op jit(solution)/shard_map/ppermute | solution.py:771
  278.7 52.1 %collective-permute-start.56 = (bf16[256,1024]{1,0:T(8,128)(2,1)}, bf16[256,1024]{1,0:T(8,128)(2,1)}, u32[]{:S(2)}, u32[]{:S(2)}) collective-permute-start(bf16[256,1024]{1,0:T(8,128)(2,1)} %get-tuple-element.525), channel_id=1, source_target_pairs={{0,16},{4,20},{8,24},{12,28},{16,0},{20,4},{24,8},{28,12},{1,17},{... | collective-permute-start | bytes 1572872 | tf_op jit(solution)/shard_map/ppermute | solution.py:771
  296.6 36.7 %collective-permute-start.53 = (bf16[128,2688]{1,0:T(8,128)(2,1)}, bf16[128,2688]{1,0:T(8,128)(2,1)}, u32[]{:S(2)}, u32[]{:S(2)}) collective-permute-start(bf16[128,2688]{1,0:T(8,128)(2,1)} %add_convert_fusion.4), channel_id=1, source_target_pairs={{0,8},{4,12},{8,0},{12,4},{16,24},{20,28},{24,16},{28,20},{1,9},{5... | collective-permute-start | bytes 2064392 | tf_op jit(solution)/shard_map/ppermute | solution.py:771
  307.2 54.7 %reduce-scatter.7.cloned.1.call-start = ((), (), s32[]{:S(2)}) async-start(), calls=%async_computation.11 | async-start | bytes 860160 | tf_op jit(solution)/shard_map/reduce_scatter | solution.py:1001
  307.5 33.3 %collective-permute-start.52 = (bf16[128,2688]{1,0:T(8,128)(2,1)}, bf16[128,2688]{1,0:T(8,128)(2,1)}, u32[]{:S(2)}, u32[]{:S(2)}) collective-permute-start(bf16[128,2688]{1,0:T(8,128)(2,1)} %add_convert_fusion.3), channel_id=1, source_target_pairs={{0,16},{4,20},{8,24},{12,28},{16,0},{20,4},{24,8},{28,12},{1,17},{... | collective-permute-start | bytes 2064392 | tf_op jit(solution)/shard_map/ppermute | solution.py:771
  315.0 58.9 %collective-permute-start.63 = (bf16[256,1536]{1,0:T(8,128)(2,1)}, bf16[256,1536]{1,0:T(8,128)(2,1)S(1)}, u32[]{:S(2)}, u32[]{:S(2)}) collective-permute-start(bf16[256,1536]{1,0:T(8,128)(2,1)} %get-tuple-element.547), channel_id=1, source_target_pairs={{0,16},{4,20},{8,24},{12,28},{16,0},{20,4},{24,8},{28,12},{1,17},{... | collective-permute-start | bytes 2359304 | tf_op jit(solution)/shard_map/ppermute | solution.py:771
  355.1 36.0 %all-to-all-start.4 = ((bf16[4,128,1024]{2,1,0:T(8,128)(2,1)}), bf16[4,128,1024]{2,1,0:T(8,128)(2,1)S(1)}, u32[]{:S(2)}, u32[]{:S(2)}) async-start(bf16[4,128,1024]{2,1,0:T(8,128)(2,1)} %bitcast.163), calls=%async_computation.5 | async-start | bytes 2097152 | tf_op jit(solution)/shard_map/all_to_all | solution.py:777
  360.2 42.8 %reduce-scatter.11.cloned.1.call-start = ((), (), s32[]{:S(2)}) async-start(), calls=%async_computation.13 | async-start | bytes 1187840 | tf_op jit(solution)/shard_map/reduce_scatter | solution.py:1001
  367.1 24.1 %collective-permute-start.69 = (bf16[256,768]{1,0:T(8,128)(2,1)}, bf16[256,768]{1,0:T(8,128)(2,1)}, u32[]{:S(2)}, u32[]{:S(2)}) collective-permute-start(bf16[256,768]{1,0:T(8,128)(2,1)} %get-tuple-element.567), channel_id=1, source_target_pairs={{0,8},{4,12},{8,0},{12,4},{16,24},{20,28},{24,16},{28,20},{1,9},{5... | collective-permute-start | bytes 1179656 | tf_op jit(solution)/shard_map/ppermute | solution.py:771
  376.1 50.5 %reduce-scatter.9.cloned.1.call-start = ((), (), s32[]{:S(2)}) async-start(), calls=%async_computation.12 | async-start | bytes 983040 | tf_op jit(solution)/shard_map/reduce_scatter | solution.py:1001
  (134 other events, 1372.5 us)
Sparse Core Ops, SparseCore 0:
  32.7 37.9 all-gather.1
  307.4 22.0 reduce-scatter.4
  336.2 22.8 reduce-scatter.6
  376.3 26.6 reduce-scatter.10
  405.2 21.3 reduce-scatter.8
